TPU v7x, 256 devices: a whole 4x4x8 slice. The times are simulated.
256 devices in a mesh: gx: 64 (over z, y_lo, x), gy: 4 (over y_hi, core).
Axes of the slice: x: 4, y: 4 (y_hi: 2, y_lo: 2; y = y_hi * 2 + y_lo), z: 8, core: 2. Of those that a mesh axis runs over, the one named last changes fastest.
Arguments:
- misfit: float32 [3, 512, 128, 128], P(None, 'gx', 'gy'), may hold values from -13 to 13
- damage: float32 [512, 128, 128], P('gx', 'gy'), may hold values from 0 to 0.9
- displacement: float32 [3, 512, 128, 128], P(None, 'gx', 'gy'), may hold values from -3 to 3
Outputs:
- adjoint: float32 [3, 512, 128, 128], P(None, 'gx', 'gy')
- sensitivity: float32 [512, 128, 128], P('gx', 'gy')
All inputs are finite; a program needn't handle non-finite values.
Results may differ from a plain program's by a relative error of at most 0.00012.
Values sent between devices are 32-bit elements; how exact they have to be, the bound alone decides.
No kernel may reach another device: no remote copies, remote signals or barrier semaphores. Data moves between devices by JAX's collectives and lax.ppermute only.
A program may use at most 64 MiB of HBM per device.

v0:
```python
import math

import jax
import jax.numpy as jnp
import numpy as np
from jax import lax
from jax.sharding import Mesh
from jax.sharding import PartitionSpec as P

ITERS = 3
GX = ("gx_0", "gx_1", "gx_2")
GY = ("gy_0", "gy_1")
GX_GY = ("gx_0", "gx_1", "gx_2", "gy_0", "gy_1")


def passed_along(x, axis, by):
    devices = lax.axis_size(axis)
    pairs = [(i, i + by) for i in range(devices) if 0 <= i + by < devices]
    return lax.ppermute(x, axis, pairs)


def over_axes(x, axes):
    for axis in axes:
        x = lax.psum(x, axis)
    return x


def kronecker(first, second):
    return 1.0 if first == second else 0.0


def element_matrix():
    modulus = 3.0
    poisson_ratio = 0.3
    lame_first = modulus * poisson_ratio / ((1.0 + poisson_ratio) * (1.0 - 2.0 * poisson_ratio))
    shear_modulus = modulus / (2.0 * (1.0 + poisson_ratio))
    signs = [
        [
            2.0 * (corner_index >> 2 & 1) - 1.0,
            2.0 * (corner_index >> 1 & 1) - 1.0,
            2.0 * (corner_index & 1) - 1.0,
        ]
        for corner_index in range(8)
    ]
    elastic = [
        [
            [
                [
                    lame_first * kronecker(i, j) * kronecker(k, l)
                    + shear_modulus
                    * (kronecker(i, k) * kronecker(j, l) + kronecker(i, l) * kronecker(j, k))
                    for l in range(3)
                ]
                for k in range(3)
            ]
            for j in range(3)
        ]
        for i in range(3)
    ]
    stiffness = np.zeros((8, 3, 8, 3))
    root_three = math.sqrt(3.0)
    for gauss_index in range(8):
        gauss_point = [signs[gauss_index][dimension] / root_three for dimension in range(3)]
        gradients = [[0.0, 0.0, 0.0] for corner_index in range(8)]
        for corner_index in range(8):
            for dimension in range(3):
                factor = 0.25 * signs[corner_index][dimension]
                for others in range(3):
                    if others != dimension:
                        factor = factor * (1.0 + signs[corner_index][others] * gauss_point[others])
                gradients[corner_index][dimension] = factor
        for first_corner in range(8):
            for i in range(3):
                for second_corner in range(8):
                    for j in range(3):
                        accumulated = 0.0
                        for k in range(3):
                            for l in range(3):
                                accumulated = (
                                    accumulated
                                    + gradients[first_corner][k]
                                    * elastic[i][k][j][l]
                                    * gradients[second_corner][l]
                                )
                        stiffness[first_corner, i, second_corner, j] = (
                            stiffness[first_corner, i, second_corner, j] + 0.125 * accumulated
                        )
    return stiffness.reshape(24, 24)


def corner_offsets():
    return [
        (corner_index >> 2 & 1, corner_index >> 1 & 1, corner_index & 1)
        for corner_index in range(8)
    ]


def corner_stack(padded, count_x, count_y, count_z):
    return jnp.stack(
        [
            padded[
                :,
                shift_x : shift_x + count_x,
                shift_y : shift_y + count_y,
                shift_z : shift_z + count_z,
            ]
            for shift_x, shift_y, shift_z in corner_offsets()
        ],
        0,
    )


def element_forces(padded, degradation):
    count_x, count_y, count_z = degradation.shape
    stacked = corner_stack(padded, count_x, count_y, count_z).reshape(24, -1)
    table = jnp.asarray(element_matrix(), jnp.float32)
    forces = jnp.dot(
        table, stacked, precision=lax.Precision.HIGHEST, preferred_element_type=jnp.float32
    )
    return forces.reshape(8, 3, count_x, count_y, count_z) * degradation


def assemble(forces):
    total = None
    for corner_index, (shift_x, shift_y, shift_z) in enumerate(corner_offsets()):
        placed = jnp.pad(
            forces[corner_index],
            ((0, 0), (shift_x, 1 - shift_x), (shift_y, 1 - shift_y), (shift_z, 1 - shift_z)),
        )
        total = placed if total is None else total + placed
    return total


def apply_owned(field, degradation):
    rim_x = passed_along(field[:, :1], GX, -1)
    extended = jnp.concatenate([field, rim_x], 1)
    rim_y = passed_along(extended[:, :, :1], GY, -1)
    extended = jnp.concatenate([extended, rim_y], 2)
    extended = jnp.pad(extended, ((0, 0), (0, 0), (0, 0), (0, 1)))
    nodes = assemble(element_forces(extended, degradation))[:, :, :, :-1]
    spill_y = passed_along(nodes[:, :, -1:], GY, 1)
    nodes = jnp.concatenate([nodes[:, :, :1] + spill_y, nodes[:, :, 1:-1]], 2)
    spill_x = passed_along(nodes[:, -1:], GX, 1)
    return jnp.concatenate([nodes[:, :1] + spill_x, nodes[:, 1:-1]], 1)


def two_products(residual, image):
    return (
        over_axes(jnp.sum(residual * residual), GX_GY),
        over_axes(jnp.sum(residual * image), GX_GY),
    )


def body(misfit, damage, displacement):
    degradation = (1.0 - damage) * (1.0 - damage) + 0.001

    def operate(field):
        return apply_owned(field, degradation)

    adjoint = jnp.zeros_like(misfit)
    residual = misfit
    image = operate(residual)
    norm_now, product = two_products(residual, image)
    alpha = norm_now / product
    direction = residual
    along = image
    for step in range(ITERS):
        adjoint = adjoint + alpha * direction
        residual = residual - alpha * along
        if step + 1 < ITERS:
            image = operate(residual)
            norm_next, product = two_products(residual, image)
            ratio = norm_next / norm_now
            alpha = norm_next / (product - ratio * norm_next / alpha)
            direction = residual + ratio * direction
            along = image + ratio * along
            norm_now = norm_next
    count_x, count_y, count_z = damage.shape
    paired = jnp.concatenate([adjoint, displacement], 0)
    pair_x = passed_along(paired[:, :1], GX, -1)
    paired = jnp.concatenate([paired, pair_x], 1)
    pair_y = passed_along(paired[:, :, :1], GY, -1)
    paired = jnp.concatenate([paired, pair_y], 2)
    paired = jnp.pad(paired, ((0, 0), (0, 0), (0, 0), (0, 1)))
    table = jnp.asarray(element_matrix(), jnp.float32)
    adjoint_corners = corner_stack(paired[:3], count_x, count_y, count_z).reshape(24, -1)
    moved_corners = corner_stack(paired[3:], count_x, count_y, count_z).reshape(24, -1)
    product_terms = jnp.dot(
        table, moved_corners, precision=lax.Precision.HIGHEST, preferred_element_type=jnp.float32
    )
    contraction = jnp.sum(adjoint_corners * product_terms, 0).reshape(count_x, count_y, count_z)
    sensitivity = 2.0 * (1.0 - damage) * contraction
    return (adjoint, sensitivity)


def solution(mesh):
    split = Mesh(mesh.devices.reshape(8, 2, 4, 2, 2), ("gx_0", "gx_1", "gx_2", "gy_0", "gy_1"))
    in_specs = (P(None, GX, GY, None), P(GX, GY, None), P(None, GX, GY, None))
    out_specs = (P(None, GX, GY, None), P(GX, GY, None))
    return jax.shard_map(body, mesh=split, in_specs=in_specs, out_specs=out_specs, check_vma=False)
```

profile of v0, /device:TPU:1, one launch (start us, length us, event | category | flops | bytes accessed | tf_op | source)
XLA Modules:
  0.0 309.8 jit_solution(6029709115871913308)
XLA Ops:
  6.9 5.7 %collective-permute-start.1 = (f32[3,9,1,128]{3,2,1,0:T(1,128)S(1)}, f32[3,9,1,128]{3,2,1,0:T(1,128)S(1)}, u32[]{:S(2)}, u32[]{:S(2)}) collective-permute-start(f32[3,9,1,128]{3,2,1,0:T(1,128)S(1)} %slice.407), channel_id=1, source_target_pairs={{1,0},{2,1},{3,2},{5,4},{6,5},{7,6},{9,8},{10,9},{11,10},{13,12},{... | collective-permute-start | bytes 41480 | tf_op jit(solution)/shard_map/ppermute | solution.py:19
  37.5 23.1 %all-reduce.30 = (f32[]{:T(128)}, f32[]{:T(128)}) all-reduce(f32[]{:T(128)} %get-tuple-element.7, f32[]{:T(128)} %get-tuple-element.6), channel_id=1, replica_groups=mesh['gx_0'=8,'gx_1'=2,'gx_2'=4,'gy_0'=2,'gy_1'=2] {'gx_0'}, use_global_device_ids=true, to_apply=%region_1.2 | all-reduce | flops 2 | bytes 16 | tf_op jit(solution)/shard_map/psum | solution.py:24
  60.6 4.6 %all-reduce.42 = (f32[]{:T(128)}, f32[]{:T(128)}) all-reduce(f32[]{:T(128)} %get-tuple-element.12, f32[]{:T(128)} %get-tuple-element.13), channel_id=1, replica_groups=mesh['gx_0'=8,'gx_1'=2,'gx_2'=4,'gy_0'=2,'gy_1'=2] {'gx_1'}, use_global_device_ids=true, to_apply=%region_2.3 | all-reduce | flops 2 | bytes 16 | tf_op jit(solution)/shard_map/psum | solution.py:24
  65.3 6.6 %all-reduce.33 = (f32[]{:T(128)}, f32[]{:T(128)}) all-reduce(f32[]{:T(128)} %get-tuple-element.36, f32[]{:T(128)} %get-tuple-element.37), channel_id=1, replica_groups=mesh['gx_0'=8,'gx_1'=2,'gx_2'=4,'gy_0'=2,'gy_1'=2] {'gx_2'}, use_global_device_ids=true, to_apply=%region_3.4 | all-reduce | flops 2 | bytes 16 | tf_op jit(solution)/shard_map/psum | solution.py:24
  71.9 5.9 %all-reduce.39 = (f32[]{:T(128)}, f32[]{:T(128)}) all-reduce(f32[]{:T(128)} %get-tuple-element.18, f32[]{:T(128)} %get-tuple-element.19), channel_id=1, replica_groups=mesh['gx_0'=8,'gx_1'=2,'gx_2'=4,'gy_0'=2,'gy_1'=2] {'gy_0'}, use_global_device_ids=true, to_apply=%region_4.5 | all-reduce | flops 2 | bytes 16 | tf_op jit(solution)/shard_map/psum | solution.py:24
  77.8 11.8 %all-reduce.36 = (f32[]{:T(128)}, f32[]{:T(128)}) all-reduce(f32[]{:T(128)} %get-tuple-element.30, f32[]{:T(128)} %get-tuple-element.31), channel_id=1, replica_groups=mesh['gx_0'=8,'gx_1'=2,'gx_2'=4,'gy_0'=2,'gy_1'=2] {'gy_1'}, use_global_device_ids=true, to_apply=%region_5.6 | all-reduce | flops 2 | bytes 16 | tf_op jit(solution)/shard_map/psum | solution.py:24
  110.7 4.6 %reshape.34 = f32[24,32768]{1,0:T(8,128)} reshape(f32[8,3,8,32,128]{4,3,2,1,0:T(8,128)} %fusion.22) | data formatting | bytes 6291456 | tf_op jit(solution)/shard_map/reshape | solution.py:115
  115.3 4.7 %convolution_bitcast_fusion.1 = f32[3,8,256,128]{3,1,2,0:T(8,128)S(1)} fusion(f32[24,24]{1,0:T(8,128)S(1)} %copy-done.5, f32[24,32768]{1,0:T(8,128)} %reshape.34), kind=kOutput, calls=%fused_computation.10 | convolution fusion | flops 226492416 | bytes 6293760 | tf_op jit(solution)/shard_map/dot_general | solution.py:117
  131.2 15.0 %all-reduce.29 = (f32[]{:T(128)}, f32[]{:T(128)}) all-reduce(f32[]{:T(128)} %get-tuple-element.5, f32[]{:T(128)} %get-tuple-element.4), channel_id=1, replica_groups=mesh['gx_0'=8,'gx_1'=2,'gx_2'=4,'gy_0'=2,'gy_1'=2] {'gx_0'}, use_global_device_ids=true, to_apply=%region_13.14 | all-reduce | flops 2 | bytes 16 | tf_op jit(solution)/shard_map/psum | solution.py:24
  146.2 4.5 %all-reduce.41 = (f32[]{:T(128)}, f32[]{:T(128)}) all-reduce(f32[]{:T(128)} %get-tuple-element.10, f32[]{:T(128)} %get-tuple-element.11), channel_id=1, replica_groups=mesh['gx_0'=8,'gx_1'=2,'gx_2'=4,'gy_0'=2,'gy_1'=2] {'gx_1'}, use_global_device_ids=true, to_apply=%region_14.15 | all-reduce | flops 2 | bytes 16 | tf_op jit(solution)/shard_map/psum | solution.py:24
  150.7 6.9 %all-reduce.32 = (f32[]{:T(128)}, f32[]{:T(128)}) all-reduce(f32[]{:T(128)} %get-tuple-element.34, f32[]{:T(128)} %get-tuple-element.35), channel_id=1, replica_groups=mesh['gx_0'=8,'gx_1'=2,'gx_2'=4,'gy_0'=2,'gy_1'=2] {'gx_2'}, use_global_device_ids=true, to_apply=%region_15.16 | all-reduce | flops 2 | bytes 16 | tf_op jit(solution)/shard_map/psum | solution.py:24
  157.6 6.0 %all-reduce.38 = (f32[]{:T(128)}, f32[]{:T(128)}) all-reduce(f32[]{:T(128)} %get-tuple-element.16, f32[]{:T(128)} %get-tuple-element.17), channel_id=1, replica_groups=mesh['gx_0'=8,'gx_1'=2,'gx_2'=4,'gy_0'=2,'gy_1'=2] {'gy_0'}, use_global_device_ids=true, to_apply=%region_16.17 | all-reduce | flops 2 | bytes 16 | tf_op jit(solution)/shard_map/psum | solution.py:24
  163.6 12.2 %all-reduce.35 = (f32[]{:T(128)}, f32[]{:T(128)}) all-reduce(f32[]{:T(128)} %get-tuple-element.28, f32[]{:T(128)} %get-tuple-element.29), channel_id=1, replica_groups=mesh['gx_0'=8,'gx_1'=2,'gx_2'=4,'gy_0'=2,'gy_1'=2] {'gy_1'}, use_global_device_ids=true, to_apply=%region_17.18 | all-reduce | flops 2 | bytes 16 | tf_op jit(solution)/shard_map/psum | solution.py:24
  200.1 4.6 %reshape.36 = f32[24,32768]{1,0:T(8,128)} reshape(f32[8,3,8,32,128]{4,3,2,1,0:T(8,128)} %fusion.30) | data formatting | bytes 6291456 | tf_op jit(solution)/shard_map/reshape | solution.py:115
  204.7 4.7 %convolution_bitcast_fusion = f32[3,8,256,128]{3,1,2,0:T(8,128)S(1)} fusion(f32[24,24]{1,0:T(8,128)S(1)} %copy-done.5, f32[24,32768]{1,0:T(8,128)} %reshape.36), kind=kOutput, calls=%fused_computation.9 | convolution fusion | flops 226492416 | bytes 6293760 | tf_op jit(solution)/shard_map/dot_general | solution.py:117
  220.3 16.3 %all-reduce.28 = (f32[]{:T(128)}, f32[]{:T(128)}) all-reduce(f32[]{:T(128)} %get-tuple-element.3, f32[]{:T(128)} %get-tuple-element.2), channel_id=1, replica_groups=mesh['gx_0'=8,'gx_1'=2,'gx_2'=4,'gy_0'=2,'gy_1'=2] {'gx_0'}, use_global_device_ids=true, to_apply=%region_25.26 | all-reduce | flops 2 | bytes 16 | tf_op jit(solution)/shard_map/psum | solution.py:24
  236.6 4.6 %all-reduce.40 = (f32[]{:T(128)}, f32[]{:T(128)}) all-reduce(f32[]{:T(128)} %get-tuple-element.8, f32[]{:T(128)} %get-tuple-element.9), channel_id=1, replica_groups=mesh['gx_0'=8,'gx_1'=2,'gx_2'=4,'gy_0'=2,'gy_1'=2] {'gx_1'}, use_global_device_ids=true, to_apply=%region_26.27 | all-reduce | flops 2 | bytes 16 | tf_op jit(solution)/shard_map/psum | solution.py:24
  241.3 6.6 %all-reduce.31 = (f32[]{:T(128)}, f32[]{:T(128)}) all-reduce(f32[]{:T(128)} %get-tuple-element.32, f32[]{:T(128)} %get-tuple-element.33), channel_id=1, replica_groups=mesh['gx_0'=8,'gx_1'=2,'gx_2'=4,'gy_0'=2,'gy_1'=2] {'gx_2'}, use_global_device_ids=true, to_apply=%region_27.28 | all-reduce | flops 2 | bytes 16 | tf_op jit(solution)/shard_map/psum | solution.py:24
  247.9 5.9 %all-reduce.37 = (f32[]{:T(128)}, f32[]{:T(128)}) all-reduce(f32[]{:T(128)} %get-tuple-element.14, f32[]{:T(128)} %get-tuple-element.15), channel_id=1, replica_groups=mesh['gx_0'=8,'gx_1'=2,'gx_2'=4,'gy_0'=2,'gy_1'=2] {'gy_0'}, use_global_device_ids=true, to_apply=%region_28.29 | all-reduce | flops 2 | bytes 16 | tf_op jit(solution)/shard_map/psum | solution.py:24
  253.8 12.0 %all-reduce.34 = (f32[]{:T(128)}, f32[]{:T(128)}) all-reduce(f32[]{:T(128)} %get-tuple-element.26, f32[]{:T(128)} %get-tuple-element.27), channel_id=1, replica_groups=mesh['gx_0'=8,'gx_1'=2,'gx_2'=4,'gy_0'=2,'gy_1'=2] {'gy_1'}, use_global_device_ids=true, to_apply=%region_29.30 | all-reduce | flops 2 | bytes 16 | tf_op jit(solution)/shard_map/psum | solution.py:24
  271.8 4.8 %collective-permute-done.12 = f32[6,1,32,128]{3,2,1,0:T(8,128)S(1)} collective-permute-done((f32[6,1,32,128]{3,2,1,0:T(8,128)S(1)}, f32[6,1,32,128]{3,2,1,0:T(8,128)S(1)}, u32[]{:S(2)}, u32[]{:S(2)}) %collective-permute-start.12) | collective-permute-done | bytes 98336 | tf_op jit(solution)/shard_map/ppermute | solution.py:19
  291.2 4.6 %reshape.39 = f32[24,32768]{1,0:T(8,128)} reshape(f32[8,3,8,32,128]{4,3,2,1,0:T(8,128)} %get-tuple-element.68) | data formatting | bytes 6291456 | tf_op jit(solution)/shard_map/reshape | solution.py:187
  299.3 4.8 %reshape.38 = f32[24,32768]{1,0:T(8,128)} reshape(f32[8,3,8,32,128]{4,3,2,1,0:T(8,128)} %fusion.38) | data formatting | bytes 6291456 | tf_op jit(solution)/shard_map/reshape | solution.py:186
  304.1 5.0 %fusion = f32[32768]{0:T(1024)S(1)} fusion(f32[24,32768]{1,0:T(8,128)} %reshape.38, f32[24,24]{1,0:T(8,128)S(1)} %copy-done.5, f32[24,32768]{1,0:T(8,128)S(1)} %copy-done.2), kind=kOutput, calls=%fused_computation.27 | convolution fusion | flops 228032512 | bytes 6424832 | tf_op jit(solution)/shard_map/dot_general | solution.py:188
  (123 shorter events, 113.5 us)
Async XLA Ops:
  1.4 5.4 %collective-permute-start = (f32[3,1,32,128]{3,2,1,0:T(8,128)S(1)}, f32[3,1,32,128]{3,2,1,0:T(8,128)S(1)}, u32[]{:S(2)}, u32[]{:S(2)}) collective-permute-start(f32[3,1,32,128]{3,2,1,0:T(8,128)S(1)} %slice.322), channel_id=1, source_target_pairs={{4,0},{8,4},{12,8},{16,12},{20,16},{24,20},{28,24},{32,28},{36,32}... | collective-permute-start | bytes 147464 | tf_op jit(solution)/shard_map/ppermute | solution.py:19
  6.9 8.2 %collective-permute-start.1 = (f32[3,9,1,128]{3,2,1,0:T(1,128)S(1)}, f32[3,9,1,128]{3,2,1,0:T(1,128)S(1)}, u32[]{:S(2)}, u32[]{:S(2)}) collective-permute-start(f32[3,9,1,128]{3,2,1,0:T(1,128)S(1)} %slice.407), channel_id=1, source_target_pairs={{1,0},{2,1},{3,2},{5,4},{6,5},{7,6},{9,8},{10,9},{11,10},{13,12},{... | collective-permute-start | bytes 41480 | tf_op jit(solution)/shard_map/ppermute | solution.py:19
  21.1 2.9 copy-start.5
  28.3 8.4 %copy-start.3 = (f32[3,8,32,128]{3,2,1,0:T(8,128)S(1)}, f32[3,8,32,128]{3,2,1,0:T(8,128)}, u32[]{:S(2)}) copy-start(f32[3,8,32,128]{3,2,1,0:T(8,128)} %param.7) | copy-start | bytes 1179652
  29.4 3.1 collective-permute-start.2
  32.5 4.3 %collective-permute-start.3 = (f32[3,1,32,128]{3,2,1,0:T(8,128)S(1)}, f32[3,1,32,128]{3,2,1,0:T(8,128)S(1)}, u32[]{:S(2)}, u32[]{:S(2)}) collective-permute-start(f32[3,1,32,128]{3,2,1,0:T(8,128)S(1)} %pad_maximum_fusion.11), channel_id=1, source_target_pairs={{0,4},{4,8},{8,12},{12,16},{16,20},{20,24},{24,28},{28,32},{32,36}... | collective-permute-start | bytes 147464 | tf_op jit(solution)/shard_map/ppermute | solution.py:19
  91.8 5.1 %collective-permute-start.4 = (f32[3,1,32,128]{3,2,1,0:T(8,128)S(1)}, f32[3,1,32,128]{3,2,1,0:T(8,128)S(1)}, u32[]{:S(2)}, u32[]{:S(2)}) collective-permute-start(f32[3,1,32,128]{3,2,1,0:T(8,128)S(1)} %slice.424), channel_id=1, source_target_pairs={{4,0},{8,4},{12,8},{16,12},{20,16},{24,20},{28,24},{32,28},{36,32}... | collective-permute-start | bytes 147464 | tf_op jit(solution)/shard_map/ppermute | solution.py:19
  96.9 7.7 %collective-permute-start.5 = (f32[3,9,1,128]{3,2,1,0:T(1,128)S(1)}, f32[3,9,1,128]{3,2,1,0:T(1,128)S(1)}, u32[]{:S(2)}, u32[]{:S(2)}) collective-permute-start(f32[3,9,1,128]{3,2,1,0:T(1,128)S(1)} %pad_maximum_fusion.14), channel_id=1, source_target_pairs={{1,0},{2,1},{3,2},{5,4},{6,5},{7,6},{9,8},{10,9},{11,10},{13,12},{... | collective-permute-start | bytes 41480 | tf_op jit(solution)/shard_map/ppermute | solution.py:19
  122.5 3.1 collective-permute-start.6
  125.6 4.8 %collective-permute-start.7 = (f32[3,1,32,128]{3,2,1,0:T(8,128)S(1)}, f32[3,1,32,128]{3,2,1,0:T(8,128)S(1)}, u32[]{:S(2)}, u32[]{:S(2)}) collective-permute-start(f32[3,1,32,128]{3,2,1,0:T(8,128)S(1)} %pad_maximum_fusion.10), channel_id=1, source_target_pairs={{0,4},{4,8},{8,12},{12,16},{16,20},{20,24},{24,28},{28,32},{32,36}... | collective-permute-start | bytes 147464 | tf_op jit(solution)/shard_map/ppermute | solution.py:19
  181.2 4.8 %collective-permute-start.8 = (f32[3,1,32,128]{3,2,1,0:T(8,128)S(1)}, f32[3,1,32,128]{3,2,1,0:T(8,128)S(1)}, u32[]{:S(2)}, u32[]{:S(2)}) collective-permute-start(f32[3,1,32,128]{3,2,1,0:T(8,128)S(1)} %slice.438), channel_id=1, source_target_pairs={{4,0},{8,4},{12,8},{16,12},{20,16},{24,20},{28,24},{32,28},{36,32}... | collective-permute-start | bytes 147464 | tf_op jit(solution)/shard_map/ppermute | solution.py:19
  186.0 7.9 %collective-permute-start.9 = (f32[3,9,1,128]{3,2,1,0:T(1,128)S(1)}, f32[3,9,1,128]{3,2,1,0:T(1,128)S(1)}, u32[]{:S(2)}, u32[]{:S(2)}) collective-permute-start(f32[3,9,1,128]{3,2,1,0:T(1,128)S(1)} %pad_maximum_fusion.13), channel_id=1, source_target_pairs={{1,0},{2,1},{3,2},{5,4},{6,5},{7,6},{9,8},{10,9},{11,10},{13,12},{... | collective-permute-start | bytes 41480 | tf_op jit(solution)/shard_map/ppermute | solution.py:19
  211.8 58.6 %copy-start = (f32[3,8,32,128]{3,2,1,0:T(8,128)S(1)}, f32[3,8,32,128]{3,2,1,0:T(8,128)}, u32[]{:S(2)}) copy-start(f32[3,8,32,128]{3,2,1,0:T(8,128)} %param.9) | copy-start | bytes 1179652
  211.9 3.2 %collective-permute-start.10 = (f32[3,9,1,128]{3,2,1,0:T(1,128)S(1)}, f32[3,9,1,128]{3,2,1,0:T(1,128)S(1)}, u32[]{:S(2)}, u32[]{:S(2)}) collective-permute-start(f32[3,9,1,128]{3,2,1,0:T(1,128)S(1)} %slice.450), channel_id=1, source_target_pairs={{0,1},{1,2},{2,3},{4,5},{5,6},{6,7},{8,9},{9,10},{10,11},{12,13},{... | collective-permute-start | bytes 41480 | tf_op jit(solution)/shard_map/ppermute | solution.py:19
  215.1 4.4 %collective-permute-start.11 = (f32[3,1,32,128]{3,2,1,0:T(8,128)S(1)}, f32[3,1,32,128]{3,2,1,0:T(8,128)S(1)}, u32[]{:S(2)}, u32[]{:S(2)}) collective-permute-start(f32[3,1,32,128]{3,2,1,0:T(8,128)S(1)} %pad_maximum_fusion.9), channel_id=1, source_target_pairs={{0,4},{4,8},{8,12},{12,16},{16,20},{20,24},{24,28},{28,32},{32,36}... | collective-permute-start | bytes 147464 | tf_op jit(solution)/shard_map/ppermute | solution.py:19
  270.5 25.4 %copy-start.1 = (f32[3,8,32,128]{3,2,1,0:T(8,128)}, f32[3,8,32,128]{3,2,1,0:T(8,128)S(1)}, u32[]{:S(2)}) copy-start(f32[3,8,32,128]{3,2,1,0:T(8,128)S(1)} %get-tuple-element.39) | copy-start | bytes 1179652
  270.5 6.1 %collective-permute-start.12 = (f32[6,1,32,128]{3,2,1,0:T(8,128)S(1)}, f32[6,1,32,128]{3,2,1,0:T(8,128)S(1)}, u32[]{:S(2)}, u32[]{:S(2)}) collective-permute-start(f32[6,1,32,128]{3,2,1,0:T(8,128)S(1)} %pad_maximum_fusion.8), channel_id=1, source_target_pairs={{4,0},{8,4},{12,8},{16,12},{20,16},{24,20},{28,24},{32,28},{36,32}... | collective-permute-start | bytes 294920 | tf_op jit(solution)/shard_map/ppermute | solution.py:19
  276.6 7.7 %collective-permute-start.13 = (f32[6,9,1,128]{3,2,1,0:T(1,128)S(1)}, f32[6,9,1,128]{3,2,1,0:T(1,128)S(1)}, u32[]{:S(2)}, u32[]{:S(2)}) collective-permute-start(f32[6,9,1,128]{3,2,1,0:T(1,128)S(1)} %pad_maximum_fusion.12), channel_id=1, source_target_pairs={{1,0},{2,1},{3,2},{5,4},{6,5},{7,6},{9,8},{10,9},{11,10},{13,12},{... | collective-permute-start | bytes 82952 | tf_op jit(solution)/shard_map/ppermute | solution.py:19
  299.3 4.8 %copy-start.2 = (f32[24,32768]{1,0:T(8,128)S(1)}, f32[24,32768]{1,0:T(8,128)}, u32[]{:S(2)}) copy-start(f32[24,32768]{1,0:T(8,128)} %reshape.39) | copy-start | bytes 9437188
  304.1 5.0 %copy-start.4 = (f32[8,32,128]{2,1,0:T(8,128)S(1)}, f32[8,32,128]{2,1,0:T(8,128)}, u32[]{:S(2)}) copy-start(f32[8,32,128]{2,1,0:T(8,128)} %param.8) | copy-start | bytes 393220
where the time goes:
time: 312 us; the launch traced here: 310 us
  blocking collectives  142 us (46%)
  local copies, waits for them, and re-layouts  52.8 us (17%)
  starting transfers between devices  36.7 us (12%)
  waiting for transfers between devices  34.3 us (11%)
  matrix products  17.1 us (5%)
  other arithmetic  16.3 us (5%)
  between operations  10.7 us (3%)
    psum x15, blocking collectives, over_axes(): x = lax.psum(x, axis)  142 us
    ppermute x14, starting transfers between devices, passed_along(): return lax.ppermute(x, axis, pairs)  36.7 us
    ppermute x14, waiting for transfers between devices, passed_along(): return lax.ppermute(x, axis, pairs)  34.3 us
    unnamed x39, local copies, waits for them, and re-layouts  24.1 us
    reshape x3, local copies, waits for them, and re-layouts, element_forces(): stacked = corner_stack(padded, count_x, count_y, count_z).reshape(24, -1)  12.2 us
    dot_general x3, matrix products, element_forces(): jnp.dot(table, stacked, precision=lax.Precision.HIGHEST, preferred_elemen...  12.1 us
    unnamed x9, other arithmetic  7.31 us
  transfers between devices with their start and end apart: 14, of which 14 were waited for; matrix products, arithmetic and copies ran while one was open for 2% of the time, Pallas kernels for 0%

commit v1 on v0

v1 whole, which is shorter than its diff:
```python
import jax
import jax.numpy as jnp
from jax import lax
from jax.experimental import pallas as pl
from jax.experimental.pallas import tpu as pltpu
from jax.sharding import PartitionSpec as P

CX, CY, CZ = 8, 32, 128
ROWS = 40
AXES = ("gx", "gy")
LAM = 3.0 * 0.3 / (1.3 * 0.4)
MU = 3.0 / 2.6
F32 = jnp.float32


def exchange(x, axis, first):
    n = lax.axis_size(axis)
    pairs = []
    for i in range(first, n - 1, 2):
        pairs += [(i, i + 1), (i + 1, i)]
    return lax.ppermute(x, axis, pairs)


def iota(shape, dim):
    return lax.broadcasted_iota(jnp.int32, shape, dim)


def degradation_of(damage):
    return (1.0 - damage) * (1.0 - damage) + 0.001


def pack_y(b_lo, b_hi, h_lo, h_hi, u_lo, out_a, out_b):
    row = iota((CX, 8, CZ), 1)
    g_lo, g_hi = degradation_of(h_lo[...]), degradation_of(h_hi[...])
    up = lambda x, k: pltpu.roll(x, k % 8, 1)
    low_1 = jnp.where(row < 3, b_lo[0], jnp.where(row < 6, up(b_lo[1], 3), up(g_lo, 6)))
    low_2 = jnp.where(
        row < 3,
        b_lo[2],
        jnp.where(
            row == 3, up(u_lo[0], 3), jnp.where(row == 4, up(u_lo[1], 4), up(u_lo[2], 5))
        ),
    )
    high = jnp.where(
        row < 2,
        up(b_hi[0], 2),
        jnp.where(row < 4, up(b_hi[1], 4), jnp.where(row < 6, up(b_hi[2], 6), g_hi)),
    )
    odd = lax.rem(lax.axis_index("gy"), 2) == 1

    @pl.when(odd)
    def _():
        out_a[0], out_a[1] = low_1, low_2
        out_b[0], out_b[1] = high, high

    @pl.when(jnp.logical_not(odd))
    def _():
        out_a[0], out_a[1] = high, high
        out_b[0], out_b[1] = low_1, low_2


def pack_x(y_a, y_b, b_ref, h_ref, u_ref, out_a, out_b, halo):
    odd_y = lax.rem(lax.axis_index("gy"), 2) == 1
    row = iota((CX, 8, CZ), 1)
    up = lambda x, k: pltpu.roll(x, k % 8, 1)
    above_1 = jnp.where(odd_y, y_b[0], y_a[0])
    above_2 = jnp.where(odd_y, y_b[1], y_a[1])
    below = jnp.where(odd_y, y_a[0], y_b[0])

    def tile(head, count, tail):
        return jnp.where(row < count, head, jnp.where(row >= 6, tail, 0.0))

    halo[0] = tile(above_1, 3, up(below, 6))
    halo[1] = tile(up(above_1, -3), 3, up(below, 4))
    halo[2] = tile(above_2, 3, up(below, 2))
    halo[3] = tile(up(above_1, -6), 2, below)
    for c in range(3):
        halo[4 + c] = jnp.where(row < 1, up(above_2, -3 - c), 0.0)
    odd_x = lax.rem(lax.axis_index("gx"), 2) == 1

    def low(out):
        for c in range(3):
            for x in range(3):
                out[3 * c + x, :CY], out[3 * c + x, CY:] = b_ref[c, x], halo[c, x]
            out[11 + c, :CY], out[11 + c, CY:] = u_ref[c, 0], halo[4 + c, 0]
        for x in range(2):
            out[9 + x, :CY], out[9 + x, CY:] = degradation_of(h_ref[x]), halo[3, x]

    def high(out):
        for c in range(3):
            for x in range(2):
                out[3 * c + x, :CY], out[3 * c + x, CY:] = b_ref[c, 6 + x], halo[c, 6 + x]
            out[3 * c + 2] = jnp.zeros((ROWS, CZ), F32)
            out[11 + c] = jnp.zeros((ROWS, CZ), F32)
        for x in range(2):
            out[9 + x, :CY], out[9 + x, CY:] = degradation_of(h_ref[6 + x]), halo[3, 6 + x]

    @pl.when(odd_x)
    def _():
        low(out_a)
        high(out_b)

    @pl.when(jnp.logical_not(odd_x))
    def _():
        high(out_a)
        low(out_b)


def yz_modes(u):
    lane = iota((ROWS, CZ), 1)
    u_next = jnp.where(lane == CZ - 1, 0.0, pltpu.roll(u, CZ - 1, 1))
    out = [None] * 4
    for z, a in enumerate((u + u_next, u_next - u)):
        a_next = pltpu.roll(a, ROWS - 1, 0)
        out[z], out[2 + z] = a + a_next, a_next - a
    return out


def yz_gather(r):
    lane = iota((ROWS, CZ), 1)
    rows = []
    for z in range(2):
        s, d = r[z], r[2 + z]
        rows.append((s - d) + pltpu.roll(s + d, 1, 0))
    s, d = rows
    return (s - d) + jnp.where(lane == 0, 0.0, pltpu.roll(s + d, 1, 1))


SS, SD, DS, DD = 0, 1, 2, 3


def strains(here, there):
    s = [[here[4 * c + k] + there[4 * c + k] if k else None for k in range(4)] for c in range(3)]
    d = [[there[4 * c + k] - here[4 * c + k] for k in range(4)] for c in range(3)]
    u, v, w = range(3)
    return [
        d[u][SS], s[v][DS], s[w][SD],
        s[u][DS] + d[v][SS], s[u][SD] + d[w][SS], s[v][SD] + s[w][DS],
        s[u][DD], d[v][SD], d[w][DS],
        d[u][SD], s[v][DD], d[u][DS], s[w][DD], d[v][DS], d[w][SD],
        d[u][DD], d[v][DD], d[w][DD],
    ]


def stresses(e, g):
    scaled = (lambda k: g * k) if g is not None else (lambda k: k)
    l16, m8, m16, m48 = scaled(LAM / 16), scaled(MU / 8), scaled(MU / 16), scaled(MU / 48)
    l48, q = scaled(LAM / 48), scaled((LAM + 4 * MU) / 144)
    trace = l16 * (e[0] + e[1] + e[2])
    out = [trace + m8 * e[k] for k in range(3)]
    out += [m16 * e[k] for k in range(3, 6)]
    three = e[6] + e[7] + e[8]
    out += [m48 * (e[k] + three) for k in range(6, 9)]
    for k in (9, 11, 13):
        both = l48 * (e[k] + e[k + 1])
        out += [both + m16 * e[k], both + m16 * e[k + 1]]
    return out + [q * e[k] for k in range(15, 18)]


def x_forces(f):
    s = [[None, f[4], f[3], f[6]], [None, f[5], f[1], f[10]], [None, f[2], f[5], f[12]]]
    d = [[f[0], f[9], f[11], f[15]], [f[3], f[7], f[13], f[16]], [f[4], f[14], f[8], f[17]]]
    return [x for c in s for x in c], [x for c in d for x in c]


def inner(a, b):
    total = a[0] * b[0]
    for x, y in zip(a[1:], b[1:]):
        total = total + x * y
    return total


def main_kernel(
    b_ref, h_ref, u_ref, halo, x_a, x_b, p1_out, p2_out, t_out, row_out,
    field, g_ref, p1, p2, modes, gathered, moved, weights, sums,
):
    odd_x = lax.rem(lax.axis_index("gx"), 2) == 1
    not_last_x = jnp.where(lax.axis_index("gx") == lax.axis_size("gx") - 1, 0.0, 1.0).astype(F32)
    not_last_y = jnp.where(lax.axis_index("gy") == lax.axis_size("gy") - 1, 0.0, 1.0).astype(F32)
    row = iota((ROWS, CZ), 0)
    keep = jnp.where(jnp.logical_and(row >= CY, row < CY + 3), not_last_y, 1.0)

    def place(above, below):
        for c in range(3):
            for x in range(2):
                field[c, x] = below[3 * c + x]
            for x in range(3):
                field[c, 10 + x] = above[3 * c + x]
            moved[c, CX] = above[11 + c]
        for x in range(2):
            g_ref[x] = below[9 + x]
            g_ref[10 + x] = above[9 + x]

    @pl.when(odd_x)
    def _():
        place(x_b, x_a)

    @pl.when(jnp.logical_not(odd_x))
    def _():
        place(x_a, x_b)

    for c in range(3):
        field[c, 2:10, :CY] = b_ref[c]
        field[c, 2:10, CY:] = halo[c]
        moved[c, :CX, :CY] = u_ref[c]
        moved[c, :CX, CY:] = halo[4 + c]
    g_ref[2:10, :CY] = degradation_of(h_ref[...])
    g_ref[2:10, CY:] = halo[3]
    sums[...] = jnp.zeros_like(sums)

    def to_modes(source, layers):
        @pl.loop(0, layers)
        def _(n):
            for c in range(3):
                for k, a in enumerate(yz_modes(source[c, n])):
                    modes[4 * c + k, n] = a

    def load(n, rows):
        return [modes[k, n, rows, :] for k in range(12)]

    to_modes(moved, CX + 1)

    @pl.loop(0, CY // 8)
    def _(j):
        rows = pl.ds(pl.multiple_of(8 * j, 8), 8)
        here = load(0, rows)
        for e in range(CX):
            there = load(e + 1, rows)
            for k, f in enumerate(stresses(strains(here, there), None)):
                weights[k, e, rows, :] = f
            here = there

    def stress_gather(layers, g_first, own_first, power):
        def chunk(rows, own):
            here = load(0, rows)
            before = None
            for e in range(layers):
                there = load(e + 1, rows)
                strain = strains(here, there)
                x = e - own_first
                if own and 0 <= x < CX:
                    stiff = [weights[k, x, rows, :] for k in range(18)]
                    t_out[power, x, rows, :] = inner(strain, stiff)
                s, d = x_forces(stresses(strain, g_ref[g_first + e, rows, :]))
                if before is not None:
                    for k in range(12):
                        lower = s[k] - d[k] if s[k] is not None else -d[k]
                        gathered[k, e - 1, rows, :] = before[k] + lower
                before = [s[k] + d[k] if s[k] is not None else d[k] for k in range(12)]
                here = there

        @pl.loop(0, CY // 8)
        def _(j):
            chunk(pl.ds(pl.multiple_of(8 * j, 8), 8), True)

        chunk(pl.ds(CY, 8), False)

    def collapse(x):
        return x[0:8] + x[8:16] + x[16:24] + x[24:32]

    def nodes(layers, target, past_end):
        @pl.loop(0, layers)
        def _(n):
            factor = keep * jnp.where(n >= past_end, not_last_x, 1.0)
            for c in range(3):
                target[c, n] = factor * yz_gather([gathered[4 * c + k, n] for k in range(4)])

    to_modes(field, 13)
    stress_gather(12, 0, 2, 0)
    nodes(11, p1, 9)
    to_modes(p1, 11)
    stress_gather(10, 1, 1, 1)
    nodes(9, p2, 8)

    @pl.loop(0, CX)
    def _(x):
        for c in range(3):
            v0, v1, v2 = b_ref[c, x], p1[c, x + 1, :CY], p2[c, x, :CY]
            p1_out[c, x] = v1
            p2_out[c, x] = v2
            for k, (a, b) in enumerate(((v0, v0), (v0, v1), (v1, v1), (v1, v2), (v2, v2))):
                sums[k] += collapse(a * b)

    to_modes(p2, 9)

    @pl.loop(0, CY // 8)
    def _(j):
        rows = pl.ds(pl.multiple_of(8 * j, 8), 8)
        here = load(0, rows)
        total = jnp.zeros((8, CZ), F32)
        for e in range(CX):
            there = load(e + 1, rows)
            strain = strains(here, there)
            t_out[2, e, rows, :] = inner(strain, [weights[k, e, rows, :] for k in range(18)])
            total = total + inner(strain, stresses(strain, g_ref[2 + e, rows, :]))
            here = there
        sums[5] += total

    lane = iota((1, CZ), 1)
    line = jnp.zeros((1, CZ), F32)
    for k in range(6):
        line = jnp.where(lane == k, jnp.sum(jnp.sum(sums[k], 0, keepdims=True), 1, keepdims=True), line)
    row_out[...] = jnp.broadcast_to(line, row_out.shape)


def combine(parts, b_ref, p1, p2, t_ref, h_ref, adjoint, sensitivity):
    line = jnp.sum(parts[...], 0, keepdims=True)
    lane = iota((1, CZ), 1)
    m = [jnp.sum(jnp.where(lane == k, line, 0.0), 1, keepdims=True) for k in range(6)]
    l10, l20 = m[2] / m[1], m[3] / m[1]
    d1, h21 = m[3] - l10 * m[2], m[4] - l20 * m[2]
    l21 = h21 / d1
    d2 = m[5] - l20 * m[3] - l21 * h21
    y1 = m[1] - l10 * m[0]
    y2 = m[2] - l20 * m[0] - l21 * y1
    c2 = y2 / d2
    c1 = y1 / d1 - l21 * c2
    c0 = m[0] / m[1] - l10 * c1 - l20 * c2
    c0, c1, c2 = [jnp.broadcast_to(c, (CY, CZ)) for c in (c0, c1, c2)]
    for x in range(CX):
        for c in range(3):
            adjoint[c, x] = c0 * b_ref[c, x] + c1 * p1[c, x] + c2 * p2[c, x]
        product = c0 * t_ref[0, x] + c1 * t_ref[1, x] + c2 * t_ref[2, x]
        sensitivity[x] = 2.0 * (1.0 - h_ref[x]) * product


VMEM = pl.BlockSpec(memory_space=pltpu.VMEM)


def shape(*dims):
    return jax.ShapeDtypeStruct(dims, F32)


def body(misfit, damage, displacement):
    edge = (3, CX, 8, CZ)
    first = lambda i: (0, 0, 0, 0)
    last = lambda i: (0, 0, 3, 0)
    y_a, y_b = pl.pallas_call(
        pack_y,
        grid=(1,),
        in_specs=[
            pl.BlockSpec(edge, first),
            pl.BlockSpec(edge, last),
            pl.BlockSpec(edge[1:], lambda i: (0, 0, 0)),
            pl.BlockSpec(edge[1:], lambda i: (0, 3, 0)),
            pl.BlockSpec(edge, first),
        ],
        out_specs=[pl.BlockSpec((2, CX, 8, CZ), first)] * 2,
        out_shape=[shape(2, CX, 8, CZ)] * 2,
        name="pack_y",
    )(misfit, misfit, damage, damage, displacement)
    y_a = exchange(y_a, "gy", 0)
    y_b = exchange(y_b, "gy", 1)
    x_a, x_b, halo = pl.pallas_call(
        pack_x,
        in_specs=[VMEM] * 5,
        out_specs=[VMEM] * 3,
        out_shape=[shape(14, ROWS, CZ)] * 2 + [shape(7, CX, 8, CZ)],
        name="pack_x",
    )(y_a, y_b, misfit, damage, displacement)
    x_a = exchange(x_a, "gx", 0)
    x_b = exchange(x_b, "gx", 1)
    devices = lax.axis_size("gx") * lax.axis_size("gy")
    p1, p2, t, line = pl.pallas_call(
        main_kernel,
        in_specs=[VMEM] * 6,
        out_specs=[VMEM] * 4,
        out_shape=[shape(3, CX, CY, CZ)] * 3 + [shape(devices, CZ)],
        scratch_shapes=[
            pltpu.VMEM((3, 13, ROWS, CZ), F32),
            pltpu.VMEM((12, ROWS, CZ), F32),
            pltpu.VMEM((3, 11, ROWS, CZ), F32),
            pltpu.VMEM((3, 9, ROWS, CZ), F32),
            pltpu.VMEM((12, 13, ROWS, CZ), F32),
            pltpu.VMEM((12, 11, ROWS, CZ), F32),
            pltpu.VMEM((3, 9, ROWS, CZ), F32),
            pltpu.VMEM((18, CX, CY, CZ), F32),
            pltpu.VMEM((6, 8, CZ), F32),
        ],
        name="main",
    )(misfit, damage, displacement, halo, x_a, x_b)
    parts = lax.all_to_all(line, AXES, 0, 0, tiled=True)
    return pl.pallas_call(
        combine,
        in_specs=[VMEM] * 6,
        out_specs=[VMEM] * 2,
        out_shape=[shape(3, CX, CY, CZ), shape(CX, CY, CZ)],
        name="combine",
    )(parts, misfit, p1, p2, t, damage)


def solution(mesh):
    field, scalar = P(None, "gx", "gy", None), P("gx", "gy", None)
    return jax.shard_map(
        body, mesh=mesh, in_specs=(field, scalar, field), out_specs=(field, scalar), check_vma=False
    )
```

time: 312 us -> 69.2 us (0.22)
  blocking collectives: 142 us -> 32.4 us
  local copies, waits for them, and re-layouts: 52.8 us -> 1.42 us
  starting transfers between devices: 36.7 us -> 6.86 us
  waiting for transfers between devices: 34.3 us -> 9.29 us
  Pallas kernels: 0 us -> 18.2 us
  matrix products: 17.1 us -> 0 us
  other arithmetic: 16.3 us -> 0 us
  between operations: 10.7 us -> 0.67 us
    psum x15 -> x0, blocking collectives: 142 us -> none  [over_axes(): x = lax.psum(x, axis)]
    all_to_all x0 -> x1, blocking collectives: none -> 32.4 us  [body(): parts = lax.all_to_all(line, AXES, 0, 0, tiled=True)]
    ppermute x14 -> x4, starting transfers between devices: 36.7 us -> 6.86 us  [exchange(): return lax.ppermute(x, axis, pairs)]
    ppermute x14 -> x4, waiting for transfers between devices: 34.3 us -> 9.29 us  [exchange(): return lax.ppermute(x, axis, pairs)]
    unnamed x39 -> x8, local copies, waits for them, and re-layouts: 24.1 us -> 1.42 us
    reshape x5 -> x0, local copies, waits for them, and re-layouts: 21.7 us -> none  [the longest x3 12.2 us: element_forces(): stacked = corner_stack(padded, count_x, count_y, count_z).reshape(24, -1)]
    pallas_call x0 -> x4, Pallas kernels: none -> 18.2 us  [the longest x1 11.8 us: body(): pl.pallas_call(main_kernel, in_specs=[VMEM] * 6, out_specs=[VMEM] * 4, ou...]
    dot_general x4 -> x0, matrix products: 17.1 us -> none  [the longest x3 12.1 us: element_forces(): jnp.dot(table, stacked, precision=lax.Precision.HIGHEST, preferred_elemen...]
  transfers between devices with their start and end apart: 14 -> 4, of which waited for: 14 -> 2; matrix products, arithmetic and copies ran while one was open for 2% -> 0% of each run, Pallas kernels for 0% -> 0%
where the time goes in v1:
time: 69.2 us; the launch traced here: 68.9 us
  blocking collectives  32.4 us (47%)
  Pallas kernels  18.2 us (26%)
  waiting for transfers between devices  9.29 us (13%)
  starting transfers between devices  6.86 us (10%)
  local copies, waits for them, and re-layouts  1.42 us (2%)
    all_to_all x1, blocking collectives, body(): parts = lax.all_to_all(line, AXES, 0, 0, tiled=True)  32.4 us
    pallas_call x1, Pallas kernels, body(): pl.pallas_call(main_kernel, in_specs=[VMEM] * 6, out_specs=[VMEM] * 4, ou...  11.8 us
    ppermute x4, waiting for transfers between devices, exchange(): return lax.ppermute(x, axis, pairs)  9.29 us
    ppermute x4, starting transfers between devices, exchange(): return lax.ppermute(x, axis, pairs)  6.86 us
    pallas_call x1, Pallas kernels, body(): pl.pallas_call(combine, in_specs=[VMEM] * 6, out_specs=[VMEM] * 2, out_sh...  2.44 us
    pallas_call x1, Pallas kernels, body(): pl.pallas_call(pack_x, in_specs=[VMEM] * 5, out_specs=[VMEM] * 3, out_sha...  2.19 us
    pallas_call x1, Pallas kernels, body(): pl.pallas_call(pack_y, grid=(1,), in_specs=[pl.BlockSpec(edge, first), pl...  1.72 us
    unnamed x8, local copies, waits for them, and re-layouts  1.42 us
  transfers between devices with their start and end apart: 4, of which 2 were waited for; matrix products, arithmetic and copies ran while one was open for 0% of the time, Pallas kernels for 0%

profile of v1, /device:TPU:1, one launch (start us, length us, event | category | flops | bytes accessed | tf_op | source)
XLA Modules:
  0.0 68.9 jit_solution(14185486004627798770)
XLA Ops:
  0.6 1.7 %pack_y.1 = (f32[2,8,8,128]{3,2,1,0:T(8,128)}, f32[2,8,8,128]{3,2,1,0:T(8,128)}) custom-call(f32[3,8,32,128]{3,2,1,0:T(8,128)} %b_ref.5, f32[3,8,32,128]{3,2,1,0:T(8,128)} %b_ref.5, f32[8,32,128]{2,1,0:T(8,128)} %h_ref.5, f32[8,32,128]{2,1,0:T(8,128)} %h_ref.5, f32[3,8,32,128]{3,2,1,0:T(8,128)} %u_ref.3), custom_call_target="tpu_custom_call" | custom-call | tf_op jit(solution)/shard_map/pack_y/pallas_call | solution.py:338
  2.3 3.2 %collective-permute-start = (f32[2,8,8,128]{3,2,1,0:T(8,128)}, f32[2,8,8,128]{3,2,1,0:T(8,128)S(1)}, u32[]{:S(2)}, u32[]{:S(2)}) collective-permute-start(f32[2,8,8,128]{3,2,1,0:T(8,128)} %get-tuple-element.11), channel_id=1, source_target_pairs={{0,1},{1,0},{2,3},{3,2},{4,5},{5,4},{6,7},{7,6},{8,9},{9,8},{10,11... | collective-permute-start | bytes 196616 | tf_op jit(solution)/shard_map/ppermute | solution.py:21
  5.6 3.0 %collective-permute-start.1 = (f32[2,8,8,128]{3,2,1,0:T(8,128)}, f32[2,8,8,128]{3,2,1,0:T(8,128)S(1)}, u32[]{:S(2)}, u32[]{:S(2)}) collective-permute-start(f32[2,8,8,128]{3,2,1,0:T(8,128)} %get-tuple-element.12), channel_id=1, source_target_pairs={{1,2},{2,1},{5,6},{6,5},{9,10},{10,9},{13,14},{14,13},{17,18},{18,... | collective-permute-start | bytes 196616 | tf_op jit(solution)/shard_map/ppermute | solution.py:21
  8.6 0.0 collective-permute-done.y_a
  8.6 0.0 copy-start.2
  8.6 4.3 %collective-permute-done.1.y_b = f32[2,8,8,128]{3,2,1,0:T(8,128)S(1)} collective-permute-done((f32[2,8,8,128]{3,2,1,0:T(8,128)}, f32[2,8,8,128]{3,2,1,0:T(8,128)S(1)}, u32[]{:S(2)}, u32[]{:S(2)}) %collective-permute-start.1) | collective-permute-done | bytes 65568 | tf_op jit(solution)/shard_map/ppermute | solution.py:21
  12.8 0.0 copy-done.2
  12.8 0.0 copy-start.3
  12.8 0.6 copy-done.3
  13.5 2.2 %pack_x.1 = (f32[14,40,128]{2,1,0:T(8,128)}, f32[14,40,128]{2,1,0:T(8,128)}, f32[7,8,8,128]{3,2,1,0:T(8,128)}) custom-call(f32[2,8,8,128]{3,2,1,0:T(8,128)} %copy-done.2, f32[2,8,8,128]{3,2,1,0:T(8,128)} %copy-done.3, f32[3,8,32,128]{3,2,1,0:T(8,128)} %b_ref.5, f32[8,32,128]{2,1,0:T(8,128)} %h_ref.5, f32[3,8,32,128]{3,2,1,0:T(8,128)} %u_ref.3), custom_call_target="tpu_custom_call" | custom-call | tf_op jit(solution)/shard_map/pack_x/pallas_call | solution.py:354
  15.7 0.0 collective-permute-start.2
  15.7 0.7 collective-permute-start.3
  16.3 5.0 %collective-permute-done.2.x_a = f32[14,40,128]{2,1,0:T(8,128)S(1)} collective-permute-done((f32[14,40,128]{2,1,0:T(8,128)}, f32[14,40,128]{2,1,0:T(8,128)S(1)}, u32[]{:S(2)}, u32[]{:S(2)}) %collective-permute-start.2) | collective-permute-done | bytes 286752 | tf_op jit(solution)/shard_map/ppermute | solution.py:21
  21.3 0.0 copy-start
  21.4 0.0 collective-permute-done.3.x_b
  21.4 0.0 copy-start.1
  21.4 0.7 %copy-done = f32[14,40,128]{2,1,0:T(8,128)} copy-done((f32[14,40,128]{2,1,0:T(8,128)}, f32[14,40,128]{2,1,0:T(8,128)S(1)}, u32[]{:S(2)}) %copy-start) | copy-done | bytes 286744
  22.1 0.1 copy-done.1
  22.1 11.8 %main.1 = (f32[3,8,32,128]{3,2,1,0:T(8,128)}, f32[3,8,32,128]{3,2,1,0:T(8,128)}, f32[3,8,32,128]{3,2,1,0:T(8,128)}, f32[256,128]{1,0:T(8,128)}) custom-call(f32[3,8,32,128]{3,2,1,0:T(8,128)} %b_ref.5, f32[8,32,128]{2,1,0:T(8,128)} %h_ref.5, f32[3,8,32,128]{3,2,1,0:T(8,128)} %u_ref.3, f32[7,8,8,128]{3,2,1,0:T(8,128)} %get-tuple-element.13.halo, ...), custom_call_target="tpu_custom_call" | custom-call | tf_op jit(solution)/shard_map/main/pallas_call | solution.py:364
  34.0 32.4 %all_to_all.11 = f32[256,1,128]{2,1,0:T(1,128)} all-to-all(f32[256,1,128]{2,1,0:T(1,128)} %bitcast.5), channel_id=1, replica_groups=mesh['gx'=64,'gy'=4] {'gx','gy'}, dimensions={0} | all-to-all | bytes 262144 | tf_op jit(solution)/shard_map/all_to_all | solution.py:382
  66.4 2.4 %combine.1 = (f32[3,8,32,128]{3,2,1,0:T(8,128)}, f32[8,32,128]{2,1,0:T(8,128)}) custom-call(f32[256,128]{1,0:T(8,128)} %bitcast.4, f32[3,8,32,128]{3,2,1,0:T(8,128)} %b_ref.5, f32[3,8,32,128]{3,2,1,0:T(8,128)} %get-tuple-element.17.p1, f32[3,8,32,128]{3,2,1,0:T(8,128)} %get-tuple-element.18.p2, f32[3,8,32,128]{3,2,1,0:T(8,128)} %get-tuple-element.19.t_ref, ...), custom_call_target="tpu_custom_call" | custom-call | tf_op jit(solution)/shard_map/combine/pallas_call | solution.py:383
Async XLA Ops:
  2.3 6.2 %collective-permute-start = (f32[2,8,8,128]{3,2,1,0:T(8,128)}, f32[2,8,8,128]{3,2,1,0:T(8,128)S(1)}, u32[]{:S(2)}, u32[]{:S(2)}) collective-permute-start(f32[2,8,8,128]{3,2,1,0:T(8,128)} %get-tuple-element.11), channel_id=1, source_target_pairs={{0,1},{1,0},{2,3},{3,2},{4,5},{5,4},{6,7},{7,6},{8,9},{9,8},{10,11... | collective-permute-start | bytes 196616 | tf_op jit(solution)/shard_map/ppermute | solution.py:21
  5.6 7.3 %collective-permute-start.1 = (f32[2,8,8,128]{3,2,1,0:T(8,128)}, f32[2,8,8,128]{3,2,1,0:T(8,128)S(1)}, u32[]{:S(2)}, u32[]{:S(2)}) collective-permute-start(f32[2,8,8,128]{3,2,1,0:T(8,128)} %get-tuple-element.12), channel_id=1, source_target_pairs={{1,2},{2,1},{5,6},{6,5},{9,10},{10,9},{13,14},{14,13},{17,18},{18,... | collective-permute-start | bytes 196616 | tf_op jit(solution)/shard_map/ppermute | solution.py:21
  8.6 4.3 %copy-start.2 = (f32[2,8,8,128]{3,2,1,0:T(8,128)}, f32[2,8,8,128]{3,2,1,0:T(8,128)S(1)}, u32[]{:S(2)}) copy-start(f32[2,8,8,128]{3,2,1,0:T(8,128)S(1)} %collective-permute-done.y_a) | copy-start | bytes 196612
  12.8 0.6 copy-start.3
  15.7 5.7 %collective-permute-start.2 = (f32[14,40,128]{2,1,0:T(8,128)}, f32[14,40,128]{2,1,0:T(8,128)S(1)}, u32[]{:S(2)}, u32[]{:S(2)}) collective-permute-start(f32[14,40,128]{2,1,0:T(8,128)} %get-tuple-element.14), channel_id=1, source_target_pairs={{0,4},{4,0},{8,12},{12,8},{16,20},{20,16},{24,28},{28,24},{32,36},... | collective-permute-start | bytes 860168 | tf_op jit(solution)/shard_map/ppermute | solution.py:21
  15.7 5.7 %collective-permute-start.3 = (f32[14,40,128]{2,1,0:T(8,128)}, f32[14,40,128]{2,1,0:T(8,128)S(1)}, u32[]{:S(2)}, u32[]{:S(2)}) collective-permute-start(f32[14,40,128]{2,1,0:T(8,128)} %get-tuple-element.15), channel_id=1, source_target_pairs={{4,8},{8,4},{12,16},{16,12},{20,24},{24,20},{28,32},{32,28},{36,40... | collective-permute-start | bytes 860168 | tf_op jit(solution)/shard_map/ppermute | solution.py:21
  21.3 0.7 %copy-start = (f32[14,40,128]{2,1,0:T(8,128)}, f32[14,40,128]{2,1,0:T(8,128)S(1)}, u32[]{:S(2)}) copy-start(f32[14,40,128]{2,1,0:T(8,128)S(1)} %collective-permute-done.2.x_a) | copy-start | bytes 860164
  21.4 0.8 %copy-start.1 = (f32[14,40,128]{2,1,0:T(8,128)}, f32[14,40,128]{2,1,0:T(8,128)S(1)}, u32[]{:S(2)}) copy-start(f32[14,40,128]{2,1,0:T(8,128)S(1)} %collective-permute-done.3.x_b) | copy-start | bytes 860164

commit v2 on v1

--- a/solution.py
+++ b/solution.py
@@ -348,6 +348,7 @@
         out_specs=[pl.BlockSpec((2, CX, 8, CZ), first)] * 2,
         out_shape=[shape(2, CX, 8, CZ)] * 2,
         name="pack_y",
+        compiler_params=pltpu.CompilerParams(vmem_limit_bytes=4 << 20),
     )(misfit, misfit, damage, damage, displacement)
     y_a = exchange(y_a, "gy", 0)
     y_b = exchange(y_b, "gy", 1)
@@ -357,6 +358,7 @@
         out_specs=[VMEM] * 3,
         out_shape=[shape(14, ROWS, CZ)] * 2 + [shape(7, CX, 8, CZ)],
         name="pack_x",
+        compiler_params=pltpu.CompilerParams(vmem_limit_bytes=8 << 20),
     )(y_a, y_b, misfit, damage, displacement)
     x_a = exchange(x_a, "gx", 0)
     x_b = exchange(x_b, "gx", 1)
@@ -378,6 +380,7 @@
             pltpu.VMEM((6, 8, CZ), F32),
         ],
         name="main",
+        compiler_params=pltpu.CompilerParams(vmem_limit_bytes=28 << 20),
     )(misfit, damage, displacement, halo, x_a, x_b)
     parts = lax.all_to_all(line, AXES, 0, 0, tiled=True)
     return pl.pallas_call(
@@ -386,6 +389,7 @@
         out_specs=[VMEM] * 2,
         out_shape=[shape(3, CX, CY, CZ), shape(CX, CY, CZ)],
         name="combine",
+        compiler_params=pltpu.CompilerParams(vmem_limit_bytes=12 << 20),
     )(parts, misfit, p1, p2, t, damage)
 
 

time: 69.2 us -> 62.5 us (0.903)
  Pallas kernels: 18.2 us -> 10.7 us
  local copies, waits for them, and re-layouts: 1.42 us -> 2.9 us
    pallas_call x1, Pallas kernels: 11.8 us -> 9.6 us  [body(): pl.pallas_call(main_kernel, in_specs=[VMEM] * 6, out_specs=[VMEM] * 4, ou...]
    pallas_call x1, Pallas kernels: 2.19 us -> 0.08 us  [body(): pl.pallas_call(pack_x, in_specs=[VMEM] * 5, out_specs=[VMEM] * 3, out_sha...]
    pallas_call x1, Pallas kernels: 1.72 us -> 0.04 us  [body(): pl.pallas_call(pack_y, grid=(1,), in_specs=[pl.BlockSpec(edge, first), pl...]
    unnamed x8 -> x12, local copies, waits for them, and re-layouts: 1.42 us -> 2.9 us
    pallas_call x1, Pallas kernels: 2.44 us -> 1.02 us  [body(): pl.pallas_call(combine, in_specs=[VMEM] * 6, out_specs=[VMEM] * 2, out_sh...]
where the time goes in v2:
time: 62.5 us; the launch traced here: 62.2 us
  blocking collectives  32 us (51%)
  Pallas kernels  10.7 us (17%)
  waiting for transfers between devices  8.7 us (14%)
  starting transfers between devices  7.2 us (12%)
  local copies, waits for them, and re-layouts  2.9 us (5%)
  between operations  0.7 us (1%)
    all_to_all x1, blocking collectives, body(): parts = lax.all_to_all(line, AXES, 0, 0, tiled=True)  32 us
    pallas_call x1, Pallas kernels, body(): pl.pallas_call(main_kernel, in_specs=[VMEM] * 6, out_specs=[VMEM] * 4, ou...  9.6 us
    ppermute x4, waiting for transfers between devices, exchange(): return lax.ppermute(x, axis, pairs)  8.7 us
    ppermute x4, starting transfers between devices, exchange(): return lax.ppermute(x, axis, pairs)  7.2 us
    unnamed x12, local copies, waits for them, and re-layouts  2.9 us
  transfers between devices with their start and end apart: 4, of which 2 were waited for; matrix products, arithmetic and copies ran while one was open for 0% of the time, Pallas kernels for 0%

profile of v2, /device:TPU:1, one launch (start us, length us, event | category | flops | bytes accessed | tf_op | source)
XLA Modules:
  0.0 62.2 jit_solution(1485429978188610844)
XLA Ops:
  0.6 0.0 copy-start
  0.6 1.0 %copy-done = f32[3,8,32,128]{3,2,1,0:T(8,128)S(1)} copy-done((f32[3,8,32,128]{3,2,1,0:T(8,128)S(1)}, f32[3,8,32,128]{3,2,1,0:T(8,128)}, u32[]{:S(2)}) %copy-start) | copy-done | bytes 393240
  1.6 0.0 copy-start.2
  1.6 1.0 %copy-done.2 = f32[3,8,32,128]{3,2,1,0:T(8,128)S(1)} copy-done((f32[3,8,32,128]{3,2,1,0:T(8,128)S(1)}, f32[3,8,32,128]{3,2,1,0:T(8,128)}, u32[]{:S(2)}) %copy-start.2) | copy-done | bytes 393240
  2.6 0.0 copy-start.4
  2.6 0.9 %copy-done.4 = f32[8,32,128]{2,1,0:T(8,128)S(1)} copy-done((f32[8,32,128]{2,1,0:T(8,128)S(1)}, f32[8,32,128]{2,1,0:T(8,128)}, u32[]{:S(2)}) %copy-start.4) | copy-done | bytes 131096
  3.5 0.0 copy-start.1
  3.5 0.0 copy-start.3
  3.5 0.0 copy-start.5
  3.6 3.3 %collective-permute-start = (f32[2,8,8,128]{3,2,1,0:T(8,128)S(1)}, f32[2,8,8,128]{3,2,1,0:T(8,128)S(1)}, u32[]{:S(2)}, u32[]{:S(2)}) collective-permute-start(f32[2,8,8,128]{3,2,1,0:T(8,128)S(1)} %get-tuple-element.11), channel_id=1, source_target_pairs={{0,1},{1,0},{2,3},{3,2},{4,5},{5,4},{6,7},{7,6},{8,9},{9,8},{10,11... | collective-permute-start | bytes 196616 | tf_op jit(solution)/shard_map/ppermute | solution.py:21
  6.9 3.1 %collective-permute-start.1 = (f32[2,8,8,128]{3,2,1,0:T(8,128)S(1)}, f32[2,8,8,128]{3,2,1,0:T(8,128)S(1)}, u32[]{:S(2)}, u32[]{:S(2)}) collective-permute-start(f32[2,8,8,128]{3,2,1,0:T(8,128)S(1)} %get-tuple-element.12), channel_id=1, source_target_pairs={{1,2},{2,1},{5,6},{6,5},{9,10},{10,9},{13,14},{14,13},{17,18},{18,... | collective-permute-start | bytes 196616 | tf_op jit(solution)/shard_map/ppermute | solution.py:21
  10.0 0.0 collective-permute-done.y_a
  10.0 3.9 %collective-permute-done.1.y_b = f32[2,8,8,128]{3,2,1,0:T(8,128)S(1)} collective-permute-done((f32[2,8,8,128]{3,2,1,0:T(8,128)S(1)}, f32[2,8,8,128]{3,2,1,0:T(8,128)S(1)}, u32[]{:S(2)}, u32[]{:S(2)}) %collective-permute-start.1) | collective-permute-done | bytes 65568 | tf_op jit(solution)/shard_map/ppermute | solution.py:21
  13.9 0.0 copy-done.1
  14.0 0.0 copy-done.3
  14.0 0.0 copy-done.5
  14.0 0.1 pack_x.1
  14.0 0.1 collective-permute-start.2
  14.1 0.7 %collective-permute-start.3 = (f32[14,40,128]{2,1,0:T(8,128)S(1)}, f32[14,40,128]{2,1,0:T(8,128)S(1)}, u32[]{:S(2)}, u32[]{:S(2)}) collective-permute-start(f32[14,40,128]{2,1,0:T(8,128)S(1)} %get-tuple-element.15), channel_id=1, source_target_pairs={{4,8},{8,4},{12,16},{16,12},{20,24},{24,20},{28,32},{32,28},{36,40... | collective-permute-start | bytes 860168 | tf_op jit(solution)/shard_map/ppermute | solution.py:21
  14.8 4.8 %collective-permute-done.2.x_a = f32[14,40,128]{2,1,0:T(8,128)S(1)} collective-permute-done((f32[14,40,128]{2,1,0:T(8,128)S(1)}, f32[14,40,128]{2,1,0:T(8,128)S(1)}, u32[]{:S(2)}, u32[]{:S(2)}) %collective-permute-start.2) | collective-permute-done | bytes 286752 | tf_op jit(solution)/shard_map/ppermute | solution.py:21
  19.6 0.0 collective-permute-done.3.x_b
  19.6 9.6 %main.1 = (f32[3,8,32,128]{3,2,1,0:T(8,128)S(1)}, f32[3,8,32,128]{3,2,1,0:T(8,128)S(1)}, f32[3,8,32,128]{3,2,1,0:T(8,128)S(1)}, f32[256,128]{1,0:T(8,128)S(1)}) custom-call(f32[3,8,32,128]{3,2,1,0:T(8,128)S(1)} %copy-done.1, f32[8,32,128]{2,1,0:T(8,128)S(1)} %copy-done.5, f32[3,8,32,128]{3,2,1,0:T(8,128)S(1)} %copy-done.3, ...), custom_call_target="tpu_custom_call" | custom-call | tf_op jit(solution)/shard_map/main/pallas_call | solution.py:366
  29.2 32.0 %all_to_all.11 = f32[256,1,128]{2,1,0:T(1,128)S(1)} all-to-all(f32[256,1,128]{2,1,0:T(1,128)S(1)} %bitcast.5), channel_id=1, replica_groups=mesh['gx'=64,'gy'=4] {'gx','gy'}, dimensions={0} | all-to-all | bytes 262144 | tf_op jit(solution)/shard_map/all_to_all | solution.py:385
  61.2 1.0 %combine.1 = (f32[3,8,32,128]{3,2,1,0:T(8,128)}, f32[8,32,128]{2,1,0:T(8,128)}) custom-call(f32[256,128]{1,0:T(8,128)S(1)} %bitcast.4, f32[3,8,32,128]{3,2,1,0:T(8,128)S(1)} %copy-done.1, f32[3,8,32,128]{3,2,1,0:T(8,128)S(1)} %get-tuple-element.17.p1, f32[3,8,32,128]{3,2,1,0:T(8,128)S(1)} %get-tuple-element.18.p2, ...), custom_call_target="tpu_custom_call" | custom-call | tf_op jit(solution)/shard_map/combine/pallas_call | solution.py:386
  (1 shorter events, 0.0 us)
Async XLA Ops:
  0.6 1.0 %copy-start = (f32[3,8,32,128]{3,2,1,0:T(8,128)S(1)}, f32[3,8,32,128]{3,2,1,0:T(8,128)}, u32[]{:S(2)}) copy-start(f32[3,8,32,128]{3,2,1,0:T(8,128)} %b_ref.5) | copy-start | bytes 1179652
  1.6 1.0 %copy-start.2 = (f32[3,8,32,128]{3,2,1,0:T(8,128)S(1)}, f32[3,8,32,128]{3,2,1,0:T(8,128)}, u32[]{:S(2)}) copy-start(f32[3,8,32,128]{3,2,1,0:T(8,128)} %u_ref.3) | copy-start | bytes 1179652
  2.6 0.9 %copy-start.4 = (f32[8,32,128]{2,1,0:T(8,128)S(1)}, f32[8,32,128]{2,1,0:T(8,128)}, u32[]{:S(2)}) copy-start(f32[8,32,128]{2,1,0:T(8,128)} %h_ref.5) | copy-start | bytes 393220
  3.5 10.4 %copy-start.1 = (f32[3,8,32,128]{3,2,1,0:T(8,128)S(1)}, f32[3,8,32,128]{3,2,1,0:T(8,128)}, u32[]{:S(2)}) copy-start(f32[3,8,32,128]{3,2,1,0:T(8,128)} %b_ref.5) | copy-start | bytes 1179652
  3.5 10.4 %copy-start.3 = (f32[3,8,32,128]{3,2,1,0:T(8,128)S(1)}, f32[3,8,32,128]{3,2,1,0:T(8,128)}, u32[]{:S(2)}) copy-start(f32[3,8,32,128]{3,2,1,0:T(8,128)} %u_ref.3) | copy-start | bytes 1179652
  3.5 10.4 %copy-start.5 = (f32[8,32,128]{2,1,0:T(8,128)S(1)}, f32[8,32,128]{2,1,0:T(8,128)}, u32[]{:S(2)}) copy-start(f32[8,32,128]{2,1,0:T(8,128)} %h_ref.5) | copy-start | bytes 393220
  3.6 6.4 %collective-permute-start = (f32[2,8,8,128]{3,2,1,0:T(8,128)S(1)}, f32[2,8,8,128]{3,2,1,0:T(8,128)S(1)}, u32[]{:S(2)}, u32[]{:S(2)}) collective-permute-start(f32[2,8,8,128]{3,2,1,0:T(8,128)S(1)} %get-tuple-element.11), channel_id=1, source_target_pairs={{0,1},{1,0},{2,3},{3,2},{4,5},{5,4},{6,7},{7,6},{8,9},{9,8},{10,11... | collective-permute-start | bytes 196616 | tf_op jit(solution)/shard_map/ppermute | solution.py:21
  6.9 7.1 %collective-permute-start.1 = (f32[2,8,8,128]{3,2,1,0:T(8,128)S(1)}, f32[2,8,8,128]{3,2,1,0:T(8,128)S(1)}, u32[]{:S(2)}, u32[]{:S(2)}) collective-permute-start(f32[2,8,8,128]{3,2,1,0:T(8,128)S(1)} %get-tuple-element.12), channel_id=1, source_target_pairs={{1,2},{2,1},{5,6},{6,5},{9,10},{10,9},{13,14},{14,13},{17,18},{18,... | collective-permute-start | bytes 196616 | tf_op jit(solution)/shard_map/ppermute | solution.py:21
  14.0 5.6 %collective-permute-start.2 = (f32[14,40,128]{2,1,0:T(8,128)S(1)}, f32[14,40,128]{2,1,0:T(8,128)S(1)}, u32[]{:S(2)}, u32[]{:S(2)}) collective-permute-start(f32[14,40,128]{2,1,0:T(8,128)S(1)} %get-tuple-element.14), channel_id=1, source_target_pairs={{0,4},{4,0},{8,12},{12,8},{16,20},{20,16},{24,28},{28,24},{32,36},... | collective-permute-start | bytes 860168 | tf_op jit(solution)/shard_map/ppermute | solution.py:21
  14.1 5.5 %collective-permute-start.3 = (f32[14,40,128]{2,1,0:T(8,128)S(1)}, f32[14,40,128]{2,1,0:T(8,128)S(1)}, u32[]{:S(2)}, u32[]{:S(2)}) collective-permute-start(f32[14,40,128]{2,1,0:T(8,128)S(1)} %get-tuple-element.15), channel_id=1, source_target_pairs={{4,8},{8,4},{12,16},{16,12},{20,24},{24,20},{28,32},{32,28},{36,40... | collective-permute-start | bytes 860168 | tf_op jit(solution)/shard_map/ppermute | solution.py:21

commit v3 on v1

v3 whole, which is shorter than its diff:
```python
import jax
import jax.numpy as jnp
from jax import lax
from jax.experimental import pallas as pl
from jax.experimental.pallas import tpu as pltpu
from jax.sharding import PartitionSpec as P

CX, CY, CZ = 8, 32, 128
ROWS = 40
AXES = ("gx", "gy")
LAM = 3.0 * 0.3 / (1.3 * 0.4)
MU = 3.0 / 2.6
F32 = jnp.float32


def exchange(x, axis, first):
    n = lax.axis_size(axis)
    pairs = []
    for i in range(first, n - 1, 2):
        pairs += [(i, i + 1), (i + 1, i)]
    return lax.ppermute(x, axis, pairs)


def iota(shape, dim):
    return lax.broadcasted_iota(jnp.int32, shape, dim)


def degradation_of(damage):
    return (1.0 - damage) * (1.0 - damage) + 0.001


def pack_y(b, h, u, out_a, out_b, b_lo, b_hi, h_lo, h_hi, u_lo, done):
    copies = []
    for k, (source, target) in enumerate(
        (
            (b.at[:, :, pl.ds(0, 8)], b_lo),
            (b.at[:, :, pl.ds(CY - 8, 8)], b_hi),
            (h.at[:, pl.ds(0, 8)], h_lo),
            (h.at[:, pl.ds(CY - 8, 8)], h_hi),
            (u.at[:, :, pl.ds(0, 8)], u_lo),
        )
    ):
        copies.append(pltpu.make_async_copy(source, target, done.at[k]))
        copies[-1].start()
    for copy in copies:
        copy.wait()
    row = iota((CX, 8, CZ), 1)
    g_lo, g_hi = degradation_of(h_lo[...]), degradation_of(h_hi[...])
    up = lambda x, k: pltpu.roll(x, k % 8, 1)
    low_1 = jnp.where(row < 3, b_lo[0], jnp.where(row < 6, up(b_lo[1], 3), up(g_lo, 6)))
    low_2 = jnp.where(
        row < 3,
        b_lo[2],
        jnp.where(
            row == 3, up(u_lo[0], 3), jnp.where(row == 4, up(u_lo[1], 4), up(u_lo[2], 5))
        ),
    )
    high = jnp.where(
        row < 2,
        up(b_hi[0], 2),
        jnp.where(row < 4, up(b_hi[1], 4), jnp.where(row < 6, up(b_hi[2], 6), g_hi)),
    )
    odd = lax.rem(lax.axis_index("gy"), 2) == 1

    @pl.when(odd)
    def _():
        out_a[0], out_a[1] = low_1, low_2
        out_b[0], out_b[1] = high, high

    @pl.when(jnp.logical_not(odd))
    def _():
        out_a[0], out_a[1] = high, high
        out_b[0], out_b[1] = low_1, low_2


def stage(b, h, u, b_out, h_out, u_out):
    b_out[...] = b[...]
    h_out[...] = h[...]
    u_out[...] = u[...]


def pack_x(y_a, y_b, b_ref, h_ref, u_ref, out_a, out_b, halo):
    odd_y = lax.rem(lax.axis_index("gy"), 2) == 1
    row = iota((CX, 8, CZ), 1)
    up = lambda x, k: pltpu.roll(x, k % 8, 1)
    above_1 = jnp.where(odd_y, y_b[0], y_a[0])
    above_2 = jnp.where(odd_y, y_b[1], y_a[1])
    below = jnp.where(odd_y, y_a[0], y_b[0])

    def tile(head, count, tail):
        return jnp.where(row < count, head, jnp.where(row >= 6, tail, 0.0))

    halo[0] = tile(above_1, 3, up(below, 6))
    halo[1] = tile(up(above_1, -3), 3, up(below, 4))
    halo[2] = tile(above_2, 3, up(below, 2))
    halo[3] = tile(up(above_1, -6), 2, below)
    for c in range(3):
        halo[4 + c] = jnp.where(row < 1, up(above_2, -3 - c), 0.0)
    odd_x = lax.rem(lax.axis_index("gx"), 2) == 1

    def low(out):
        for c in range(3):
            for x in range(3):
                out[3 * c + x, :CY], out[3 * c + x, CY:] = b_ref[c, x], halo[c, x]
            out[11 + c, :CY], out[11 + c, CY:] = u_ref[c, 0], halo[4 + c, 0]
        for x in range(2):
            out[9 + x, :CY], out[9 + x, CY:] = degradation_of(h_ref[x]), halo[3, x]

    def high(out):
        for c in range(3):
            for x in range(2):
                out[3 * c + x, :CY], out[3 * c + x, CY:] = b_ref[c, 6 + x], halo[c, 6 + x]
            out[3 * c + 2] = jnp.zeros((ROWS, CZ), F32)
            out[11 + c] = jnp.zeros((ROWS, CZ), F32)
        for x in range(2):
            out[9 + x, :CY], out[9 + x, CY:] = degradation_of(h_ref[6 + x]), halo[3, 6 + x]

    @pl.when(odd_x)
    def _():
        low(out_a)
        high(out_b)

    @pl.when(jnp.logical_not(odd_x))
    def _():
        high(out_a)
        low(out_b)


def yz_modes(u):
    lane = iota((ROWS, CZ), 1)
    u_next = jnp.where(lane == CZ - 1, 0.0, pltpu.roll(u, CZ - 1, 1))
    out = [None] * 4
    for z, a in enumerate((u + u_next, u_next - u)):
        a_next = pltpu.roll(a, ROWS - 1, 0)
        out[z], out[2 + z] = a + a_next, a_next - a
    return out


def yz_gather(r):
    lane = iota((ROWS, CZ), 1)
    rows = []
    for z in range(2):
        s, d = r[z], r[2 + z]
        rows.append((s - d) + pltpu.roll(s + d, 1, 0))
    s, d = rows
    return (s - d) + jnp.where(lane == 0, 0.0, pltpu.roll(s + d, 1, 1))


SS, SD, DS, DD = 0, 1, 2, 3


def strains(here, there):
    s = [[here[4 * c + k] + there[4 * c + k] if k else None for k in range(4)] for c in range(3)]
    d = [[there[4 * c + k] - here[4 * c + k] for k in range(4)] for c in range(3)]
    u, v, w = range(3)
    return [
        d[u][SS], s[v][DS], s[w][SD],
        s[u][DS] + d[v][SS], s[u][SD] + d[w][SS], s[v][SD] + s[w][DS],
        s[u][DD], d[v][SD], d[w][DS],
        d[u][SD], s[v][DD], d[u][DS], s[w][DD], d[v][DS], d[w][SD],
        d[u][DD], d[v][DD], d[w][DD],
    ]


def stresses(e, g):
    scaled = (lambda k: g * k) if g is not None else (lambda k: k)
    l16, m8, m16, m48 = scaled(LAM / 16), scaled(MU / 8), scaled(MU / 16), scaled(MU / 48)
    l48, q = scaled(LAM / 48), scaled((LAM + 4 * MU) / 144)
    trace = l16 * (e[0] + e[1] + e[2])
    out = [trace + m8 * e[k] for k in range(3)]
    out += [m16 * e[k] for k in range(3, 6)]
    three = e[6] + e[7] + e[8]
    out += [m48 * (e[k] + three) for k in range(6, 9)]
    for k in (9, 11, 13):
        both = l48 * (e[k] + e[k + 1])
        out += [both + m16 * e[k], both + m16 * e[k + 1]]
    return out + [q * e[k] for k in range(15, 18)]


def x_forces(f):
    s = [[None, f[4], f[3], f[6]], [None, f[5], f[1], f[10]], [None, f[2], f[5], f[12]]]
    d = [[f[0], f[9], f[11], f[15]], [f[3], f[7], f[13], f[16]], [f[4], f[14], f[8], f[17]]]
    return [x for c in s for x in c], [x for c in d for x in c]


def inner(a, b):
    total = a[0] * b[0]
    for x, y in zip(a[1:], b[1:]):
        total = total + x * y
    return total


def load(place, rows):
    ref, slot = place
    return [ref[k, slot, rows, :] for k in range(12)]


def to_modes(node, place):
    ref, slot = place
    for c in range(3):
        for k, a in enumerate(yz_modes(node(c))):
            ref[4 * c + k, slot] = a


def each_chunk(step, halo_too):
    @pl.loop(0, CY // 8)
    def _(j):
        step(pl.ds(pl.multiple_of(8 * j, 8), 8), True)

    if halo_too:
        step(pl.ds(CY, 8), False)


def sweep(elements, modes, g, add, put, visit=None):
    def step(rows, own):
        here = load(modes[elements[0]], rows)
        before = None

        def store(n, lower):
            if n not in put:
                return
            total = before
            if lower is not None:
                total = lower if total is None else [p + q for p, q in zip(total, lower)]
            if n in add:
                total = [p + q for p, q in zip(total, load(add[n], rows))]
            ref, slot = put[n]
            for k in range(12):
                ref[k, slot, rows, :] = total[k]

        for e in elements:
            there = load(modes[e + 1], rows)
            strain = strains(here, there)
            if own and visit is not None:
                visit(e, strain, rows)
            s, d = x_forces(stresses(strain, g(e, rows)))
            if e in put:
                store(e, [p - q if p is not None else -q for p, q in zip(s, d)])
            before = [p + q if p is not None else q for p, q in zip(s, d)]
            here = there
        store(elements[-1] + 1, None)

    each_chunk(step, True)


def finish(gathered, target, edge, factor=None):
    ref, slot = gathered
    out, at = target
    for c in range(3):
        v = yz_gather([ref[4 * c + k, slot] for k in range(4)])
        if factor is not None:
            v = v * factor
        out[c, at, :CY] = v[:CY]
        out[c, at, CY:] = v[CY:] * edge


def collapse(x):
    return x[0:8] + x[8:16] + x[16:24] + x[24:32]


def row_edge():
    row = iota((8, CZ), 0)
    last = lax.axis_index("gy") == lax.axis_size("gy") - 1
    return jnp.where(row < 3, jnp.where(last, 0.0, 1.0).astype(F32), 1.0)


KEPT = ("b", 0), ("b", 7), ("p1", 1), ("p1", 6), ("p2", 2), ("p2", 5), ("u", 7)
OPEN = ("p1", 0), ("p1", 7), ("p2", 1), ("p2", 6)
KEPT_WEIGHTS = (0, 1, 5, 6)


def inner_kernel(
    b_ref, h_ref, u_ref, halo, p1, p2, t, kept, opened, weights_out, sums,
    modes, gathered, weights, g_ref,
):
    edge = row_edge()
    g_ref[:, :CY] = degradation_of(h_ref[...])
    g_ref[:, CY:] = halo[3]
    g = lambda e, rows: g_ref[e, rows, :]
    keep = {name: (kept, k) for k, name in enumerate(KEPT)}
    open_at = {name: (opened, k) for k, name in enumerate(OPEN)}
    at = lambda name, n: keep.get((name, n), (modes, n))

    def own(ref, first, n):
        return lambda c: jnp.concatenate([ref[c, n], halo[first + c, n]], 0)

    u_modes = {n: at("u", n) for n in range(CX)}
    for n in range(CX):
        to_modes(own(u_ref, 4, n), u_modes[n])

    def stiffen(rows, _):
        here = load(u_modes[0], rows)
        for e in range(7):
            there = load(u_modes[e + 1], rows)
            for k, f in enumerate(stresses(strains(here, there), None)):
                if e in KEPT_WEIGHTS:
                    weights_out[k, KEPT_WEIGHTS.index(e), rows, :] = f
                else:
                    weights[k, e, rows, :] = f
            here = there

    each_chunk(stiffen, False)

    def weight(e, rows):
        if e in KEPT_WEIGHTS:
            return [weights_out[k, KEPT_WEIGHTS.index(e), rows, :] for k in range(18)]
        return [weights[k, e, rows, :] for k in range(18)]

    def visit(power):
        def f(e, strain, rows):
            t[power, e, rows, :] = inner(strain, weight(e, rows))

        return f

    b_modes = {n: at("b", n) for n in range(CX)}
    for n in range(CX):
        to_modes(own(b_ref, 0, n), b_modes[n])
    put = {n: (gathered, n) for n in range(1, 7)}
    put.update({0: open_at["p1", 0], 7: open_at["p1", 7]})
    sweep(range(0, 7), b_modes, g, {}, put, visit(0))
    for n in range(1, 7):
        finish(put[n], (p1, n - 1), edge)

    p1_modes = {n: at("p1", n) for n in range(1, 7)}
    for n in range(1, 7):
        to_modes(lambda c, n=n: p1[c, n - 1], p1_modes[n])
    put = {n: (gathered, n) for n in range(2, 6)}
    put.update({1: open_at["p2", 1], 6: open_at["p2", 6]})
    sweep(range(1, 6), p1_modes, g, {}, put, visit(1))
    for n in range(2, 6):
        finish(put[n], (p2, n - 2), edge)

    p2_modes = {n: at("p2", n) for n in range(2, 6)}
    for n in range(2, 6):
        to_modes(lambda c, n=n: p2[c, n - 2], p2_modes[n])
    sums[...] = jnp.zeros_like(sums)

    def energy(rows, _):
        here = load(p2_modes[2], rows)
        total = jnp.zeros((8, CZ), F32)
        for e in range(2, 5):
            there = load(p2_modes[e + 1], rows)
            strain = strains(here, there)
            t[2, e, rows, :] = inner(strain, weight(e, rows))
            total = total + inner(strain, stresses(strain, g(e, rows)))
            here = there
        sums[5] += total

    each_chunk(energy, False)
    total = [jnp.zeros((8, CZ), F32)] * 5
    for n in range(CX):
        for c in range(3):
            v = [b_ref[c, n]]
            if 1 <= n < 7:
                v.append(p1[c, n - 1, :CY])
            if 2 <= n < 6:
                v.append(p2[c, n - 2, :CY])
            for k, (i, j) in enumerate(((0, 0), (0, 1), (1, 1), (1, 2), (2, 2))):
                if j < len(v):
                    total[k] = total[k] + collapse(v[i] * v[j])
    for k in range(5):
        sums[k] = total[k]


def outer_kernel(
    b_ref, h_ref, halo, x_a, x_b, p1, p2, kept, opened, weights_in, sums_in,
    q1, q2, t, row_out, above, below, g_ref, modes, gathered, weights, sums,
):
    edge = row_edge()
    odd_x = lax.rem(lax.axis_index("gx"), 2) == 1
    last_x = lax.axis_index("gx") == lax.axis_size("gx") - 1
    past_x = jnp.where(last_x, 0.0, 1.0).astype(F32)

    @pl.when(odd_x)
    def _():
        above[...] = x_b[...]
        below[...] = x_a[...]

    @pl.when(jnp.logical_not(odd_x))
    def _():
        above[...] = x_a[...]
        below[...] = x_b[...]

    for k, e in enumerate((0, 1, 5, 6, 7)):
        g_ref[k, :CY] = degradation_of(h_ref[e])
        g_ref[k, CY:] = halo[3, e]

    def g(e, rows):
        if e < 0:
            return below[11 + e, rows, :]
        if e >= CX:
            return above[1 + e, rows, :]
        return g_ref[(0, 1, 5, 6, 7).index(e), rows, :]

    keep = {name: (kept, k) for k, name in enumerate(KEPT)}
    open_at = {name: (opened, k) for k, name in enumerate(OPEN)}
    new = [0]

    def fresh(nodes):
        out = {n: (modes, new[0] + k) for k, n in enumerate(nodes)}
        new[0] += len(nodes)
        return out

    u_modes = fresh([8])
    to_modes(lambda c: above[11 + c], u_modes[8])
    u_modes[7] = keep["u", 7]

    def stiffen(rows, _):
        f = stresses(strains(load(u_modes[7], rows), load(u_modes[8], rows)), None)
        for k in range(18):
            weights[k, rows, :] = f[k]

    each_chunk(stiffen, False)

    def weight(e, rows):
        if e == 7:
            return [weights[k, rows, :] for k in range(18)]
        return [weights_in[k, KEPT_WEIGHTS.index(e), rows, :] for k in range(18)]

    def visit(power):
        def f(e, strain, rows):
            if (power, e) in OUTER_T:
                t[OUTER_T.index((power, e)), rows, :] = inner(strain, weight(e, rows))

        return f

    b_modes = fresh([-2, -1, 8, 9, 10])
    for n in (-2, -1):
        to_modes(lambda c, n=n: below[3 * c + n + 2], b_modes[n])
    for n in (8, 9, 10):
        to_modes(lambda c, n=n: above[3 * c + n - 8], b_modes[n])
    b_modes.update({0: keep["b", 0], 7: keep["b", 7]})
    nodes = (-1, 0, 7, 8, 9)
    put = {n: (gathered, k) for k, n in enumerate(nodes)}
    sweep((-2, -1), b_modes, g, {0: open_at["p1", 0]}, put, visit(0))
    sweep((7, 8, 9), b_modes, g, {7: open_at["p1", 7]}, put, visit(0))
    for k, n in enumerate(nodes):
        finish(put[n], (q1, k), edge, past_x if n >= CX else None)

    p1_modes = fresh(nodes)
    for k, n in enumerate(nodes):
        to_modes(lambda c, k=k: q1[c, k], p1_modes[n])
    p1_modes.update({1: keep["p1", 1], 6: keep["p1", 6]})
    nodes = (0, 1, 6, 7, 8)
    put = {n: (gathered, k) for k, n in enumerate(nodes)}
    sweep((-1, 0), p1_modes, g, {1: open_at["p2", 1]}, put, visit(1))
    sweep((6, 7, 8), p1_modes, g, {6: open_at["p2", 6]}, put, visit(1))
    for k, n in enumerate(nodes):
        finish(put[n], (q2, k), edge, past_x if n >= CX else None)

    p2_modes = fresh(nodes)
    for k, n in enumerate(nodes):
        to_modes(lambda c, k=k: q2[c, k], p2_modes[n])
    p2_modes.update({2: keep["p2", 2], 5: keep["p2", 5]})
    sums[...] = sums_in[...]

    def energy(rows, _):
        total = jnp.zeros((8, CZ), F32)
        for elements in ((0, 1), (5, 6, 7)):
            here = load(p2_modes[elements[0]], rows)
            for e in elements:
                there = load(p2_modes[e + 1], rows)
                strain = strains(here, there)
                visit(2)(e, strain, rows)
                total = total + inner(strain, stresses(strain, g(e, rows)))
                here = there
        sums[5] += total

    each_chunk(energy, False)
    total = [sums[k] for k in range(5)]
    for n in (0, 1, 6, 7):
        for c in range(3):
            v1 = q1[c, (-1, 0, 7).index(n), :CY] if n in (0, 7) else p1[c, n - 1, :CY]
            v = (b_ref[c, n], v1, q2[c, (0, 1, 6, 7).index(n), :CY])
            for k, (i, j) in enumerate(((0, 0), (0, 1), (1, 1), (1, 2), (2, 2))):
                if k >= (1 if n in (0, 7) else 3):
                    total[k] = total[k] + collapse(v[i] * v[j])
    total.append(sums[5])
    lane = iota((1, CZ), 1)
    line = jnp.zeros((1, CZ), F32)
    for k in range(6):
        value = jnp.sum(jnp.sum(total[k], 0, keepdims=True), 1, keepdims=True)
        line = jnp.where(lane == k, value, line)
    row_out[...] = jnp.broadcast_to(line, row_out.shape)


OUTER_T = [(0, 7), (1, 0), (1, 6), (1, 7), (2, 0), (2, 1), (2, 5), (2, 6), (2, 7)]


def combine(parts, b_ref, h_ref, p1, p2, q1, q2, t_in, t_out, adjoint, sensitivity):
    line = jnp.sum(parts[...], 0, keepdims=True)
    lane = iota((1, CZ), 1)
    m = [jnp.sum(jnp.where(lane == k, line, 0.0), 1, keepdims=True) for k in range(6)]
    l10, l20 = m[2] / m[1], m[3] / m[1]
    d1, h21 = m[3] - l10 * m[2], m[4] - l20 * m[2]
    l21 = h21 / d1
    d2 = m[5] - l20 * m[3] - l21 * h21
    y1 = m[1] - l10 * m[0]
    y2 = m[2] - l20 * m[0] - l21 * y1
    c2 = y2 / d2
    c1 = y1 / d1 - l21 * c2
    c0 = m[0] / m[1] - l10 * c1 - l20 * c2
    weight = [jnp.broadcast_to(c, (CY, CZ)) for c in (c0, c1, c2)]
    for x in range(CX):
        for c in range(3):
            v1 = q1[c, (-1, 0, 7).index(x), :CY] if x in (0, 7) else p1[c, x - 1, :CY]
            v2 = p2[c, x - 2, :CY] if 2 <= x < 6 else q2[c, (0, 1, 6, 7).index(x), :CY]
            adjoint[c, x] = weight[0] * b_ref[c, x] + weight[1] * v1 + weight[2] * v2
        product = None
        for k in range(3):
            part = t_out[OUTER_T.index((k, x))] if (k, x) in OUTER_T else t_in[k, x]
            product = weight[k] * part if product is None else product + weight[k] * part
        sensitivity[x] = 2.0 * (1.0 - h_ref[x]) * product


VMEM = pl.BlockSpec(memory_space=pltpu.VMEM)


def shape(*dims):
    return jax.ShapeDtypeStruct(dims, F32)


def call(kernel, name, megabytes, inputs, outputs, scratch=(), in_specs=None):
    return pl.pallas_call(
        kernel,
        in_specs=in_specs or [VMEM] * len(inputs),
        out_specs=[VMEM] * len(outputs),
        out_shape=[shape(*dims) for dims in outputs],
        scratch_shapes=[s if not isinstance(s, tuple) else pltpu.VMEM(s, F32) for s in scratch],
        compiler_params=pltpu.CompilerParams(vmem_limit_bytes=megabytes and megabytes << 20),
        name=name,
    )(*inputs)


def body(misfit, damage, displacement):
    tile = (CX, 8, CZ)
    y_a, y_b = call(
        pack_y, "pack_y", None,
        (misfit, damage, displacement),
        [(2,) + tile] * 2,
        [(3,) + tile, (3,) + tile, tile, tile, (3,) + tile, pltpu.SemaphoreType.DMA((5,))],
        [pl.BlockSpec(memory_space=pltpu.HBM)] * 3,
    )
    y_b = exchange(y_b, "gy", 1)
    y_a = exchange(y_a, "gy", 0)
    misfit, damage, displacement = call(
        stage, "stage", 4,
        (misfit, damage, displacement),
        [(3, CX, CY, CZ), (CX, CY, CZ), (3, CX, CY, CZ)],
    )
    x_a, x_b, halo = call(
        pack_x, "pack_x", 6,
        (y_a, y_b, misfit, damage, displacement),
        [(14, ROWS, CZ)] * 2 + [(7,) + tile],
    )
    x_b = exchange(x_b, "gx", 1)
    x_a = exchange(x_a, "gx", 0)
    devices = lax.axis_size("gx") * lax.axis_size("gy")
    layer = (ROWS, CZ)
    p1, p2, t_in, kept, opened, weights, sums = call(
        inner_kernel, "inner", 20,
        (misfit, damage, displacement, halo),
        [
            (3, 6) + layer, (3, 4) + layer, (3, CX, CY, CZ), (12, len(KEPT)) + layer,
            (12, len(OPEN)) + layer, (18, len(KEPT_WEIGHTS), CY, CZ), (6, 8, CZ),
        ],
        [(12, CX) + layer, (12, CX) + layer, (18, CX, CY, CZ), (CX,) + layer],
    )
    q1, q2, t_out, line = call(
        outer_kernel, "outer", 20,
        (misfit, damage, halo, x_a, x_b, p1, p2, kept, opened, weights, sums),
        [(3, 5) + layer, (3, 5) + layer, (len(OUTER_T), CY, CZ), (devices, CZ)],
        [
            (14,) + layer, (14,) + layer, (5,) + layer, (12, 16) + layer, (12, 5) + layer,
            (18, CY, CZ), (6, 8, CZ),
        ],
    )
    parts = lax.all_to_all(line, AXES, 0, 0, tiled=True)
    return call(
        combine, "combine", 8,
        (parts, misfit, damage, p1, p2, q1, q2, t_in, t_out),
        [(3, CX, CY, CZ), (CX, CY, CZ)],
    )


def solution(mesh):
    field, scalar = P(None, "gx", "gy", None), P("gx", "gy", None)
    return jax.shard_map(
        body, mesh=mesh, in_specs=(field, scalar, field), out_specs=(field, scalar), check_vma=False
    )
```

time: 69.2 us -> 54.4 us (0.79)
  Pallas kernels: 18.2 us -> 8.8 us
  waiting for transfers between devices: 9.29 us -> 2.82 us
  local copies, waits for them, and re-layouts: 1.42 us -> 2.89 us
    pallas_call x4 -> x6, Pallas kernels: 18.2 us -> 8.8 us  [call(): pl.pallas_call(kernel, in_specs=in_specs or [VMEM] * len(inputs), out_spe...]
    ppermute x4, waiting for transfers between devices: 9.29 us -> 2.82 us  [exchange(): return lax.ppermute(x, axis, pairs)]
    unnamed x8 -> x6, local copies, waits for them, and re-layouts: 1.42 us -> 2.89 us
  transfers between devices with their start and end apart: 4 -> 4, of which waited for: 2 -> 2; matrix products, arithmetic and copies ran while one was open for 0% -> 0% of each run, Pallas kernels for 0% -> 6%
where the time goes in v3:
time: 54.4 us; the launch traced here: 54.1 us
  blocking collectives  31.9 us (59%)
  Pallas kernels  8.8 us (16%)
  starting transfers between devices  7.07 us (13%)
  local copies, waits for them, and re-layouts  2.89 us (5%)
  waiting for transfers between devices  2.82 us (5%)
  between operations  0.7 us (1%)
    all_to_all x1, blocking collectives, body(): parts = lax.all_to_all(line, AXES, 0, 0, tiled=True)  31.9 us
    pallas_call x6, Pallas kernels, call(): pl.pallas_call(kernel, in_specs=in_specs or [VMEM] * len(inputs), out_spe...  8.8 us
    ppermute x4, starting transfers between devices, exchange(): return lax.ppermute(x, axis, pairs)  7.07 us
    unnamed x6, local copies, waits for them, and re-layouts  2.89 us
    ppermute x4, waiting for transfers between devices, exchange(): return lax.ppermute(x, axis, pairs)  2.82 us
  transfers between devices with their start and end apart: 4, of which 2 were waited for; matrix products, arithmetic and copies ran while one was open for 0% of the time, Pallas kernels for 6%

profile of v3, /device:TPU:1, one launch (start us, length us, event | category | flops | bytes accessed | tf_op | source)
XLA Modules:
  0.0 54.1 jit_solution(14989746316517944479)
XLA Ops:
  0.6 1.8 %pack_y.1 = (f32[2,8,8,128]{3,2,1,0:T(8,128)}, f32[2,8,8,128]{3,2,1,0:T(8,128)}) custom-call(f32[3,8,32,128]{3,2,1,0:T(8,128)} %b.3, f32[8,32,128]{2,1,0:T(8,128)} %h.3, f32[3,8,32,128]{3,2,1,0:T(8,128)} %u.3), custom_call_target="tpu_custom_call" | custom-call | tf_op jit(solution)/shard_map/pack_y/pallas_call | solution.py:524
  2.4 3.3 %collective-permute-start = (f32[2,8,8,128]{3,2,1,0:T(8,128)}, f32[2,8,8,128]{3,2,1,0:T(8,128)S(1)}, u32[]{:S(2)}, u32[]{:S(2)}) collective-permute-start(f32[2,8,8,128]{3,2,1,0:T(8,128)} %get-tuple-element.23), channel_id=1, source_target_pairs={{0,1},{1,0},{2,3},{3,2},{4,5},{5,4},{6,7},{7,6},{8,9},{9,8},{10,11... | collective-permute-start | bytes 196616 | tf_op jit(solution)/shard_map/ppermute | solution.py:21
  5.7 3.0 %collective-permute-start.1 = (f32[2,8,8,128]{3,2,1,0:T(8,128)}, f32[2,8,8,128]{3,2,1,0:T(8,128)S(1)}, u32[]{:S(2)}, u32[]{:S(2)}) collective-permute-start(f32[2,8,8,128]{3,2,1,0:T(8,128)} %get-tuple-element.24), channel_id=1, source_target_pairs={{1,2},{2,1},{5,6},{6,5},{9,10},{10,9},{13,14},{14,13},{17,18},{18,... | collective-permute-start | bytes 196616 | tf_op jit(solution)/shard_map/ppermute | solution.py:21
  8.7 0.0 copy-start
  8.7 1.0 %copy-done = f32[3,8,32,128]{3,2,1,0:T(8,128)S(1)} copy-done((f32[3,8,32,128]{3,2,1,0:T(8,128)S(1)}, f32[3,8,32,128]{3,2,1,0:T(8,128)}, u32[]{:S(2)}) %copy-start) | copy-done | bytes 393240
  9.7 0.0 copy-start.1
  9.7 1.0 %copy-done.1 = f32[3,8,32,128]{3,2,1,0:T(8,128)S(1)} copy-done((f32[3,8,32,128]{3,2,1,0:T(8,128)S(1)}, f32[3,8,32,128]{3,2,1,0:T(8,128)}, u32[]{:S(2)}) %copy-start.1) | copy-done | bytes 393240
  10.7 0.0 copy-start.2
  10.7 0.9 %copy-done.2 = f32[8,32,128]{2,1,0:T(8,128)S(1)} copy-done((f32[8,32,128]{2,1,0:T(8,128)S(1)}, f32[8,32,128]{2,1,0:T(8,128)}, u32[]{:S(2)}) %copy-start.2) | copy-done | bytes 131096
  11.6 0.1 stage.1
  11.7 0.0 collective-permute-done.y_a
  11.7 1.3 %collective-permute-done.1.y_b = f32[2,8,8,128]{3,2,1,0:T(8,128)S(1)} collective-permute-done((f32[2,8,8,128]{3,2,1,0:T(8,128)}, f32[2,8,8,128]{3,2,1,0:T(8,128)S(1)}, u32[]{:S(2)}, u32[]{:S(2)}) %collective-permute-start.1) | collective-permute-done | bytes 65568 | tf_op jit(solution)/shard_map/ppermute | solution.py:21
  13.0 0.1 pack_x.1
  13.0 0.1 collective-permute-start.2
  13.1 0.7 %collective-permute-start.3 = (f32[14,40,128]{2,1,0:T(8,128)S(1)}, f32[14,40,128]{2,1,0:T(8,128)S(1)}, u32[]{:S(2)}, u32[]{:S(2)}) collective-permute-start(f32[14,40,128]{2,1,0:T(8,128)S(1)} %get-tuple-element.28), channel_id=1, source_target_pairs={{4,8},{8,4},{12,16},{16,12},{20,24},{24,20},{28,32},{32,28},{36,40... | collective-permute-start | bytes 860168 | tf_op jit(solution)/shard_map/ppermute | solution.py:21
  13.8 3.3 %inner.1 = (f32[3,6,40,128]{3,2,1,0:T(8,128)S(1)}, f32[3,4,40,128]{3,2,1,0:T(8,128)S(1)}, f32[3,8,32,128]{3,2,1,0:T(8,128)S(1)}, f32[12,7,40,128]{3,2,1,0:T(8,12...) custom-call(f32[3,8,32,128]{3,2,1,0:T(8,128)S(1)} %get-tuple-element.21.b_ref, ...), custom_call_target="tpu_custom_call" | custom-call | tf_op jit(solution)/shard_map/inner/pallas_call | solution.py:524
  17.1 1.5 %collective-permute-done.2.x_a = f32[14,40,128]{2,1,0:T(8,128)S(1)} collective-permute-done((f32[14,40,128]{2,1,0:T(8,128)S(1)}, f32[14,40,128]{2,1,0:T(8,128)S(1)}, u32[]{:S(2)}, u32[]{:S(2)}) %collective-permute-start.2) | collective-permute-done | bytes 286752 | tf_op jit(solution)/shard_map/ppermute | solution.py:21
  18.6 0.0 collective-permute-done.3.x_b
  18.6 2.6 %outer.1 = (f32[3,5,40,128]{3,2,1,0:T(8,128)S(1)}, f32[3,5,40,128]{3,2,1,0:T(8,128)S(1)}, f32[9,32,128]{2,1,0:T(8,128)S(1)}, f32[256,128]{1,0:T(8,128)S(1)}) custom-call(f32[3,8,32,128]{3,2,1,0:T(8,128)S(1)} %get-tuple-element.21.b_ref, f32[8,32,128]{2,1,0:T(8,128)S(1)} %get-tuple-element.22.h_ref, f32[7,8,8,128]{3,2,1,0:T(8,128)S(1)} %get-tuple-element.26.halo, ...), custom_call_target="tpu_custom_call" | custom-call | tf_op jit(solution)/shard_map/outer/pallas_call | solution.py:524
  21.2 31.9 %all_to_all.11 = f32[256,1,128]{2,1,0:T(1,128)S(1)} all-to-all(f32[256,1,128]{2,1,0:T(1,128)S(1)} %bitcast.5), channel_id=1, replica_groups=mesh['gx'=64,'gy'=4] {'gx','gy'}, dimensions={0} | all-to-all | bytes 262144 | tf_op jit(solution)/shard_map/all_to_all | solution.py:578
  53.1 1.0 %combine.1 = (f32[3,8,32,128]{3,2,1,0:T(8,128)}, f32[8,32,128]{2,1,0:T(8,128)}) custom-call(f32[256,128]{1,0:T(8,128)S(1)} %bitcast.4, f32[3,8,32,128]{3,2,1,0:T(8,128)S(1)} %get-tuple-element.21.b_ref, f32[8,32,128]{2,1,0:T(8,128)S(1)} %get-tuple-element.22.h_ref, f32[3,6,40,128]{3,2,1,0:T(8,128)S(1)} %get-tuple-element.29.p1, ...), custom_call_target="tpu_custom_call" | custom-call | tf_op jit(solution)/shard_map/combine/pallas_call | solution.py:524
Async XLA Ops:
  2.4 9.3 %collective-permute-start = (f32[2,8,8,128]{3,2,1,0:T(8,128)}, f32[2,8,8,128]{3,2,1,0:T(8,128)S(1)}, u32[]{:S(2)}, u32[]{:S(2)}) collective-permute-start(f32[2,8,8,128]{3,2,1,0:T(8,128)} %get-tuple-element.23), channel_id=1, source_target_pairs={{0,1},{1,0},{2,3},{3,2},{4,5},{5,4},{6,7},{7,6},{8,9},{9,8},{10,11... | collective-permute-start | bytes 196616 | tf_op jit(solution)/shard_map/ppermute | solution.py:21
  5.7 7.3 %collective-permute-start.1 = (f32[2,8,8,128]{3,2,1,0:T(8,128)}, f32[2,8,8,128]{3,2,1,0:T(8,128)S(1)}, u32[]{:S(2)}, u32[]{:S(2)}) collective-permute-start(f32[2,8,8,128]{3,2,1,0:T(8,128)} %get-tuple-element.24), channel_id=1, source_target_pairs={{1,2},{2,1},{5,6},{6,5},{9,10},{10,9},{13,14},{14,13},{17,18},{18,... | collective-permute-start | bytes 196616 | tf_op jit(solution)/shard_map/ppermute | solution.py:21
  8.7 1.0 %copy-start = (f32[3,8,32,128]{3,2,1,0:T(8,128)S(1)}, f32[3,8,32,128]{3,2,1,0:T(8,128)}, u32[]{:S(2)}) copy-start(f32[3,8,32,128]{3,2,1,0:T(8,128)} %b.3) | copy-start | bytes 1179652
  9.7 1.0 %copy-start.1 = (f32[3,8,32,128]{3,2,1,0:T(8,128)S(1)}, f32[3,8,32,128]{3,2,1,0:T(8,128)}, u32[]{:S(2)}) copy-start(f32[3,8,32,128]{3,2,1,0:T(8,128)} %u.3) | copy-start | bytes 1179652
  10.7 0.9 %copy-start.2 = (f32[8,32,128]{2,1,0:T(8,128)S(1)}, f32[8,32,128]{2,1,0:T(8,128)}, u32[]{:S(2)}) copy-start(f32[8,32,128]{2,1,0:T(8,128)} %h.3) | copy-start | bytes 393220
  13.0 5.6 %collective-permute-start.2 = (f32[14,40,128]{2,1,0:T(8,128)S(1)}, f32[14,40,128]{2,1,0:T(8,128)S(1)}, u32[]{:S(2)}, u32[]{:S(2)}) collective-permute-start(f32[14,40,128]{2,1,0:T(8,128)S(1)} %get-tuple-element.27), channel_id=1, source_target_pairs={{0,4},{4,0},{8,12},{12,8},{16,20},{20,16},{24,28},{28,24},{32,36},... | collective-permute-start | bytes 860168 | tf_op jit(solution)/shard_map/ppermute | solution.py:21
  13.1 5.5 %collective-permute-start.3 = (f32[14,40,128]{2,1,0:T(8,128)S(1)}, f32[14,40,128]{2,1,0:T(8,128)S(1)}, u32[]{:S(2)}, u32[]{:S(2)}) collective-permute-start(f32[14,40,128]{2,1,0:T(8,128)S(1)} %get-tuple-element.28), channel_id=1, source_target_pairs={{4,8},{8,4},{12,16},{16,12},{20,24},{24,20},{28,32},{32,28},{36,40... | collective-permute-start | bytes 860168 | tf_op jit(solution)/shard_map/ppermute | solution.py:21

commit v4 on v3

--- a/solution.py
+++ b/solution.py
@@ -4,6 +4,7 @@
 from jax.experimental import pallas as pl
 from jax.experimental.pallas import tpu as pltpu
 from jax.sharding import PartitionSpec as P
+
 
 CX, CY, CZ = 8, 32, 128
 ROWS = 40
@@ -79,7 +80,7 @@
     u_out[...] = u[...]
 
 
-def pack_x(y_a, y_b, b_ref, h_ref, u_ref, out_a, out_b, halo):
+def pack_x(y_a, y_b, b_ref, h_ref, out_a, out_b, halo):
     odd_y = lax.rem(lax.axis_index("gy"), 2) == 1
     row = iota((CX, 8, CZ), 1)
     up = lambda x, k: pltpu.roll(x, k % 8, 1)
@@ -102,7 +103,6 @@
         for c in range(3):
             for x in range(3):
                 out[3 * c + x, :CY], out[3 * c + x, CY:] = b_ref[c, x], halo[c, x]
-            out[11 + c, :CY], out[11 + c, CY:] = u_ref[c, 0], halo[4 + c, 0]
         for x in range(2):
             out[9 + x, :CY], out[9 + x, CY:] = degradation_of(h_ref[x]), halo[3, x]
 
@@ -111,7 +111,6 @@
             for x in range(2):
                 out[3 * c + x, :CY], out[3 * c + x, CY:] = b_ref[c, 6 + x], halo[c, 6 + x]
             out[3 * c + 2] = jnp.zeros((ROWS, CZ), F32)
-            out[11 + c] = jnp.zeros((ROWS, CZ), F32)
         for x in range(2):
             out[9 + x, :CY], out[9 + x, CY:] = degradation_of(h_ref[6 + x]), halo[3, 6 + x]
 
@@ -270,10 +269,12 @@
 
 
 def inner_kernel(
-    b_ref, h_ref, u_ref, halo, p1, p2, t, kept, opened, weights_out, sums,
+    b_ref, h_ref, u_ref, halo, p1, p2, t, kept, opened, weights_out, sums, u_first,
     modes, gathered, weights, g_ref,
 ):
     edge = row_edge()
+    u_first[:, :CY] = u_ref[:, 0]
+    u_first[:, CY:] = halo[4:7, 0]
     g_ref[:, :CY] = degradation_of(h_ref[...])
     g_ref[:, CY:] = halo[3]
     g = lambda e, rows: g_ref[e, rows, :]
@@ -364,7 +365,7 @@
 
 def outer_kernel(
     b_ref, h_ref, halo, x_a, x_b, p1, p2, kept, opened, weights_in, sums_in,
-    q1, q2, t, row_out, above, below, g_ref, modes, gathered, weights, sums,
+    q1, q2, t, row_out, strain_7, above, below, g_ref, modes, gathered, sums,
 ):
     edge = row_edge()
     odd_x = lax.rem(lax.axis_index("gx"), 2) == 1
@@ -401,25 +402,15 @@
         new[0] += len(nodes)
         return out
 
-    u_modes = fresh([8])
-    to_modes(lambda c: above[11 + c], u_modes[8])
-    u_modes[7] = keep["u", 7]
-
-    def stiffen(rows, _):
-        f = stresses(strains(load(u_modes[7], rows), load(u_modes[8], rows)), None)
-        for k in range(18):
-            weights[k, rows, :] = f[k]
-
-    each_chunk(stiffen, False)
-
     def weight(e, rows):
-        if e == 7:
-            return [weights[k, rows, :] for k in range(18)]
         return [weights_in[k, KEPT_WEIGHTS.index(e), rows, :] for k in range(18)]
 
     def visit(power):
         def f(e, strain, rows):
-            if (power, e) in OUTER_T:
+            if e == 7:
+                for k in range(18):
+                    strain_7[power, k, rows, :] = strain[k]
+            elif (power, e) in OUTER_T:
                 t[OUTER_T.index((power, e)), rows, :] = inner(strain, weight(e, rows))
 
         return f
@@ -484,10 +475,15 @@
     row_out[...] = jnp.broadcast_to(line, row_out.shape)
 
 
-OUTER_T = [(0, 7), (1, 0), (1, 6), (1, 7), (2, 0), (2, 1), (2, 5), (2, 6), (2, 7)]
-
-
-def combine(parts, b_ref, h_ref, p1, p2, q1, q2, t_in, t_out, adjoint, sensitivity):
+OUTER_T = [(1, 0), (1, 6), (2, 0), (2, 1), (2, 5), (2, 6)]
+
+
+def combine(
+    parts, b_ref, h_ref, p1, p2, q1, q2, t_in, t_out, strain_7, kept, u_next, adjoint, sensitivity,
+    modes,
+):
+    u_here, u_there = (kept, KEPT.index(("u", 7))), (modes, 0)
+    to_modes(lambda c: u_next[c], u_there)
     line = jnp.sum(parts[...], 0, keepdims=True)
     lane = iota((1, CZ), 1)
     m = [jnp.sum(jnp.where(lane == k, line, 0.0), 1, keepdims=True) for k in range(6)]
@@ -506,11 +502,21 @@
             v1 = q1[c, (-1, 0, 7).index(x), :CY] if x in (0, 7) else p1[c, x - 1, :CY]
             v2 = p2[c, x - 2, :CY] if 2 <= x < 6 else q2[c, (0, 1, 6, 7).index(x), :CY]
             adjoint[c, x] = weight[0] * b_ref[c, x] + weight[1] * v1 + weight[2] * v2
+        if x == 7:
+            continue
         product = None
         for k in range(3):
             part = t_out[OUTER_T.index((k, x))] if (k, x) in OUTER_T else t_in[k, x]
             product = weight[k] * part if product is None else product + weight[k] * part
         sensitivity[x] = 2.0 * (1.0 - h_ref[x]) * product
+    for j in range(0, CY, 8):
+        rows = pl.ds(j, 8)
+        stiff = stresses(strains(load(u_here, rows), load(u_there, rows)), None)
+        product = None
+        for k in range(3):
+            part = weight[k][:8] * inner([strain_7[k, i, rows, :] for i in range(18)], stiff)
+            product = part if product is None else product + part
+        sensitivity[7, rows, :] = 2.0 * (1.0 - h_ref[7, rows, :]) * product
 
 
 VMEM = pl.BlockSpec(memory_space=pltpu.VMEM)
@@ -520,7 +526,7 @@
     return jax.ShapeDtypeStruct(dims, F32)
 
 
-def call(kernel, name, megabytes, inputs, outputs, scratch=(), in_specs=None):
+def call(kernel, megabytes, inputs, outputs, scratch=(), in_specs=None):
     return pl.pallas_call(
         kernel,
         in_specs=in_specs or [VMEM] * len(inputs),
@@ -528,14 +534,13 @@
         out_shape=[shape(*dims) for dims in outputs],
         scratch_shapes=[s if not isinstance(s, tuple) else pltpu.VMEM(s, F32) for s in scratch],
         compiler_params=pltpu.CompilerParams(vmem_limit_bytes=megabytes and megabytes << 20),
-        name=name,
     )(*inputs)
 
 
 def body(misfit, damage, displacement):
     tile = (CX, 8, CZ)
     y_a, y_b = call(
-        pack_y, "pack_y", None,
+        pack_y, None,
         (misfit, damage, displacement),
         [(2,) + tile] * 2,
         [(3,) + tile, (3,) + tile, tile, tile, (3,) + tile, pltpu.SemaphoreType.DMA((5,))],
@@ -544,42 +549,46 @@
     y_b = exchange(y_b, "gy", 1)
     y_a = exchange(y_a, "gy", 0)
     misfit, damage, displacement = call(
-        stage, "stage", 4,
+        stage, 4,
         (misfit, damage, displacement),
         [(3, CX, CY, CZ), (CX, CY, CZ), (3, CX, CY, CZ)],
     )
     x_a, x_b, halo = call(
-        pack_x, "pack_x", 6,
-        (y_a, y_b, misfit, damage, displacement),
-        [(14, ROWS, CZ)] * 2 + [(7,) + tile],
+        pack_x, 6,
+        (y_a, y_b, misfit, damage),
+        [(11, ROWS, CZ)] * 2 + [(7,) + tile],
     )
     x_b = exchange(x_b, "gx", 1)
     x_a = exchange(x_a, "gx", 0)
     devices = lax.axis_size("gx") * lax.axis_size("gy")
     layer = (ROWS, CZ)
-    p1, p2, t_in, kept, opened, weights, sums = call(
-        inner_kernel, "inner", 20,
+    p1, p2, t_in, kept, opened, weights, sums, u_first = call(
+        inner_kernel, 20,
         (misfit, damage, displacement, halo),
         [
             (3, 6) + layer, (3, 4) + layer, (3, CX, CY, CZ), (12, len(KEPT)) + layer,
-            (12, len(OPEN)) + layer, (18, len(KEPT_WEIGHTS), CY, CZ), (6, 8, CZ),
+            (12, len(OPEN)) + layer, (18, len(KEPT_WEIGHTS), CY, CZ), (6, 8, CZ), (3,) + layer,
         ],
         [(12, CX) + layer, (12, CX) + layer, (18, CX, CY, CZ), (CX,) + layer],
     )
-    q1, q2, t_out, line = call(
-        outer_kernel, "outer", 20,
+    n = lax.axis_size("gx")
+    u_next = lax.ppermute(u_first, "gx", [(i, i - 1) for i in range(1, n)])
+    q1, q2, t_out, line, strain_7 = call(
+        outer_kernel, 20,
         (misfit, damage, halo, x_a, x_b, p1, p2, kept, opened, weights, sums),
-        [(3, 5) + layer, (3, 5) + layer, (len(OUTER_T), CY, CZ), (devices, CZ)],
+        [(3, 5) + layer, (3, 5) + layer, (len(OUTER_T), CY, CZ), (devices, CZ), (3, 18, CY, CZ)],
         [
-            (14,) + layer, (14,) + layer, (5,) + layer, (12, 16) + layer, (12, 5) + layer,
-            (18, CY, CZ), (6, 8, CZ),
+            (11,) + layer, (11,) + layer, (5,) + layer, (12, 15) + layer, (12, 5) + layer,
+            (6, 8, CZ),
         ],
     )
+    line, u_next = lax.optimization_barrier((line, u_next))
     parts = lax.all_to_all(line, AXES, 0, 0, tiled=True)
     return call(
-        combine, "combine", 8,
-        (parts, misfit, damage, p1, p2, q1, q2, t_in, t_out),
+        combine, 8,
+        (parts, misfit, damage, p1, p2, q1, q2, t_in, t_out, strain_7, kept, u_next),
         [(3, CX, CY, CZ), (CX, CY, CZ)],
+        [(12, 1, ROWS, CZ)],
     )
 
 

time: 54.4 us -> 57.1 us (1.050)
  waiting for transfers between devices: 2.82 us -> 4.4 us
  starting transfers between devices: 7.07 us -> 8.36 us
    ppermute x0 -> x1, waiting for transfers between devices: none -> 3.1 us  [body(): u_next = lax.ppermute(u_first, 'gx', [(i, i - 1) for i in range(1, n)])]
    ppermute x4, waiting for transfers between devices: 2.82 us -> 1.3 us  [exchange(): return lax.ppermute(x, axis, pairs)]
    ppermute x0 -> x1, starting transfers between devices: none -> 1.29 us  [body(): u_next = lax.ppermute(u_first, 'gx', [(i, i - 1) for i in range(1, n)])]
  transfers between devices with their start and end apart: 4 -> 5, of which waited for: 2 -> 2; matrix products, arithmetic and copies ran while one was open for 0% -> 0% of each run, Pallas kernels for 6% -> 10%
where the time goes in v4:
time: 57.1 us; the launch traced here: 56.8 us
  blocking collectives  31.9 us (56%)
  Pallas kernels  8.53 us (15%)
  starting transfers between devices  8.36 us (15%)
  waiting for transfers between devices  4.4 us (8%)
  local copies, waits for them, and re-layouts  2.89 us (5%)
  between operations  0.73 us (1%)
    all_to_all x1, blocking collectives, body(): parts = lax.all_to_all(line, AXES, 0, 0, tiled=True)  31.9 us
    pallas_call x6, Pallas kernels, call(): pl.pallas_call(kernel, in_specs=in_specs or [VMEM] * len(inputs), out_spe...  8.53 us
    ppermute x4, starting transfers between devices, exchange(): return lax.ppermute(x, axis, pairs)  7.07 us
    ppermute x1, waiting for transfers between devices, body(): u_next = lax.ppermute(u_first, 'gx', [(i, i - 1) for i in range(1, n)])  3.1 us
    unnamed x6, local copies, waits for them, and re-layouts  2.89 us
    ppermute x4, waiting for transfers between devices, exchange(): return lax.ppermute(x, axis, pairs)  1.3 us
    ppermute x1, starting transfers between devices, body(): u_next = lax.ppermute(u_first, 'gx', [(i, i - 1) for i in range(1, n)])  1.29 us
  transfers between devices with their start and end apart: 5, of which 2 were waited for; matrix products, arithmetic and copies ran while one was open for 0% of the time, Pallas kernels for 10%

profile of v4, /device:TPU:1, one launch (start us, length us, event | category | flops | bytes accessed | tf_op | source)
XLA Modules:
  0.0 56.8 jit_solution(2097939701132246234)
XLA Ops:
  0.6 1.8 %shard_map.51 = (f32[2,8,8,128]{3,2,1,0:T(8,128)}, f32[2,8,8,128]{3,2,1,0:T(8,128)}) custom-call(f32[3,8,32,128]{3,2,1,0:T(8,128)} %b.3, f32[8,32,128]{2,1,0:T(8,128)} %h.3, f32[3,8,32,128]{3,2,1,0:T(8,128)} %u.3), custom_call_target="tpu_custom_call" | custom-call | tf_op jit(solution)/shard_map/pallas_call | solution.py:530
  2.4 3.3 %collective-permute-start = (f32[2,8,8,128]{3,2,1,0:T(8,128)}, f32[2,8,8,128]{3,2,1,0:T(8,128)S(1)}, u32[]{:S(2)}, u32[]{:S(2)}) collective-permute-start(f32[2,8,8,128]{3,2,1,0:T(8,128)} %get-tuple-element.27), channel_id=1, source_target_pairs={{0,1},{1,0},{2,3},{3,2},{4,5},{5,4},{6,7},{7,6},{8,9},{9,8},{10,11... | collective-permute-start | bytes 196616 | tf_op jit(solution)/shard_map/ppermute | solution.py:22
  5.7 3.0 %collective-permute-start.1 = (f32[2,8,8,128]{3,2,1,0:T(8,128)}, f32[2,8,8,128]{3,2,1,0:T(8,128)S(1)}, u32[]{:S(2)}, u32[]{:S(2)}) collective-permute-start(f32[2,8,8,128]{3,2,1,0:T(8,128)} %get-tuple-element.28), channel_id=1, source_target_pairs={{1,2},{2,1},{5,6},{6,5},{9,10},{10,9},{13,14},{14,13},{17,18},{18,... | collective-permute-start | bytes 196616 | tf_op jit(solution)/shard_map/ppermute | solution.py:22
  8.7 0.0 copy-start
  8.7 1.0 %copy-done = f32[3,8,32,128]{3,2,1,0:T(8,128)S(1)} copy-done((f32[3,8,32,128]{3,2,1,0:T(8,128)S(1)}, f32[3,8,32,128]{3,2,1,0:T(8,128)}, u32[]{:S(2)}) %copy-start) | copy-done | bytes 393240
  9.7 0.0 copy-start.1
  9.7 1.0 %copy-done.1 = f32[3,8,32,128]{3,2,1,0:T(8,128)S(1)} copy-done((f32[3,8,32,128]{3,2,1,0:T(8,128)S(1)}, f32[3,8,32,128]{3,2,1,0:T(8,128)}, u32[]{:S(2)}) %copy-start.1) | copy-done | bytes 393240
  10.7 0.0 copy-start.2
  10.7 0.9 %copy-done.2 = f32[8,32,128]{2,1,0:T(8,128)S(1)} copy-done((f32[8,32,128]{2,1,0:T(8,128)S(1)}, f32[8,32,128]{2,1,0:T(8,128)}, u32[]{:S(2)}) %copy-start.2) | copy-done | bytes 131096
  11.6 0.1 shard_map.50
  11.7 0.0 collective-permute-done.y_a
  11.7 1.3 %collective-permute-done.1.y_b = f32[2,8,8,128]{3,2,1,0:T(8,128)S(1)} collective-permute-done((f32[2,8,8,128]{3,2,1,0:T(8,128)}, f32[2,8,8,128]{3,2,1,0:T(8,128)S(1)}, u32[]{:S(2)}, u32[]{:S(2)}) %collective-permute-start.1) | collective-permute-done | bytes 65568 | tf_op jit(solution)/shard_map/ppermute | solution.py:22
  13.0 0.1 shard_map.52
  13.0 0.1 collective-permute-start.2
  13.1 0.7 %collective-permute-start.3 = (f32[11,40,128]{2,1,0:T(8,128)S(1)}, f32[11,40,128]{2,1,0:T(8,128)S(1)}, u32[]{:S(2)}, u32[]{:S(2)}) collective-permute-start(f32[11,40,128]{2,1,0:T(8,128)S(1)} %get-tuple-element.31), channel_id=1, source_target_pairs={{4,8},{8,4},{12,16},{16,12},{20,24},{24,20},{28,32},{32,28},{36,40... | collective-permute-start | bytes 675848 | tf_op jit(solution)/shard_map/ppermute | solution.py:22
  13.8 3.2 %shard_map.53 = (f32[3,6,40,128]{3,2,1,0:T(8,128)S(1)}, f32[3,4,40,128]{3,2,1,0:T(8,128)S(1)}, f32[3,8,32,128]{3,2,1,0:T(8,128)S(1)}, f32[12,7,40,128]{3,2,1,0:T...) custom-call(f32[3,8,32,128]{3,2,1,0:T(8,128)S(1)} %get-tuple-element, ...), custom_call_target="tpu_custom_call" | custom-call | tf_op jit(solution)/shard_map/pallas_call | solution.py:530
  17.0 1.3 %collective-permute-start.4 = (f32[3,40,128]{2,1,0:T(8,128)S(1)}, f32[3,40,128]{2,1,0:T(8,128)S(1)}, u32[]{:S(2)}, u32[]{:S(2)}) collective-permute-start(f32[3,40,128]{2,1,0:T(8,128)S(1)} %get-tuple-element.40), channel_id=1, source_target_pairs={{4,0},{8,4},{12,8},{16,12},{20,16},{24,20},{28,24},{32,28},{36,32}... | collective-permute-start | bytes 184328 | tf_op jit(solution)/shard_map/ppermute | solution.py:575
  18.3 0.0 collective-permute-done.2.x_a
  18.3 0.0 collective-permute-done.3.x_b
  18.4 2.4 %shard_map.54 = (f32[3,5,40,128]{3,2,1,0:T(8,128)S(1)}, f32[3,5,40,128]{3,2,1,0:T(8,128)S(1)}, f32[6,32,128]{2,1,0:T(8,128)S(1)}, f32[256,128]{1,0:T(8,128)S(1)}, f32[3,18,32,128]{3,2,1,0:T(8,128)S(1)}) custom-call(f32[3,8,32,128]{3,2,1,0:T(8,128)S(1)} %get-tuple-element.25.b_ref, f32[8,32,128]{2,1,0:T(8,128)S(1)} %get-tuple-element.26.h_ref, ...), custom_call_target="tpu_custom_call" | custom-call | tf_op jit(solution)/shard_map/pallas_call | solution.py:530
  20.7 3.1 %collective-permute-done.4.u_next = f32[3,40,128]{2,1,0:T(8,128)S(1)} collective-permute-done((f32[3,40,128]{2,1,0:T(8,128)S(1)}, f32[3,40,128]{2,1,0:T(8,128)S(1)}, u32[]{:S(2)}, u32[]{:S(2)}) %collective-permute-start.4) | collective-permute-done | bytes 61472 | tf_op jit(solution)/shard_map/ppermute | solution.py:575
  23.8 31.9 %all_to_all.11 = f32[256,1,128]{2,1,0:T(1,128)S(1)} all-to-all(f32[256,1,128]{2,1,0:T(1,128)S(1)} %bitcast.5), channel_id=1, replica_groups=mesh['gx'=64,'gy'=4] {'gx','gy'}, dimensions={0} | all-to-all | bytes 262144 | tf_op jit(solution)/shard_map/all_to_all | solution.py:586
  55.7 1.1 %shard_map.55 = (f32[3,8,32,128]{3,2,1,0:T(8,128)}, f32[8,32,128]{2,1,0:T(8,128)}) custom-call(f32[256,128]{1,0:T(8,128)S(1)} %bitcast.4, f32[3,8,32,128]{3,2,1,0:T(8,128)S(1)} %get-tuple-element.25.b_ref, f32[8,32,128]{2,1,0:T(8,128)S(1)} %get-tuple-element.26.h_ref, f32[3,6,40,128]{3,2,1,0:T(8,128)S(1)} %get-tuple-element.33.p1, ...), custom_call_target="tpu_custom_call" | custom-call | tf_op jit(solution)/shard_map/pallas_call | solution.py:530
Async XLA Ops:
  2.4 9.3 %collective-permute-start = (f32[2,8,8,128]{3,2,1,0:T(8,128)}, f32[2,8,8,128]{3,2,1,0:T(8,128)S(1)}, u32[]{:S(2)}, u32[]{:S(2)}) collective-permute-start(f32[2,8,8,128]{3,2,1,0:T(8,128)} %get-tuple-element.27), channel_id=1, source_target_pairs={{0,1},{1,0},{2,3},{3,2},{4,5},{5,4},{6,7},{7,6},{8,9},{9,8},{10,11... | collective-permute-start | bytes 196616 | tf_op jit(solution)/shard_map/ppermute | solution.py:22
  5.7 7.3 %collective-permute-start.1 = (f32[2,8,8,128]{3,2,1,0:T(8,128)}, f32[2,8,8,128]{3,2,1,0:T(8,128)S(1)}, u32[]{:S(2)}, u32[]{:S(2)}) collective-permute-start(f32[2,8,8,128]{3,2,1,0:T(8,128)} %get-tuple-element.28), channel_id=1, source_target_pairs={{1,2},{2,1},{5,6},{6,5},{9,10},{10,9},{13,14},{14,13},{17,18},{18,... | collective-permute-start | bytes 196616 | tf_op jit(solution)/shard_map/ppermute | solution.py:22
  8.7 1.0 %copy-start = (f32[3,8,32,128]{3,2,1,0:T(8,128)S(1)}, f32[3,8,32,128]{3,2,1,0:T(8,128)}, u32[]{:S(2)}) copy-start(f32[3,8,32,128]{3,2,1,0:T(8,128)} %b.3) | copy-start | bytes 1179652
  9.7 1.0 %copy-start.1 = (f32[3,8,32,128]{3,2,1,0:T(8,128)S(1)}, f32[3,8,32,128]{3,2,1,0:T(8,128)}, u32[]{:S(2)}) copy-start(f32[3,8,32,128]{3,2,1,0:T(8,128)} %u.3) | copy-start | bytes 1179652
  10.7 0.9 %copy-start.2 = (f32[8,32,128]{2,1,0:T(8,128)S(1)}, f32[8,32,128]{2,1,0:T(8,128)}, u32[]{:S(2)}) copy-start(f32[8,32,128]{2,1,0:T(8,128)} %h.3) | copy-start | bytes 393220
  13.0 5.3 %collective-permute-start.2 = (f32[11,40,128]{2,1,0:T(8,128)S(1)}, f32[11,40,128]{2,1,0:T(8,128)S(1)}, u32[]{:S(2)}, u32[]{:S(2)}) collective-permute-start(f32[11,40,128]{2,1,0:T(8,128)S(1)} %get-tuple-element.30), channel_id=1, source_target_pairs={{0,4},{4,0},{8,12},{12,8},{16,20},{20,16},{24,28},{28,24},{32,36},... | collective-permute-start | bytes 675848 | tf_op jit(solution)/shard_map/ppermute | solution.py:22
  13.1 5.2 %collective-permute-start.3 = (f32[11,40,128]{2,1,0:T(8,128)S(1)}, f32[11,40,128]{2,1,0:T(8,128)S(1)}, u32[]{:S(2)}, u32[]{:S(2)}) collective-permute-start(f32[11,40,128]{2,1,0:T(8,128)S(1)} %get-tuple-element.31), channel_id=1, source_target_pairs={{4,8},{8,4},{12,16},{16,12},{20,24},{24,20},{28,32},{32,28},{36,40... | collective-permute-start | bytes 675848 | tf_op jit(solution)/shard_map/ppermute | solution.py:22
  17.0 6.8 %collective-permute-start.4 = (f32[3,40,128]{2,1,0:T(8,128)S(1)}, f32[3,40,128]{2,1,0:T(8,128)S(1)}, u32[]{:S(2)}, u32[]{:S(2)}) collective-permute-start(f32[3,40,128]{2,1,0:T(8,128)S(1)} %get-tuple-element.40), channel_id=1, source_target_pairs={{4,0},{8,4},{12,8},{16,12},{20,16},{24,20},{28,24},{32,28},{36,32}... | collective-permute-start | bytes 184328 | tf_op jit(solution)/shard_map/ppermute | solution.py:575

commit v5 on v4

--- a/solution.py
+++ b/solution.py
@@ -30,23 +30,18 @@
     return (1.0 - damage) * (1.0 - damage) + 0.001
 
 
-def pack_y(b, h, u, out_a, out_b, b_lo, b_hi, h_lo, h_hi, u_lo, done):
+def pack_y(b, h, u, out_a, out_b, b_all, h_all, u_all, done):
     copies = []
-    for k, (source, target) in enumerate(
-        (
-            (b.at[:, :, pl.ds(0, 8)], b_lo),
-            (b.at[:, :, pl.ds(CY - 8, 8)], b_hi),
-            (h.at[:, pl.ds(0, 8)], h_lo),
-            (h.at[:, pl.ds(CY - 8, 8)], h_hi),
-            (u.at[:, :, pl.ds(0, 8)], u_lo),
-        )
-    ):
+    for k, (source, target) in enumerate(((h, h_all), (b, b_all), (u, u_all))):
         copies.append(pltpu.make_async_copy(source, target, done.at[k]))
         copies[-1].start()
     for copy in copies:
         copy.wait()
+    b_lo, b_hi = b_all[:, :, :8], b_all[:, :, CY - 8 :]
+    h_lo, h_hi = h_all[:, :8], h_all[:, CY - 8 :]
+    u_lo = u_all[:, :, :8]
     row = iota((CX, 8, CZ), 1)
-    g_lo, g_hi = degradation_of(h_lo[...]), degradation_of(h_hi[...])
+    g_lo, g_hi = degradation_of(h_lo), degradation_of(h_hi)
     up = lambda x, k: pltpu.roll(x, k % 8, 1)
     low_1 = jnp.where(row < 3, b_lo[0], jnp.where(row < 6, up(b_lo[1], 3), up(g_lo, 6)))
     low_2 = jnp.where(
@@ -74,13 +69,7 @@
         out_b[0], out_b[1] = low_1, low_2
 
 
-def stage(b, h, u, b_out, h_out, u_out):
-    b_out[...] = b[...]
-    h_out[...] = h[...]
-    u_out[...] = u[...]
-
-
-def pack_x(y_a, y_b, b_ref, h_ref, out_a, out_b, halo):
+def pack_x(y_a, y_b, b_ref, h_ref, u_ref, out_a, out_b, halo, u_first):
     odd_y = lax.rem(lax.axis_index("gy"), 2) == 1
     row = iota((CX, 8, CZ), 1)
     up = lambda x, k: pltpu.roll(x, k % 8, 1)
@@ -97,6 +86,8 @@
     halo[3] = tile(up(above_1, -6), 2, below)
     for c in range(3):
         halo[4 + c] = jnp.where(row < 1, up(above_2, -3 - c), 0.0)
+    u_first[:, :CY] = u_ref[:, 0]
+    u_first[:, CY:] = halo[4:7, 0]
     odd_x = lax.rem(lax.axis_index("gx"), 2) == 1
 
     def low(out):
@@ -269,12 +260,10 @@
 
 
 def inner_kernel(
-    b_ref, h_ref, u_ref, halo, p1, p2, t, kept, opened, weights_out, sums, u_first,
+    b_ref, h_ref, u_ref, halo, p1, p2, t, kept, opened, weights_out, sums,
     modes, gathered, weights, g_ref,
 ):
     edge = row_edge()
-    u_first[:, :CY] = u_ref[:, 0]
-    u_first[:, CY:] = halo[4:7, 0]
     g_ref[:, :CY] = degradation_of(h_ref[...])
     g_ref[:, CY:] = halo[3]
     g = lambda e, rows: g_ref[e, rows, :]
@@ -533,46 +522,41 @@
         out_specs=[VMEM] * len(outputs),
         out_shape=[shape(*dims) for dims in outputs],
         scratch_shapes=[s if not isinstance(s, tuple) else pltpu.VMEM(s, F32) for s in scratch],
-        compiler_params=pltpu.CompilerParams(vmem_limit_bytes=megabytes and megabytes << 20),
+        compiler_params=pltpu.CompilerParams(vmem_limit_bytes=megabytes and int(megabytes * 2**20)),
     )(*inputs)
 
 
 def body(misfit, damage, displacement):
     tile = (CX, 8, CZ)
-    y_a, y_b = call(
-        pack_y, None,
-        (misfit, damage, displacement),
-        [(2,) + tile] * 2,
-        [(3,) + tile, (3,) + tile, tile, tile, (3,) + tile, pltpu.SemaphoreType.DMA((5,))],
+    y_a, y_b, misfit, damage, displacement = call(
+        pack_y, 4,
+        [pltpu.with_memory_space_constraint(x, pltpu.HBM) for x in (misfit, damage, displacement)],
+        [(2,) + tile, (2,) + tile, (3, CX, CY, CZ), (CX, CY, CZ), (3, CX, CY, CZ)],
+        [pltpu.SemaphoreType.DMA((3,))],
         [pl.BlockSpec(memory_space=pltpu.HBM)] * 3,
     )
     y_b = exchange(y_b, "gy", 1)
     y_a = exchange(y_a, "gy", 0)
-    misfit, damage, displacement = call(
-        stage, 4,
-        (misfit, damage, displacement),
-        [(3, CX, CY, CZ), (CX, CY, CZ), (3, CX, CY, CZ)],
-    )
-    x_a, x_b, halo = call(
+    x_a, x_b, halo, u_first = call(
         pack_x, 6,
-        (y_a, y_b, misfit, damage),
-        [(11, ROWS, CZ)] * 2 + [(7,) + tile],
+        (y_a, y_b, misfit, damage, displacement),
+        [(11, ROWS, CZ)] * 2 + [(7,) + tile, (3, ROWS, CZ)],
     )
     x_b = exchange(x_b, "gx", 1)
     x_a = exchange(x_a, "gx", 0)
     devices = lax.axis_size("gx") * lax.axis_size("gy")
     layer = (ROWS, CZ)
-    p1, p2, t_in, kept, opened, weights, sums, u_first = call(
+    n = lax.axis_size("gx")
+    u_next = lax.ppermute(u_first, "gx", [(i, i - 1) for i in range(1, n)])
+    p1, p2, t_in, kept, opened, weights, sums = call(
         inner_kernel, 20,
         (misfit, damage, displacement, halo),
         [
             (3, 6) + layer, (3, 4) + layer, (3, CX, CY, CZ), (12, len(KEPT)) + layer,
-            (12, len(OPEN)) + layer, (18, len(KEPT_WEIGHTS), CY, CZ), (6, 8, CZ), (3,) + layer,
+            (12, len(OPEN)) + layer, (18, len(KEPT_WEIGHTS), CY, CZ), (6, 8, CZ),
         ],
         [(12, CX) + layer, (12, CX) + layer, (18, CX, CY, CZ), (CX,) + layer],
     )
-    n = lax.axis_size("gx")
-    u_next = lax.ppermute(u_first, "gx", [(i, i - 1) for i in range(1, n)])
     q1, q2, t_out, line, strain_7 = call(
         outer_kernel, 20,
         (misfit, damage, halo, x_a, x_b, p1, p2, kept, opened, weights, sums),

time: 57.1 us -> 53.8 us (0.942)
  local copies, waits for them, and re-layouts: 2.89 us -> 0 us
  blocking collectives: 31.9 us -> 32.5 us
    ppermute x1, waiting for transfers between devices: 3.1 us -> 0.01 us  [body(): u_next = lax.ppermute(u_first, 'gx', [(i, i - 1) for i in range(1, n)])]
    unnamed x6 -> x0, local copies, waits for them, and re-layouts: 2.89 us -> none
    ppermute x4, waiting for transfers between devices: 1.3 us -> 4.05 us  [exchange(): return lax.ppermute(x, axis, pairs)]
    all_to_all x1, blocking collectives: 31.9 us -> 32.5 us  [body(): parts = lax.all_to_all(line, AXES, 0, 0, tiled=True)]
    pallas_call x6 -> x5, Pallas kernels: 8.53 us -> 7.96 us  [call(): pl.pallas_call(kernel, in_specs=in_specs or [VMEM] * len(inputs), out_spe...]
  transfers between devices with their start and end apart: 5 -> 5, of which waited for: 2 -> 1; matrix products, arithmetic and copies ran while one was open for 0% -> 0% of each run, Pallas kernels for 10% -> 10%
where the time goes in v5:
time: 53.8 us; the launch traced here: 53.6 us
  blocking collectives  32.5 us (60%)
  starting transfers between devices  8.37 us (16%)
  Pallas kernels  7.96 us (15%)
  waiting for transfers between devices  4.06 us (8%)
  between operations  0.72 us (1%)
    all_to_all x1, blocking collectives, body(): parts = lax.all_to_all(line, AXES, 0, 0, tiled=True)  32.5 us
    pallas_call x5, Pallas kernels, call(): pl.pallas_call(kernel, in_specs=in_specs or [VMEM] * len(inputs), out_spe...  7.96 us
    ppermute x4, starting transfers between devices, exchange(): return lax.ppermute(x, axis, pairs)  7.07 us
    ppermute x4, waiting for transfers between devices, exchange(): return lax.ppermute(x, axis, pairs)  4.05 us
    ppermute x1, starting transfers between devices, body(): u_next = lax.ppermute(u_first, 'gx', [(i, i - 1) for i in range(1, n)])  1.29 us
  transfers between devices with their start and end apart: 5, of which 1 were waited for; matrix products, arithmetic and copies ran while one was open for 0% of the time, Pallas kernels for 10%

profile of v5, /device:TPU:1, one launch (start us, length us, event | category | flops | bytes accessed | tf_op | source)
XLA Modules:
  0.0 53.6 jit_solution(4222810431270089507)
XLA Ops:
  0.6 1.3 %shard_map.50 = (f32[2,8,8,128]{3,2,1,0:T(8,128)S(1)}, f32[2,8,8,128]{3,2,1,0:T(8,128)S(1)}, f32[3,8,32,128]{3,2,1,0:T(8,128)S(1)}, f32[8,32,128]{2,1,0:T(8,128)S(1)}, f32[3,8,32,128]{3,2,1,0:T(8,128)S(1)}) custom-call(f32[3,8,32,128]{3,2,1,0:T(8,128)} %b.1, f32[8,32,128]{2,1,0:T(8,128)} %h.1, f32[3,8,32,128]{3,2,1,0:T(8,128)} %u.1), custom_call_target="tpu_custom_call" | custom-call | tf_op jit(solution)/shard_map/pallas_call | solution.py:519
  1.9 3.3 %collective-permute-start = (f32[2,8,8,128]{3,2,1,0:T(8,128)S(1)}, f32[2,8,8,128]{3,2,1,0:T(8,128)S(1)}, u32[]{:S(2)}, u32[]{:S(2)}) collective-permute-start(f32[2,8,8,128]{3,2,1,0:T(8,128)S(1)} %get-tuple-element.27), channel_id=1, source_target_pairs={{0,1},{1,0},{2,3},{3,2},{4,5},{5,4},{6,7},{7,6},{8,9},{9,8},{10,11... | collective-permute-start | bytes 196616 | tf_op jit(solution)/shard_map/ppermute | solution.py:22
  5.2 3.0 %collective-permute-start.1 = (f32[2,8,8,128]{3,2,1,0:T(8,128)S(1)}, f32[2,8,8,128]{3,2,1,0:T(8,128)S(1)}, u32[]{:S(2)}, u32[]{:S(2)}) collective-permute-start(f32[2,8,8,128]{3,2,1,0:T(8,128)S(1)} %get-tuple-element.28), channel_id=1, source_target_pairs={{1,2},{2,1},{5,6},{6,5},{9,10},{10,9},{13,14},{14,13},{17,18},{18,... | collective-permute-start | bytes 196616 | tf_op jit(solution)/shard_map/ppermute | solution.py:22
  8.2 0.0 collective-permute-done.y_a
  8.2 4.0 %collective-permute-done.1.y_b = f32[2,8,8,128]{3,2,1,0:T(8,128)S(1)} collective-permute-done((f32[2,8,8,128]{3,2,1,0:T(8,128)S(1)}, f32[2,8,8,128]{3,2,1,0:T(8,128)S(1)}, u32[]{:S(2)}, u32[]{:S(2)}) %collective-permute-start.1) | collective-permute-done | bytes 65568 | tf_op jit(solution)/shard_map/ppermute | solution.py:22
  12.3 0.1 shard_map.51
  12.3 0.1 collective-permute-start.2
  12.4 0.7 %collective-permute-start.3 = (f32[11,40,128]{2,1,0:T(8,128)S(1)}, f32[11,40,128]{2,1,0:T(8,128)S(1)}, u32[]{:S(2)}, u32[]{:S(2)}) collective-permute-start(f32[11,40,128]{2,1,0:T(8,128)S(1)} %get-tuple-element.32), channel_id=1, source_target_pairs={{4,8},{8,4},{12,16},{16,12},{20,24},{24,20},{28,32},{32,28},{36,40... | collective-permute-start | bytes 675848 | tf_op jit(solution)/shard_map/ppermute | solution.py:22
  13.1 1.3 %collective-permute-start.4 = (f32[3,40,128]{2,1,0:T(8,128)S(1)}, f32[3,40,128]{2,1,0:T(8,128)S(1)}, u32[]{:S(2)}, u32[]{:S(2)}) collective-permute-start(f32[3,40,128]{2,1,0:T(8,128)S(1)} %get-tuple-element.40), channel_id=1, source_target_pairs={{4,0},{8,4},{12,8},{16,12},{20,16},{24,20},{28,24},{32,28},{36,32}... | collective-permute-start | bytes 184328 | tf_op jit(solution)/shard_map/ppermute | solution.py:550
  14.4 3.2 %shard_map.52 = (f32[3,6,40,128]{3,2,1,0:T(8,128)S(1)}, f32[3,4,40,128]{3,2,1,0:T(8,128)S(1)}, f32[3,8,32,128]{3,2,1,0:T(8,128)S(1)}, f32[12,7,40,128]{3,2,1,0:T...) custom-call(f32[3,8,32,128]{3,2,1,0:T(8,128)S(1)} %get-tuple-element.25.b_ref,, ...), custom_call_target="tpu_custom_call" | custom-call | tf_op jit(solution)/shard_map/pallas_call | solution.py:519
  17.6 0.0 collective-permute-done.2.x_a
  17.6 0.0 collective-permute-done.3.x_b
  17.7 2.4 %shard_map.53 = (f32[3,5,40,128]{3,2,1,0:T(8,128)S(1)}, f32[3,5,40,128]{3,2,1,0:T(8,128)S(1)}, f32[6,32,128]{2,1,0:T(8,128)S(1)}, f32[256,128]{1,0:T(8,128)S(1)}, f32[3,18,32,128]{3,2,1,0:T(8,128)S(1)}) custom-call(f32[3,8,32,128]{3,2,1,0:T(8,128)S(1)} %get-tuple-element.25.b_ref, f32[8,32,128]{2,1,0:T(8,128)S(1)} %get-tuple-element.26.h_ref, ...), custom_call_target="tpu_custom_call" | custom-call | tf_op jit(solution)/shard_map/pallas_call | solution.py:519
  20.0 0.0 collective-permute-done.4.u_next
  20.0 32.5 %all_to_all.11 = f32[256,1,128]{2,1,0:T(1,128)S(1)} all-to-all(f32[256,1,128]{2,1,0:T(1,128)S(1)} %bitcast.5), channel_id=1, replica_groups=mesh['gx'=64,'gy'=4] {'gx','gy'}, dimensions={0} | all-to-all | bytes 262144 | tf_op jit(solution)/shard_map/all_to_all | solution.py:570
  52.6 1.1 %shard_map.54 = (f32[3,8,32,128]{3,2,1,0:T(8,128)}, f32[8,32,128]{2,1,0:T(8,128)}) custom-call(f32[256,128]{1,0:T(8,128)S(1)} %bitcast.4, f32[3,8,32,128]{3,2,1,0:T(8,128)S(1)} %get-tuple-element.25.b_ref, f32[8,32,128]{2,1,0:T(8,128)S(1)} %get-tuple-element.26.h_ref, f32[3,6,40,128]{3,2,1,0:T(8,128)S(1)} %get-tuple-element.33.p1, ...), custom_call_target="tpu_custom_call" | custom-call | tf_op jit(solution)/shard_map/pallas_call | solution.py:519
Async XLA Ops:
  1.9 6.3 %collective-permute-start = (f32[2,8,8,128]{3,2,1,0:T(8,128)S(1)}, f32[2,8,8,128]{3,2,1,0:T(8,128)S(1)}, u32[]{:S(2)}, u32[]{:S(2)}) collective-permute-start(f32[2,8,8,128]{3,2,1,0:T(8,128)S(1)} %get-tuple-element.27), channel_id=1, source_target_pairs={{0,1},{1,0},{2,3},{3,2},{4,5},{5,4},{6,7},{7,6},{8,9},{9,8},{10,11... | collective-permute-start | bytes 196616 | tf_op jit(solution)/shard_map/ppermute | solution.py:22
  5.2 7.1 %collective-permute-start.1 = (f32[2,8,8,128]{3,2,1,0:T(8,128)S(1)}, f32[2,8,8,128]{3,2,1,0:T(8,128)S(1)}, u32[]{:S(2)}, u32[]{:S(2)}) collective-permute-start(f32[2,8,8,128]{3,2,1,0:T(8,128)S(1)} %get-tuple-element.28), channel_id=1, source_target_pairs={{1,2},{2,1},{5,6},{6,5},{9,10},{10,9},{13,14},{14,13},{17,18},{18,... | collective-permute-start | bytes 196616 | tf_op jit(solution)/shard_map/ppermute | solution.py:22
  12.3 5.3 %collective-permute-start.2 = (f32[11,40,128]{2,1,0:T(8,128)S(1)}, f32[11,40,128]{2,1,0:T(8,128)S(1)}, u32[]{:S(2)}, u32[]{:S(2)}) collective-permute-start(f32[11,40,128]{2,1,0:T(8,128)S(1)} %get-tuple-element.31), channel_id=1, source_target_pairs={{0,4},{4,0},{8,12},{12,8},{16,20},{20,16},{24,28},{28,24},{32,36},... | collective-permute-start | bytes 675848 | tf_op jit(solution)/shard_map/ppermute | solution.py:22
  12.4 5.2 %collective-permute-start.3 = (f32[11,40,128]{2,1,0:T(8,128)S(1)}, f32[11,40,128]{2,1,0:T(8,128)S(1)}, u32[]{:S(2)}, u32[]{:S(2)}) collective-permute-start(f32[11,40,128]{2,1,0:T(8,128)S(1)} %get-tuple-element.32), channel_id=1, source_target_pairs={{4,8},{8,4},{12,16},{16,12},{20,24},{24,20},{28,32},{32,28},{36,40... | collective-permute-start | bytes 675848 | tf_op jit(solution)/shard_map/ppermute | solution.py:22
  13.1 6.9 %collective-permute-start.4 = (f32[3,40,128]{2,1,0:T(8,128)S(1)}, f32[3,40,128]{2,1,0:T(8,128)S(1)}, u32[]{:S(2)}, u32[]{:S(2)}) collective-permute-start(f32[3,40,128]{2,1,0:T(8,128)S(1)} %get-tuple-element.40), channel_id=1, source_target_pairs={{4,0},{8,4},{12,8},{16,12},{20,16},{24,20},{28,24},{32,28},{36,32}... | collective-permute-start | bytes 184328 | tf_op jit(solution)/shard_map/ppermute | solution.py:550

commit v6 on v5

--- a/solution.py
+++ b/solution.py
@@ -30,13 +30,14 @@
     return (1.0 - damage) * (1.0 - damage) + 0.001
 
 
-def pack_y(b, h, u, out_a, out_b, b_all, h_all, u_all, done):
+def pack_y(b, h, u, out_a, out_b, b_all, h_all, u_all, u_first, done):
     copies = []
     for k, (source, target) in enumerate(((h, h_all), (b, b_all), (u, u_all))):
         copies.append(pltpu.make_async_copy(source, target, done.at[k]))
         copies[-1].start()
     for copy in copies:
         copy.wait()
+    u_first[...] = u_all[:, 0]
     b_lo, b_hi = b_all[:, :, :8], b_all[:, :, CY - 8 :]
     h_lo, h_hi = h_all[:, :8], h_all[:, CY - 8 :]
     u_lo = u_all[:, :, :8]
@@ -69,7 +70,7 @@
         out_b[0], out_b[1] = low_1, low_2
 
 
-def pack_x(y_a, y_b, b_ref, h_ref, u_ref, out_a, out_b, halo, u_first):
+def pack_x(y_a, y_b, b_ref, h_ref, out_a, out_b, halo):
     odd_y = lax.rem(lax.axis_index("gy"), 2) == 1
     row = iota((CX, 8, CZ), 1)
     up = lambda x, k: pltpu.roll(x, k % 8, 1)
@@ -86,14 +87,15 @@
     halo[3] = tile(up(above_1, -6), 2, below)
     for c in range(3):
         halo[4 + c] = jnp.where(row < 1, up(above_2, -3 - c), 0.0)
-    u_first[:, :CY] = u_ref[:, 0]
-    u_first[:, CY:] = halo[4:7, 0]
     odd_x = lax.rem(lax.axis_index("gx"), 2) == 1
 
     def low(out):
         for c in range(3):
             for x in range(3):
-                out[3 * c + x, :CY], out[3 * c + x, CY:] = b_ref[c, x], halo[c, x]
+                edge = halo[c, x]
+                if x == 0:
+                    edge = jnp.where(row[0] == 3, pltpu.roll(halo[4 + c, 0], 3, 0), edge)
+                out[3 * c + x, :CY], out[3 * c + x, CY:] = b_ref[c, x], edge
         for x in range(2):
             out[9 + x, :CY], out[9 + x, CY:] = degradation_of(h_ref[x]), halo[3, x]
 
@@ -354,7 +356,7 @@
 
 def outer_kernel(
     b_ref, h_ref, halo, x_a, x_b, p1, p2, kept, opened, weights_in, sums_in,
-    q1, q2, t, row_out, strain_7, above, below, g_ref, modes, gathered, sums,
+    q1, q2, t, row_out, strain_7, u_edge, above, below, g_ref, modes, gathered, sums,
 ):
     edge = row_edge()
     odd_x = lax.rem(lax.axis_index("gx"), 2) == 1
@@ -371,6 +373,8 @@
         above[...] = x_a[...]
         below[...] = x_b[...]
 
+    for c in range(3):
+        u_edge[c] = pltpu.roll(above[3 * c, CY:], 5, 0)
     for k, e in enumerate((0, 1, 5, 6, 7)):
         g_ref[k, :CY] = degradation_of(h_ref[e])
         g_ref[k, CY:] = halo[3, e]
@@ -468,11 +472,11 @@
 
 
 def combine(
-    parts, b_ref, h_ref, p1, p2, q1, q2, t_in, t_out, strain_7, kept, u_next, adjoint, sensitivity,
+    parts, b_ref, h_ref, p1, p2, q1, q2, t_in, t_out, strain_7, kept, u_next, u_edge, adjoint, sensitivity,
     modes,
 ):
     u_here, u_there = (kept, KEPT.index(("u", 7))), (modes, 0)
-    to_modes(lambda c: u_next[c], u_there)
+    to_modes(lambda c: jnp.concatenate([u_next[c], u_edge[c]], 0), u_there)
     line = jnp.sum(parts[...], 0, keepdims=True)
     lane = iota((1, CZ), 1)
     m = [jnp.sum(jnp.where(lane == k, line, 0.0), 1, keepdims=True) for k in range(6)]
@@ -528,26 +532,28 @@
 
 def body(misfit, damage, displacement):
     tile = (CX, 8, CZ)
-    y_a, y_b, misfit, damage, displacement = call(
+    y_a, y_b, misfit, damage, displacement, u_first = call(
         pack_y, 4,
         [pltpu.with_memory_space_constraint(x, pltpu.HBM) for x in (misfit, damage, displacement)],
-        [(2,) + tile, (2,) + tile, (3, CX, CY, CZ), (CX, CY, CZ), (3, CX, CY, CZ)],
+        [
+            (2,) + tile, (2,) + tile, (3, CX, CY, CZ), (CX, CY, CZ), (3, CX, CY, CZ), (3, CY, CZ),
+        ],
         [pltpu.SemaphoreType.DMA((3,))],
         [pl.BlockSpec(memory_space=pltpu.HBM)] * 3,
     )
     y_b = exchange(y_b, "gy", 1)
     y_a = exchange(y_a, "gy", 0)
-    x_a, x_b, halo, u_first = call(
+    n = lax.axis_size("gx")
+    u_next = lax.ppermute(u_first, "gx", [(i, i - 1) for i in range(1, n)])
+    x_a, x_b, halo = call(
         pack_x, 6,
-        (y_a, y_b, misfit, damage, displacement),
-        [(11, ROWS, CZ)] * 2 + [(7,) + tile, (3, ROWS, CZ)],
+        (y_a, y_b, misfit, damage),
+        [(11, ROWS, CZ)] * 2 + [(7,) + tile],
     )
     x_b = exchange(x_b, "gx", 1)
     x_a = exchange(x_a, "gx", 0)
     devices = lax.axis_size("gx") * lax.axis_size("gy")
     layer = (ROWS, CZ)
-    n = lax.axis_size("gx")
-    u_next = lax.ppermute(u_first, "gx", [(i, i - 1) for i in range(1, n)])
     p1, p2, t_in, kept, opened, weights, sums = call(
         inner_kernel, 20,
         (misfit, damage, displacement, halo),
@@ -557,10 +563,10 @@
         ],
         [(12, CX) + layer, (12, CX) + layer, (18, CX, CY, CZ), (CX,) + layer],
     )
-    q1, q2, t_out, line, strain_7 = call(
+    q1, q2, t_out, line, strain_7, u_edge = call(
         outer_kernel, 20,
         (misfit, damage, halo, x_a, x_b, p1, p2, kept, opened, weights, sums),
-        [(3, 5) + layer, (3, 5) + layer, (len(OUTER_T), CY, CZ), (devices, CZ), (3, 18, CY, CZ)],
+        [(3, 5) + layer, (3, 5) + layer, (len(OUTER_T), CY, CZ), (devices, CZ), (3, 18, CY, CZ), (3, 8, CZ)],
         [
             (11,) + layer, (11,) + layer, (5,) + layer, (12, 15) + layer, (12, 5) + layer,
             (6, 8, CZ),
@@ -570,7 +576,7 @@
     parts = lax.all_to_all(line, AXES, 0, 0, tiled=True)
     return call(
         combine, 8,
-        (parts, misfit, damage, p1, p2, q1, q2, t_in, t_out, strain_7, kept, u_next),
+        (parts, misfit, damage, p1, p2, q1, q2, t_in, t_out, strain_7, kept, u_next, u_edge),
         [(3, CX, CY, CZ), (CX, CY, CZ)],
         [(12, 1, ROWS, CZ)],
     )

time: 53.8 us -> 53.9 us (level)
  no operation moved by 1% of the time
where the time goes in v6:
time: 53.9 us; the launch traced here: 53.7 us
  blocking collectives  32.5 us (60%)
  starting transfers between devices  8.36 us (16%)
  Pallas kernels  7.98 us (15%)
  waiting for transfers between devices  4.06 us (8%)
  between operations  0.72 us (1%)
    all_to_all x1, blocking collectives, body(): parts = lax.all_to_all(line, AXES, 0, 0, tiled=True)  32.5 us
    pallas_call x5, Pallas kernels, call(): pl.pallas_call(kernel, in_specs=in_specs or [VMEM] * len(inputs), out_spe...  7.98 us
    ppermute x4, starting transfers between devices, exchange(): return lax.ppermute(x, axis, pairs)  7.07 us
    ppermute x4, waiting for transfers between devices, exchange(): return lax.ppermute(x, axis, pairs)  4.05 us
    ppermute x1, starting transfers between devices, body(): u_next = lax.ppermute(u_first, 'gx', [(i, i - 1) for i in range(1, n)])  1.29 us
  transfers between devices with their start and end apart: 5, of which 1 were waited for; matrix products, arithmetic and copies ran while one was open for 0% of the time, Pallas kernels for 10%

profile of v6, /device:TPU:1, one launch (start us, length us, event | category | flops | bytes accessed | tf_op | source)
XLA Modules:
  0.0 53.7 jit_solution(17717368331378363784)
XLA Ops:
  0.6 1.3 %shard_map.50 = (f32[2,8,8,128]{3,2,1,0:T(8,128)S(1)}, f32[2,8,8,128]{3,2,1,0:T(8,128)S(1)}, f32[3,8,32,128]{3,2,1,0:T(8,128)S(1)}, f32[8,32,128]{2,1,0:T(8,128)...) custom-call(f32[3,8,32,128]{3,2,1,0:T(8,128)} %b.1, f32[8,32,128]{2,1,0:T(8,128)} %h.1, f32[3,8,32,128]{3,2,1,0:T(8,128)} %u.1), custom_call_target="tpu_custom_call" | custom-call | tf_op jit(solution)/shard_map/pallas_call | solution.py:523
  1.9 3.3 %collective-permute-start = (f32[2,8,8,128]{3,2,1,0:T(8,128)S(1)}, f32[2,8,8,128]{3,2,1,0:T(8,128)S(1)}, u32[]{:S(2)}, u32[]{:S(2)}) collective-permute-start(f32[2,8,8,128]{3,2,1,0:T(8,128)S(1)} %get-tuple-element.28), channel_id=1, source_target_pairs={{0,1},{1,0},{2,3},{3,2},{4,5},{5,4},{6,7},{7,6},{8,9},{9,8},{10,11... | collective-permute-start | bytes 196616 | tf_op jit(solution)/shard_map/ppermute | solution.py:22
  5.2 3.0 %collective-permute-start.1 = (f32[2,8,8,128]{3,2,1,0:T(8,128)S(1)}, f32[2,8,8,128]{3,2,1,0:T(8,128)S(1)}, u32[]{:S(2)}, u32[]{:S(2)}) collective-permute-start(f32[2,8,8,128]{3,2,1,0:T(8,128)S(1)} %get-tuple-element.29), channel_id=1, source_target_pairs={{1,2},{2,1},{5,6},{6,5},{9,10},{10,9},{13,14},{14,13},{17,18},{18,... | collective-permute-start | bytes 196616 | tf_op jit(solution)/shard_map/ppermute | solution.py:22
  8.2 0.0 collective-permute-done.y_a
  8.2 4.0 %collective-permute-done.1.y_b = f32[2,8,8,128]{3,2,1,0:T(8,128)S(1)} collective-permute-done((f32[2,8,8,128]{3,2,1,0:T(8,128)S(1)}, f32[2,8,8,128]{3,2,1,0:T(8,128)S(1)}, u32[]{:S(2)}, u32[]{:S(2)}) %collective-permute-start.1) | collective-permute-done | bytes 65568 | tf_op jit(solution)/shard_map/ppermute | solution.py:22
  12.3 0.1 shard_map.51
  12.3 0.1 collective-permute-start.2
  12.4 0.7 %collective-permute-start.3 = (f32[11,40,128]{2,1,0:T(8,128)S(1)}, f32[11,40,128]{2,1,0:T(8,128)S(1)}, u32[]{:S(2)}, u32[]{:S(2)}) collective-permute-start(f32[11,40,128]{2,1,0:T(8,128)S(1)} %get-tuple-element.32), channel_id=1, source_target_pairs={{4,8},{8,4},{12,16},{16,12},{20,24},{24,20},{28,32},{32,28},{36,40... | collective-permute-start | bytes 675848 | tf_op jit(solution)/shard_map/ppermute | solution.py:22
  13.1 1.3 %collective-permute-start.4 = (f32[3,32,128]{2,1,0:T(8,128)S(1)}, f32[3,32,128]{2,1,0:T(8,128)S(1)}, u32[]{:S(2)}, u32[]{:S(2)}) collective-permute-start(f32[3,32,128]{2,1,0:T(8,128)S(1)} %get-tuple-element.41), channel_id=1, source_target_pairs={{4,0},{8,4},{12,8},{16,12},{20,16},{24,20},{28,24},{32,28},{36,32}... | collective-permute-start | bytes 147464 | tf_op jit(solution)/shard_map/ppermute | solution.py:547
  14.4 3.2 %shard_map.52 = (f32[3,6,40,128]{3,2,1,0:T(8,128)S(1)}, f32[3,4,40,128]{3,2,1,0:T(8,128)S(1)}, f32[3,8,32,128]{3,2,1,0:T(8,128)S(1)}, f32[12,7,40,128]{3,2,1,0:T...) custom-call(f32[3,8,32,128]{3,2,1,0:T(8,128)S(1)} %get-tuple-element.26.b_ref,, ...), custom_call_target="tpu_custom_call" | custom-call | tf_op jit(solution)/shard_map/pallas_call | solution.py:523
  17.6 0.0 collective-permute-done.2.x_a
  17.7 0.0 collective-permute-done.3.x_b
  17.7 2.3 %shard_map.53 = (f32[3,5,40,128]{3,2,1,0:T(8,128)S(1)}, f32[3,5,40,128]{3,2,1,0:T(8,128)S(1)}, f32[6,32,128]{2,1,0:T(8,128)S(1)}, f32[256,128]{1,0:T(8,128)S(1)}...) custom-call(f32[3,8,32,128]{3,2,1,0:T(8,128)S(1)} %get-tuple-element.26.b_ref, ...), custom_call_target="tpu_custom_call" | custom-call | tf_op jit(solution)/shard_map/pallas_call | solution.py:523
  20.0 0.0 collective-permute-done.4.u_next
  20.0 32.5 %all_to_all.11 = f32[256,1,128]{2,1,0:T(1,128)S(1)} all-to-all(f32[256,1,128]{2,1,0:T(1,128)S(1)} %bitcast.5), channel_id=1, replica_groups=mesh['gx'=64,'gy'=4] {'gx','gy'}, dimensions={0} | all-to-all | bytes 262144 | tf_op jit(solution)/shard_map/all_to_all | solution.py:576
  52.6 1.1 %shard_map.54 = (f32[3,8,32,128]{3,2,1,0:T(8,128)}, f32[8,32,128]{2,1,0:T(8,128)}) custom-call(f32[256,128]{1,0:T(8,128)S(1)} %bitcast.4, f32[3,8,32,128]{3,2,1,0:T(8,128)S(1)} %get-tuple-element.26.b_ref, f32[8,32,128]{2,1,0:T(8,128)S(1)} %get-tuple-element.27.h_ref, f32[3,6,40,128]{3,2,1,0:T(8,128)S(1)} %get-tuple-element.34.p1, ...), custom_call_target="tpu_custom_call" | custom-call | tf_op jit(solution)/shard_map/pallas_call | solution.py:523
Async XLA Ops:
  1.9 6.3 %collective-permute-start = (f32[2,8,8,128]{3,2,1,0:T(8,128)S(1)}, f32[2,8,8,128]{3,2,1,0:T(8,128)S(1)}, u32[]{:S(2)}, u32[]{:S(2)}) collective-permute-start(f32[2,8,8,128]{3,2,1,0:T(8,128)S(1)} %get-tuple-element.28), channel_id=1, source_target_pairs={{0,1},{1,0},{2,3},{3,2},{4,5},{5,4},{6,7},{7,6},{8,9},{9,8},{10,11... | collective-permute-start | bytes 196616 | tf_op jit(solution)/shard_map/ppermute | solution.py:22
  5.2 7.1 %collective-permute-start.1 = (f32[2,8,8,128]{3,2,1,0:T(8,128)S(1)}, f32[2,8,8,128]{3,2,1,0:T(8,128)S(1)}, u32[]{:S(2)}, u32[]{:S(2)}) collective-permute-start(f32[2,8,8,128]{3,2,1,0:T(8,128)S(1)} %get-tuple-element.29), channel_id=1, source_target_pairs={{1,2},{2,1},{5,6},{6,5},{9,10},{10,9},{13,14},{14,13},{17,18},{18,... | collective-permute-start | bytes 196616 | tf_op jit(solution)/shard_map/ppermute | solution.py:22
  12.3 5.3 %collective-permute-start.2 = (f32[11,40,128]{2,1,0:T(8,128)S(1)}, f32[11,40,128]{2,1,0:T(8,128)S(1)}, u32[]{:S(2)}, u32[]{:S(2)}) collective-permute-start(f32[11,40,128]{2,1,0:T(8,128)S(1)} %get-tuple-element.31), channel_id=1, source_target_pairs={{0,4},{4,0},{8,12},{12,8},{16,20},{20,16},{24,28},{28,24},{32,36},... | collective-permute-start | bytes 675848 | tf_op jit(solution)/shard_map/ppermute | solution.py:22
  12.4 5.2 %collective-permute-start.3 = (f32[11,40,128]{2,1,0:T(8,128)S(1)}, f32[11,40,128]{2,1,0:T(8,128)S(1)}, u32[]{:S(2)}, u32[]{:S(2)}) collective-permute-start(f32[11,40,128]{2,1,0:T(8,128)S(1)} %get-tuple-element.32), channel_id=1, source_target_pairs={{4,8},{8,4},{12,16},{16,12},{20,24},{24,20},{28,32},{32,28},{36,40... | collective-permute-start | bytes 675848 | tf_op jit(solution)/shard_map/ppermute | solution.py:22
  13.1 6.9 %collective-permute-start.4 = (f32[3,32,128]{2,1,0:T(8,128)S(1)}, f32[3,32,128]{2,1,0:T(8,128)S(1)}, u32[]{:S(2)}, u32[]{:S(2)}) collective-permute-start(f32[3,32,128]{2,1,0:T(8,128)S(1)} %get-tuple-element.41), channel_id=1, source_target_pairs={{4,0},{8,4},{12,8},{16,12},{20,16},{24,20},{28,24},{32,28},{36,32}... | collective-permute-start | bytes 147464 | tf_op jit(solution)/shard_map/ppermute | solution.py:547

commit v7 on v6

--- a/solution.py
+++ b/solution.py
@@ -197,14 +197,14 @@
 def each_chunk(step, halo_too):
     @pl.loop(0, CY // 8)
     def _(j):
-        step(pl.ds(pl.multiple_of(8 * j, 8), 8), True)
+        step(pl.ds(pl.multiple_of(8 * j, 8), 8))
 
     if halo_too:
-        step(pl.ds(CY, 8), False)
-
-
-def sweep(elements, modes, g, add, put, visit=None):
-    def step(rows, own):
+        step(pl.ds(CY, 8))
+
+
+def sweep(elements, modes, g, add, put):
+    def step(rows):
         here = load(modes[elements[0]], rows)
         before = None
 
@@ -222,10 +222,7 @@
 
         for e in elements:
             there = load(modes[e + 1], rows)
-            strain = strains(here, there)
-            if own and visit is not None:
-                visit(e, strain, rows)
-            s, d = x_forces(stresses(strain, g(e, rows)))
+            s, d = x_forces(stresses(strains(here, there), g(e, rows)))
             if e in put:
                 store(e, [p - q if p is not None else -q for p, q in zip(s, d)])
             before = [p + q if p is not None else q for p, q in zip(s, d)]
@@ -256,15 +253,21 @@
     return jnp.where(row < 3, jnp.where(last, 0.0, 1.0).astype(F32), 1.0)
 
 
-KEPT = ("b", 0), ("b", 7), ("p1", 1), ("p1", 6), ("p2", 2), ("p2", 5), ("u", 7)
+KEPT = ("b", 0), ("b", 7), ("p1", 1), ("p1", 6), ("p2", 2), ("p2", 5)
 OPEN = ("p1", 0), ("p1", 7), ("p2", 1), ("p2", 6)
-KEPT_WEIGHTS = (0, 1, 5, 6)
-
-
-def inner_kernel(
-    b_ref, h_ref, u_ref, halo, p1, p2, t, kept, opened, weights_out, sums,
-    modes, gathered, weights, g_ref,
-):
+
+
+def add_energy(total, elements, modes, g, rows):
+    here = load(modes[elements[0]], rows)
+    for e in elements:
+        there = load(modes[e + 1], rows)
+        strain = strains(here, there)
+        total = total + inner(strain, stresses(strain, g(e, rows)))
+        here = there
+    return total
+
+
+def inner_kernel(b_ref, h_ref, halo, p1, p2, kept, opened, sums, modes, gathered, g_ref):
     edge = row_edge()
     g_ref[:, :CY] = degradation_of(h_ref[...])
     g_ref[:, CY:] = halo[3]
@@ -273,43 +276,12 @@
     open_at = {name: (opened, k) for k, name in enumerate(OPEN)}
     at = lambda name, n: keep.get((name, n), (modes, n))
 
-    def own(ref, first, n):
-        return lambda c: jnp.concatenate([ref[c, n], halo[first + c, n]], 0)
-
-    u_modes = {n: at("u", n) for n in range(CX)}
-    for n in range(CX):
-        to_modes(own(u_ref, 4, n), u_modes[n])
-
-    def stiffen(rows, _):
-        here = load(u_modes[0], rows)
-        for e in range(7):
-            there = load(u_modes[e + 1], rows)
-            for k, f in enumerate(stresses(strains(here, there), None)):
-                if e in KEPT_WEIGHTS:
-                    weights_out[k, KEPT_WEIGHTS.index(e), rows, :] = f
-                else:
-                    weights[k, e, rows, :] = f
-            here = there
-
-    each_chunk(stiffen, False)
-
-    def weight(e, rows):
-        if e in KEPT_WEIGHTS:
-            return [weights_out[k, KEPT_WEIGHTS.index(e), rows, :] for k in range(18)]
-        return [weights[k, e, rows, :] for k in range(18)]
-
-    def visit(power):
-        def f(e, strain, rows):
-            t[power, e, rows, :] = inner(strain, weight(e, rows))
-
-        return f
-
     b_modes = {n: at("b", n) for n in range(CX)}
     for n in range(CX):
-        to_modes(own(b_ref, 0, n), b_modes[n])
+        to_modes(lambda c, n=n: jnp.concatenate([b_ref[c, n], halo[c, n]], 0), b_modes[n])
     put = {n: (gathered, n) for n in range(1, 7)}
     put.update({0: open_at["p1", 0], 7: open_at["p1", 7]})
-    sweep(range(0, 7), b_modes, g, {}, put, visit(0))
+    sweep(range(0, 7), b_modes, g, {}, put)
     for n in range(1, 7):
         finish(put[n], (p1, n - 1), edge)
 
@@ -318,7 +290,7 @@
         to_modes(lambda c, n=n: p1[c, n - 1], p1_modes[n])
     put = {n: (gathered, n) for n in range(2, 6)}
     put.update({1: open_at["p2", 1], 6: open_at["p2", 6]})
-    sweep(range(1, 6), p1_modes, g, {}, put, visit(1))
+    sweep(range(1, 6), p1_modes, g, {}, put)
     for n in range(2, 6):
         finish(put[n], (p2, n - 2), edge)
 
@@ -327,16 +299,8 @@
         to_modes(lambda c, n=n: p2[c, n - 2], p2_modes[n])
     sums[...] = jnp.zeros_like(sums)
 
-    def energy(rows, _):
-        here = load(p2_modes[2], rows)
-        total = jnp.zeros((8, CZ), F32)
-        for e in range(2, 5):
-            there = load(p2_modes[e + 1], rows)
-            strain = strains(here, there)
-            t[2, e, rows, :] = inner(strain, weight(e, rows))
-            total = total + inner(strain, stresses(strain, g(e, rows)))
-            here = there
-        sums[5] += total
+    def energy(rows):
+        sums[5] += add_energy(jnp.zeros((8, CZ), F32), range(2, 5), p2_modes, g, rows)
 
     each_chunk(energy, False)
     total = [jnp.zeros((8, CZ), F32)] * 5
@@ -355,8 +319,8 @@
 
 
 def outer_kernel(
-    b_ref, h_ref, halo, x_a, x_b, p1, p2, kept, opened, weights_in, sums_in,
-    q1, q2, t, row_out, strain_7, u_edge, above, below, g_ref, modes, gathered, sums,
+    b_ref, h_ref, halo, x_a, x_b, p1, p2, kept, opened, sums_in,
+    q1, q2, row_out, b_next, u_edge, above, below, g_ref, modes, gathered, sums,
 ):
     edge = row_edge()
     odd_x = lax.rem(lax.axis_index("gx"), 2) == 1
@@ -375,6 +339,7 @@
 
     for c in range(3):
         u_edge[c] = pltpu.roll(above[3 * c, CY:], 5, 0)
+        b_next[c] = above[3 * c]
     for k, e in enumerate((0, 1, 5, 6, 7)):
         g_ref[k, :CY] = degradation_of(h_ref[e])
         g_ref[k, CY:] = halo[3, e]
@@ -394,19 +359,6 @@
         out = {n: (modes, new[0] + k) for k, n in enumerate(nodes)}
         new[0] += len(nodes)
         return out
-
-    def weight(e, rows):
-        return [weights_in[k, KEPT_WEIGHTS.index(e), rows, :] for k in range(18)]
-
-    def visit(power):
-        def f(e, strain, rows):
-            if e == 7:
-                for k in range(18):
-                    strain_7[power, k, rows, :] = strain[k]
-            elif (power, e) in OUTER_T:
-                t[OUTER_T.index((power, e)), rows, :] = inner(strain, weight(e, rows))
-
-        return f
 
     b_modes = fresh([-2, -1, 8, 9, 10])
     for n in (-2, -1):
@@ -416,8 +368,8 @@
     b_modes.update({0: keep["b", 0], 7: keep["b", 7]})
     nodes = (-1, 0, 7, 8, 9)
     put = {n: (gathered, k) for k, n in enumerate(nodes)}
-    sweep((-2, -1), b_modes, g, {0: open_at["p1", 0]}, put, visit(0))
-    sweep((7, 8, 9), b_modes, g, {7: open_at["p1", 7]}, put, visit(0))
+    sweep((-2, -1), b_modes, g, {0: open_at["p1", 0]}, put)
+    sweep((7, 8, 9), b_modes, g, {7: open_at["p1", 7]}, put)
     for k, n in enumerate(nodes):
         finish(put[n], (q1, k), edge, past_x if n >= CX else None)
 
@@ -427,8 +379,8 @@
     p1_modes.update({1: keep["p1", 1], 6: keep["p1", 6]})
     nodes = (0, 1, 6, 7, 8)
     put = {n: (gathered, k) for k, n in enumerate(nodes)}
-    sweep((-1, 0), p1_modes, g, {1: open_at["p2", 1]}, put, visit(1))
-    sweep((6, 7, 8), p1_modes, g, {6: open_at["p2", 6]}, put, visit(1))
+    sweep((-1, 0), p1_modes, g, {1: open_at["p2", 1]}, put)
+    sweep((6, 7, 8), p1_modes, g, {6: open_at["p2", 6]}, put)
     for k, n in enumerate(nodes):
         finish(put[n], (q2, k), edge, past_x if n >= CX else None)
 
@@ -438,16 +390,10 @@
     p2_modes.update({2: keep["p2", 2], 5: keep["p2", 5]})
     sums[...] = sums_in[...]
 
-    def energy(rows, _):
+    def energy(rows):
         total = jnp.zeros((8, CZ), F32)
         for elements in ((0, 1), (5, 6, 7)):
-            here = load(p2_modes[elements[0]], rows)
-            for e in elements:
-                there = load(p2_modes[e + 1], rows)
-                strain = strains(here, there)
-                visit(2)(e, strain, rows)
-                total = total + inner(strain, stresses(strain, g(e, rows)))
-                here = there
+            total = add_energy(total, elements, p2_modes, g, rows)
         sums[5] += total
 
     each_chunk(energy, False)
@@ -468,15 +414,34 @@
     row_out[...] = jnp.broadcast_to(line, row_out.shape)
 
 
-OUTER_T = [(1, 0), (1, 6), (2, 0), (2, 1), (2, 5), (2, 6)]
-
-
-def combine(
-    parts, b_ref, h_ref, p1, p2, q1, q2, t_in, t_out, strain_7, kept, u_next, u_edge, adjoint, sensitivity,
-    modes,
+def products(
+    b_ref, u_ref, halo, b_next, u_next, u_edge, p1, p2, q1, q2, t, b_modes, p1_modes, p2_modes, u_modes,
 ):
-    u_here, u_there = (kept, KEPT.index(("u", 7))), (modes, 0)
-    to_modes(lambda c: jnp.concatenate([u_next[c], u_edge[c]], 0), u_there)
+    for n in range(CX + 1):
+        if n < CX:
+            to_modes(lambda c: jnp.concatenate([b_ref[c, n], halo[c, n]], 0), (b_modes, n))
+            to_modes(lambda c: jnp.concatenate([u_ref[c, n], halo[4 + c, n]], 0), (u_modes, n))
+        else:
+            to_modes(lambda c: b_next[c], (b_modes, n))
+            to_modes(lambda c: jnp.concatenate([u_next[c], u_edge[c]], 0), (u_modes, n))
+        to_modes(lambda c: q1[c, Q1.index(n)] if n in Q1 else p1[c, n - 1], (p1_modes, n))
+        to_modes(lambda c: q2[c, Q2.index(n)] if n in Q2 else p2[c, n - 2], (p2_modes, n))
+    fields = (b_modes, p1_modes, p2_modes)
+
+    def step(rows):
+        for e in range(CX):
+            stiff = stresses(strains(load((u_modes, e), rows), load((u_modes, e + 1), rows)), None)
+            for k, m in enumerate(fields):
+                strain = strains(load((m, e), rows), load((m, e + 1), rows))
+                t[k, e, rows, :] = inner(strain, stiff)
+
+    each_chunk(step, False)
+
+
+Q1, Q2 = (-1, 0, 7, 8, 9), (0, 1, 6, 7, 8)
+
+
+def combine(parts, b_ref, h_ref, p1, p2, q1, q2, t, adjoint, sensitivity):
     line = jnp.sum(parts[...], 0, keepdims=True)
     lane = iota((1, CZ), 1)
     m = [jnp.sum(jnp.where(lane == k, line, 0.0), 1, keepdims=True) for k in range(6)]
@@ -492,24 +457,11 @@
     weight = [jnp.broadcast_to(c, (CY, CZ)) for c in (c0, c1, c2)]
     for x in range(CX):
         for c in range(3):
-            v1 = q1[c, (-1, 0, 7).index(x), :CY] if x in (0, 7) else p1[c, x - 1, :CY]
-            v2 = p2[c, x - 2, :CY] if 2 <= x < 6 else q2[c, (0, 1, 6, 7).index(x), :CY]
+            v1 = q1[c, Q1.index(x), :CY] if x in Q1 else p1[c, x - 1, :CY]
+            v2 = q2[c, Q2.index(x), :CY] if x in Q2 else p2[c, x - 2, :CY]
             adjoint[c, x] = weight[0] * b_ref[c, x] + weight[1] * v1 + weight[2] * v2
-        if x == 7:
-            continue
-        product = None
-        for k in range(3):
-            part = t_out[OUTER_T.index((k, x))] if (k, x) in OUTER_T else t_in[k, x]
-            product = weight[k] * part if product is None else product + weight[k] * part
+        product = weight[0] * t[0, x] + weight[1] * t[1, x] + weight[2] * t[2, x]
         sensitivity[x] = 2.0 * (1.0 - h_ref[x]) * product
-    for j in range(0, CY, 8):
-        rows = pl.ds(j, 8)
-        stiff = stresses(strains(load(u_here, rows), load(u_there, rows)), None)
-        product = None
-        for k in range(3):
-            part = weight[k][:8] * inner([strain_7[k, i, rows, :] for i in range(18)], stiff)
-            product = part if product is None else product + part
-        sensitivity[7, rows, :] = 2.0 * (1.0 - h_ref[7, rows, :]) * product
 
 
 VMEM = pl.BlockSpec(memory_space=pltpu.VMEM)
@@ -543,8 +495,6 @@
     )
     y_b = exchange(y_b, "gy", 1)
     y_a = exchange(y_a, "gy", 0)
-    n = lax.axis_size("gx")
-    u_next = lax.ppermute(u_first, "gx", [(i, i - 1) for i in range(1, n)])
     x_a, x_b, halo = call(
         pack_x, 6,
         (y_a, y_b, misfit, damage),
@@ -554,31 +504,37 @@
     x_a = exchange(x_a, "gx", 0)
     devices = lax.axis_size("gx") * lax.axis_size("gy")
     layer = (ROWS, CZ)
-    p1, p2, t_in, kept, opened, weights, sums = call(
+    p1, p2, kept, opened, sums = call(
         inner_kernel, 20,
-        (misfit, damage, displacement, halo),
+        (misfit, damage, halo),
         [
-            (3, 6) + layer, (3, 4) + layer, (3, CX, CY, CZ), (12, len(KEPT)) + layer,
-            (12, len(OPEN)) + layer, (18, len(KEPT_WEIGHTS), CY, CZ), (6, 8, CZ),
+            (3, 6) + layer, (3, 4) + layer, (12, len(KEPT)) + layer, (12, len(OPEN)) + layer,
+            (6, 8, CZ),
         ],
-        [(12, CX) + layer, (12, CX) + layer, (18, CX, CY, CZ), (CX,) + layer],
-    )
-    q1, q2, t_out, line, strain_7, u_edge = call(
+        [(12, CX) + layer, (12, CX) + layer, (CX,) + layer],
+    )
+    q1, q2, line, b_next, u_edge = call(
         outer_kernel, 20,
-        (misfit, damage, halo, x_a, x_b, p1, p2, kept, opened, weights, sums),
-        [(3, 5) + layer, (3, 5) + layer, (len(OUTER_T), CY, CZ), (devices, CZ), (3, 18, CY, CZ), (3, 8, CZ)],
+        (misfit, damage, halo, x_a, x_b, p1, p2, kept, opened, sums),
+        [(3, 5) + layer, (3, 5) + layer, (devices, CZ), (3,) + layer, (3, 8, CZ)],
         [
             (11,) + layer, (11,) + layer, (5,) + layer, (12, 15) + layer, (12, 5) + layer,
             (6, 8, CZ),
         ],
     )
-    line, u_next = lax.optimization_barrier((line, u_next))
     parts = lax.all_to_all(line, AXES, 0, 0, tiled=True)
+    n = lax.axis_size("gx")
+    u_next = lax.ppermute(u_first, "gx", [(i, i - 1) for i in range(1, n)])
+    (t,) = call(
+        products, 20,
+        (misfit, displacement, halo, b_next, u_next, u_edge, p1, p2, q1, q2),
+        [(3, CX, CY, CZ)],
+        [(12, CX + 1) + layer] * 4,
+    )
     return call(
         combine, 8,
-        (parts, misfit, damage, p1, p2, q1, q2, t_in, t_out, strain_7, kept, u_next, u_edge),
+        (parts, misfit, damage, p1, p2, q1, q2, t),
         [(3, CX, CY, CZ), (CX, CY, CZ)],
-        [(12, 1, ROWS, CZ)],
     )
 
 

time: 53.9 us -> 53.2 us (0.987)
  blocking collectives: 32.5 us -> 0 us
  starting transfers between devices: 8.36 us -> 27.3 us
  waiting for transfers between devices: 4.06 us -> 15.6 us
  Pallas kernels: 7.98 us -> 9.43 us
    all_to_all x1 -> x0, blocking collectives: 32.5 us -> none  [body(): parts = lax.all_to_all(line, AXES, 0, 0, tiled=True)]
    all_to_all x0 -> x1, starting transfers between devices: none -> 18.9 us  [body(): parts = lax.all_to_all(line, AXES, 0, 0, tiled=True)]
    all_to_all x0 -> x1, waiting for transfers between devices: none -> 5.61 us  [body(): parts = lax.all_to_all(line, AXES, 0, 0, tiled=True)]
    ppermute x1, waiting for transfers between devices: 0.01 us -> 3.96 us  [body(): u_next = lax.ppermute(u_first, 'gx', [(i, i - 1) for i in range(1, n)])]
    ppermute x4, waiting for transfers between devices: 4.05 us -> 6.07 us  [exchange(): return lax.ppermute(x, axis, pairs)]
    pallas_call x5 -> x6, Pallas kernels: 7.98 us -> 9.43 us  [call(): pl.pallas_call(kernel, in_specs=in_specs or [VMEM] * len(inputs), out_spe...]
  transfers between devices with their start and end apart: 5 -> 6, of which waited for: 1 -> 4; matrix products, arithmetic and copies ran while one was open for 0% -> 0% of each run, Pallas kernels for 10% -> 8%
where the time goes in v7:
time: 53.2 us; the launch traced here: 53 us
  starting transfers between devices  27.3 us (51%)
  waiting for transfers between devices  15.6 us (29%)
  Pallas kernels  9.43 us (18%)
  between operations  0.7 us (1%)
    all_to_all x1, starting transfers between devices, body(): parts = lax.all_to_all(line, AXES, 0, 0, tiled=True)  18.9 us
    pallas_call x6, Pallas kernels, call(): pl.pallas_call(kernel, in_specs=in_specs or [VMEM] * len(inputs), out_spe...  9.43 us
    ppermute x4, starting transfers between devices, exchange(): return lax.ppermute(x, axis, pairs)  7.07 us
    ppermute x4, waiting for transfers between devices, exchange(): return lax.ppermute(x, axis, pairs)  6.07 us
    all_to_all x1, waiting for transfers between devices, body(): parts = lax.all_to_all(line, AXES, 0, 0, tiled=True)  5.61 us
    ppermute x1, waiting for transfers between devices, body(): u_next = lax.ppermute(u_first, 'gx', [(i, i - 1) for i in range(1, n)])  3.96 us
    ppermute x1, starting transfers between devices, body(): u_next = lax.ppermute(u_first, 'gx', [(i, i - 1) for i in range(1, n)])  1.29 us
  transfers between devices with their start and end apart: 6, of which 4 were waited for; matrix products, arithmetic and copies ran while one was open for 0% of the time, Pallas kernels for 8%

profile of v7, /device:TPU:1, one launch (start us, length us, event | category | flops | bytes accessed | tf_op | source)
XLA Modules:
  0.0 53.0 jit_solution(17841022287823029926)
XLA Ops:
  0.6 1.3 %shard_map.50 = (f32[2,8,8,128]{3,2,1,0:T(8,128)S(1)}, f32[2,8,8,128]{3,2,1,0:T(8,128)S(1)}, f32[3,8,32,128]{3,2,1,0:T(8,128)S(1)}, f32[8,32,128]{2,1,0:T(8,128)...) custom-call(f32[3,8,32,128]{3,2,1,0:T(8,128)} %b.1, f32[8,32,128]{2,1,0:T(8,128)} %h.1, f32[3,8,32,128]{3,2,1,0:T(8,128)} %u.1), custom_call_target="tpu_custom_call" | custom-call | tf_op jit(solution)/shard_map/pallas_call | solution.py:475
  1.9 3.3 %collective-permute-start = (f32[2,8,8,128]{3,2,1,0:T(8,128)S(1)}, f32[2,8,8,128]{3,2,1,0:T(8,128)S(1)}, u32[]{:S(2)}, u32[]{:S(2)}) collective-permute-start(f32[2,8,8,128]{3,2,1,0:T(8,128)S(1)} %get-tuple-element.23), channel_id=1, source_target_pairs={{0,1},{1,0},{2,3},{3,2},{4,5},{5,4},{6,7},{7,6},{8,9},{9,8},{10,11... | collective-permute-start | bytes 196616 | tf_op jit(solution)/shard_map/ppermute | solution.py:22
  5.2 3.0 %collective-permute-start.1 = (f32[2,8,8,128]{3,2,1,0:T(8,128)S(1)}, f32[2,8,8,128]{3,2,1,0:T(8,128)S(1)}, u32[]{:S(2)}, u32[]{:S(2)}) collective-permute-start(f32[2,8,8,128]{3,2,1,0:T(8,128)S(1)} %get-tuple-element.24), channel_id=1, source_target_pairs={{1,2},{2,1},{5,6},{6,5},{9,10},{10,9},{13,14},{14,13},{17,18},{18,... | collective-permute-start | bytes 196616 | tf_op jit(solution)/shard_map/ppermute | solution.py:22
  8.2 0.0 collective-permute-done.y_a
  8.2 4.0 %collective-permute-done.1.y_b = f32[2,8,8,128]{3,2,1,0:T(8,128)S(1)} collective-permute-done((f32[2,8,8,128]{3,2,1,0:T(8,128)S(1)}, f32[2,8,8,128]{3,2,1,0:T(8,128)S(1)}, u32[]{:S(2)}, u32[]{:S(2)}) %collective-permute-start.1) | collective-permute-done | bytes 65568 | tf_op jit(solution)/shard_map/ppermute | solution.py:22
  12.3 0.1 shard_map.51
  12.3 0.1 collective-permute-start.2
  12.4 0.7 %collective-permute-start.3 = (f32[11,40,128]{2,1,0:T(8,128)S(1)}, f32[11,40,128]{2,1,0:T(8,128)S(1)}, u32[]{:S(2)}, u32[]{:S(2)}) collective-permute-start(f32[11,40,128]{2,1,0:T(8,128)S(1)} %get-tuple-element.27), channel_id=1, source_target_pairs={{4,8},{8,4},{12,16},{16,12},{20,24},{24,20},{28,32},{32,28},{36,40... | collective-permute-start | bytes 675848 | tf_op jit(solution)/shard_map/ppermute | solution.py:22
  13.1 2.1 %shard_map.52 = (f32[3,6,40,128]{3,2,1,0:T(8,128)S(1)}, f32[3,4,40,128]{3,2,1,0:T(8,128)S(1)}, f32[12,6,40,128]{3,2,1,0:T(8,128)S(1)}, f32[12,4,40,128]{3,2,1,0:T(8,128)S(1)}, f32[6,8,128]{2,1,0:T(8,128)S(1)}) custom-call(f32[3,8,32,128]{3,2,1,0:T(8,128)S(1)} %get-tuple-element.21.b_ref, f32[8,32,128]{2,1,0:T(8,128)S(1)} %get-tuple-element.22.h_ref, ...), custom_call_target="tpu_custom_call" | custom-call | tf_op jit(solution)/shard_map/pallas_call | solution.py:475
  15.2 2.0 %collective-permute-done.2.x_a = f32[11,40,128]{2,1,0:T(8,128)S(1)} collective-permute-done((f32[11,40,128]{2,1,0:T(8,128)S(1)}, f32[11,40,128]{2,1,0:T(8,128)S(1)}, u32[]{:S(2)}, u32[]{:S(2)}) %collective-permute-start.2) | collective-permute-done | bytes 225312 | tf_op jit(solution)/shard_map/ppermute | solution.py:22
  17.2 0.0 collective-permute-done.3.x_b
  17.2 2.8 %shard_map.53 = (f32[3,5,40,128]{3,2,1,0:T(8,128)S(1)}, f32[3,5,40,128]{3,2,1,0:T(8,128)S(1)}, f32[256,128]{1,0:T(8,128)}, f32[3,40,128]{2,1,0:T(8,128)S(1)}, f32[3,8,128]{2,1,0:T(8,128)S(1)}) custom-call(f32[3,8,32,128]{3,2,1,0:T(8,128)S(1)} %get-tuple-element.21.b_ref, f32[8,32,128]{2,1,0:T(8,128)S(1)} %get-tuple-element.22.h_ref, ...), custom_call_target="tpu_custom_call" | custom-call | tf_op jit(solution)/shard_map/pallas_call | solution.py:475
  20.0 18.9 %all-to-all-start = ((f32[256,1,128]{2,1,0:T(1,128)}), f32[256,1,128]{2,1,0:T(1,128)S(1)}, u32[]{:S(2)}, u32[]{:S(2)}) async-start(f32[256,1,128]{2,1,0:T(1,128)} %bitcast.1), calls=%async_computation | async-start | bytes 262144 | tf_op jit(solution)/shard_map/all_to_all | solution.py:525
  38.9 1.3 %collective-permute-start.4 = (f32[3,32,128]{2,1,0:T(8,128)S(1)}, f32[3,32,128]{2,1,0:T(8,128)S(1)}, u32[]{:S(2)}, u32[]{:S(2)}) collective-permute-start(f32[3,32,128]{2,1,0:T(8,128)S(1)} %get-tuple-element.38), channel_id=1, source_target_pairs={{4,0},{8,4},{12,8},{16,12},{20,16},{24,20},{28,24},{32,28},{36,32}... | collective-permute-start | bytes 147464 | tf_op jit(solution)/shard_map/ppermute | solution.py:527
  40.2 4.0 %collective-permute-done.4.u_next = f32[3,32,128]{2,1,0:T(8,128)S(1)} collective-permute-done((f32[3,32,128]{2,1,0:T(8,128)S(1)}, f32[3,32,128]{2,1,0:T(8,128)S(1)}, u32[]{:S(2)}, u32[]{:S(2)}) %collective-permute-start.4) | collective-permute-done | bytes 49184 | tf_op jit(solution)/shard_map/ppermute | solution.py:527
  44.2 2.2 %shard_map.54.t = f32[3,8,32,128]{3,2,1,0:T(8,128)S(1)} custom-call(f32[3,8,32,128]{3,2,1,0:T(8,128)S(1)} %get-tuple-element.21.b_ref, f32[3,8,32,128]{3,2,1,0:T(8,128)S(1)} %get-tuple-element.36.u_ref, f32[7,8,8,128]{3,2,1,0:T(8,128)S(1)} %get-tuple-element.25.halo, f32[3,40,128]{2,1,0:T(8,128)S(1)} %get-tuple-element.37.b_next, ...), custom_call_target="tpu_custom_call" | custom-call | tf_op jit(solution)/shard_map/pallas_call | solution.py:475
  46.4 5.6 %all-to-all-done = f32[256,1,128]{2,1,0:T(1,128)S(1)} async-done(((f32[256,1,128]{2,1,0:T(1,128)}), f32[256,1,128]{2,1,0:T(1,128)S(1)}, u32[]{:S(2)}, u32[]{:S(2)}) %all-to-all-start) | async-done | bytes 131104 | tf_op jit(solution)/shard_map/all_to_all | solution.py:525
  52.0 1.0 %shard_map.55 = (f32[3,8,32,128]{3,2,1,0:T(8,128)}, f32[8,32,128]{2,1,0:T(8,128)}) custom-call(f32[256,128]{1,0:T(8,128)S(1)} %bitcast.4, f32[3,8,32,128]{3,2,1,0:T(8,128)S(1)} %get-tuple-element.21.b_ref, f32[8,32,128]{2,1,0:T(8,128)S(1)} %get-tuple-element.22.h_ref, f32[3,6,40,128]{3,2,1,0:T(8,128)S(1)} %get-tuple-element.28.p1, ...), custom_call_target="tpu_custom_call" | custom-call | tf_op jit(solution)/shard_map/pallas_call | solution.py:475
Async XLA Ops:
  1.9 6.3 %collective-permute-start = (f32[2,8,8,128]{3,2,1,0:T(8,128)S(1)}, f32[2,8,8,128]{3,2,1,0:T(8,128)S(1)}, u32[]{:S(2)}, u32[]{:S(2)}) collective-permute-start(f32[2,8,8,128]{3,2,1,0:T(8,128)S(1)} %get-tuple-element.23), channel_id=1, source_target_pairs={{0,1},{1,0},{2,3},{3,2},{4,5},{5,4},{6,7},{7,6},{8,9},{9,8},{10,11... | collective-permute-start | bytes 196616 | tf_op jit(solution)/shard_map/ppermute | solution.py:22
  5.2 7.1 %collective-permute-start.1 = (f32[2,8,8,128]{3,2,1,0:T(8,128)S(1)}, f32[2,8,8,128]{3,2,1,0:T(8,128)S(1)}, u32[]{:S(2)}, u32[]{:S(2)}) collective-permute-start(f32[2,8,8,128]{3,2,1,0:T(8,128)S(1)} %get-tuple-element.24), channel_id=1, source_target_pairs={{1,2},{2,1},{5,6},{6,5},{9,10},{10,9},{13,14},{14,13},{17,18},{18,... | collective-permute-start | bytes 196616 | tf_op jit(solution)/shard_map/ppermute | solution.py:22
  12.3 4.9 %collective-permute-start.2 = (f32[11,40,128]{2,1,0:T(8,128)S(1)}, f32[11,40,128]{2,1,0:T(8,128)S(1)}, u32[]{:S(2)}, u32[]{:S(2)}) collective-permute-start(f32[11,40,128]{2,1,0:T(8,128)S(1)} %get-tuple-element.26), channel_id=1, source_target_pairs={{0,4},{4,0},{8,12},{12,8},{16,20},{20,16},{24,28},{28,24},{32,36},... | collective-permute-start | bytes 675848 | tf_op jit(solution)/shard_map/ppermute | solution.py:22
  12.4 4.8 %collective-permute-start.3 = (f32[11,40,128]{2,1,0:T(8,128)S(1)}, f32[11,40,128]{2,1,0:T(8,128)S(1)}, u32[]{:S(2)}, u32[]{:S(2)}) collective-permute-start(f32[11,40,128]{2,1,0:T(8,128)S(1)} %get-tuple-element.27), channel_id=1, source_target_pairs={{4,8},{8,4},{12,16},{16,12},{20,24},{24,20},{28,32},{32,28},{36,40... | collective-permute-start | bytes 675848 | tf_op jit(solution)/shard_map/ppermute | solution.py:22
  20.0 32.0 %all-to-all-start = ((f32[256,1,128]{2,1,0:T(1,128)}), f32[256,1,128]{2,1,0:T(1,128)S(1)}, u32[]{:S(2)}, u32[]{:S(2)}) async-start(f32[256,1,128]{2,1,0:T(1,128)} %bitcast.1), calls=%async_computation | async-start | bytes 262144 | tf_op jit(solution)/shard_map/all_to_all | solution.py:525
  38.9 5.3 %collective-permute-start.4 = (f32[3,32,128]{2,1,0:T(8,128)S(1)}, f32[3,32,128]{2,1,0:T(8,128)S(1)}, u32[]{:S(2)}, u32[]{:S(2)}) collective-permute-start(f32[3,32,128]{2,1,0:T(8,128)S(1)} %get-tuple-element.38), channel_id=1, source_target_pairs={{4,0},{8,4},{12,8},{16,12},{20,16},{24,20},{28,24},{32,28},{36,32}... | collective-permute-start | bytes 147464 | tf_op jit(solution)/shard_map/ppermute | solution.py:527

commit v8 on v7

--- a/solution.py
+++ b/solution.py
@@ -30,14 +30,13 @@
     return (1.0 - damage) * (1.0 - damage) + 0.001
 
 
-def pack_y(b, h, u, out_a, out_b, b_all, h_all, u_all, u_first, done):
+def pack_y(b, h, u, out_a, out_b, b_all, h_all, u_all, done):
     copies = []
     for k, (source, target) in enumerate(((h, h_all), (b, b_all), (u, u_all))):
         copies.append(pltpu.make_async_copy(source, target, done.at[k]))
         copies[-1].start()
     for copy in copies:
         copy.wait()
-    u_first[...] = u_all[:, 0]
     b_lo, b_hi = b_all[:, :, :8], b_all[:, :, CY - 8 :]
     h_lo, h_hi = h_all[:, :8], h_all[:, CY - 8 :]
     u_lo = u_all[:, :, :8]
@@ -70,7 +69,7 @@
         out_b[0], out_b[1] = low_1, low_2
 
 
-def pack_x(y_a, y_b, b_ref, h_ref, out_a, out_b, halo):
+def pack_x(y_a, y_b, b_ref, h_ref, u_ref, out_a, out_b, halo):
     odd_y = lax.rem(lax.axis_index("gy"), 2) == 1
     row = iota((CX, 8, CZ), 1)
     up = lambda x, k: pltpu.roll(x, k % 8, 1)
@@ -89,23 +88,29 @@
         halo[4 + c] = jnp.where(row < 1, up(above_2, -3 - c), 0.0)
     odd_x = lax.rem(lax.axis_index("gx"), 2) == 1
 
+    def put(out, plane, own, edge):
+        out[plane * ROWS : plane * ROWS + CY] = own
+        out[plane * ROWS + CY : (plane + 1) * ROWS] = edge
+
     def low(out):
         for c in range(3):
             for x in range(3):
                 edge = halo[c, x]
                 if x == 0:
                     edge = jnp.where(row[0] == 3, pltpu.roll(halo[4 + c, 0], 3, 0), edge)
-                out[3 * c + x, :CY], out[3 * c + x, CY:] = b_ref[c, x], edge
+                put(out, 3 * c + x, b_ref[c, x], edge)
+            out[11 * ROWS + c * CY : 11 * ROWS + (c + 1) * CY] = u_ref[c, 0]
         for x in range(2):
-            out[9 + x, :CY], out[9 + x, CY:] = degradation_of(h_ref[x]), halo[3, x]
+            put(out, 9 + x, degradation_of(h_ref[x]), halo[3, x])
 
     def high(out):
         for c in range(3):
             for x in range(2):
-                out[3 * c + x, :CY], out[3 * c + x, CY:] = b_ref[c, 6 + x], halo[c, 6 + x]
-            out[3 * c + 2] = jnp.zeros((ROWS, CZ), F32)
+                put(out, 3 * c + x, b_ref[c, 6 + x], halo[c, 6 + x])
+            out[(3 * c + 2) * ROWS : (3 * c + 3) * ROWS] = jnp.zeros((ROWS, CZ), F32)
+            out[11 * ROWS + c * CY : 11 * ROWS + (c + 1) * CY] = jnp.zeros((CY, CZ), F32)
         for x in range(2):
-            out[9 + x, :CY], out[9 + x, CY:] = degradation_of(h_ref[6 + x]), halo[3, 6 + x]
+            put(out, 9 + x, degradation_of(h_ref[6 + x]), halo[3, 6 + x])
 
     @pl.when(odd_x)
     def _():
@@ -320,26 +325,30 @@
 
 def outer_kernel(
     b_ref, h_ref, halo, x_a, x_b, p1, p2, kept, opened, sums_in,
-    q1, q2, row_out, b_next, u_edge, above, below, g_ref, modes, gathered, sums,
+    q1, q2, row_out, b_next, u_next, above, below, g_ref, modes, gathered, sums,
 ):
     edge = row_edge()
     odd_x = lax.rem(lax.axis_index("gx"), 2) == 1
     last_x = lax.axis_index("gx") == lax.axis_size("gx") - 1
     past_x = jnp.where(last_x, 0.0, 1.0).astype(F32)
 
+    def split(x_above, x_below):
+        for k in range(11):
+            above[k] = x_above[k * ROWS : (k + 1) * ROWS]
+            below[k] = x_below[k * ROWS : (k + 1) * ROWS]
+        for c in range(3):
+            u_next[c, :CY] = x_above[11 * ROWS + c * CY : 11 * ROWS + (c + 1) * CY]
+            u_next[c, CY:] = pltpu.roll(x_above[3 * c * ROWS + CY : (3 * c + 1) * ROWS], 5, 0)
+            b_next[c] = x_above[3 * c * ROWS : (3 * c + 1) * ROWS]
+
     @pl.when(odd_x)
     def _():
-        above[...] = x_b[...]
-        below[...] = x_a[...]
+        split(x_b, x_a)
 
     @pl.when(jnp.logical_not(odd_x))
     def _():
-        above[...] = x_a[...]
-        below[...] = x_b[...]
-
-    for c in range(3):
-        u_edge[c] = pltpu.roll(above[3 * c, CY:], 5, 0)
-        b_next[c] = above[3 * c]
+        split(x_a, x_b)
+
     for k, e in enumerate((0, 1, 5, 6, 7)):
         g_ref[k, :CY] = degradation_of(h_ref[e])
         g_ref[k, CY:] = halo[3, e]
@@ -415,7 +424,7 @@
 
 
 def products(
-    b_ref, u_ref, halo, b_next, u_next, u_edge, p1, p2, q1, q2, t, b_modes, p1_modes, p2_modes, u_modes,
+    b_ref, u_ref, halo, b_next, u_next, p1, p2, q1, q2, t, b_modes, p1_modes, p2_modes, u_modes,
 ):
     for n in range(CX + 1):
         if n < CX:
@@ -423,7 +432,7 @@
             to_modes(lambda c: jnp.concatenate([u_ref[c, n], halo[4 + c, n]], 0), (u_modes, n))
         else:
             to_modes(lambda c: b_next[c], (b_modes, n))
-            to_modes(lambda c: jnp.concatenate([u_next[c], u_edge[c]], 0), (u_modes, n))
+            to_modes(lambda c: u_next[c], (u_modes, n))
         to_modes(lambda c: q1[c, Q1.index(n)] if n in Q1 else p1[c, n - 1], (p1_modes, n))
         to_modes(lambda c: q2[c, Q2.index(n)] if n in Q2 else p2[c, n - 2], (p2_modes, n))
     fields = (b_modes, p1_modes, p2_modes)
@@ -484,11 +493,11 @@
 
 def body(misfit, damage, displacement):
     tile = (CX, 8, CZ)
-    y_a, y_b, misfit, damage, displacement, u_first = call(
+    y_a, y_b, misfit, damage, displacement = call(
         pack_y, 4,
         [pltpu.with_memory_space_constraint(x, pltpu.HBM) for x in (misfit, damage, displacement)],
         [
-            (2,) + tile, (2,) + tile, (3, CX, CY, CZ), (CX, CY, CZ), (3, CX, CY, CZ), (3, CY, CZ),
+            (2,) + tile, (2,) + tile, (3, CX, CY, CZ), (CX, CY, CZ), (3, CX, CY, CZ),
         ],
         [pltpu.SemaphoreType.DMA((3,))],
         [pl.BlockSpec(memory_space=pltpu.HBM)] * 3,
@@ -497,8 +506,8 @@
     y_a = exchange(y_a, "gy", 0)
     x_a, x_b, halo = call(
         pack_x, 6,
-        (y_a, y_b, misfit, damage),
-        [(11, ROWS, CZ)] * 2 + [(7,) + tile],
+        (y_a, y_b, misfit, damage, displacement),
+        [(11 * ROWS + 3 * CY, CZ)] * 2 + [(7,) + tile],
     )
     x_b = exchange(x_b, "gx", 1)
     x_a = exchange(x_a, "gx", 0)
@@ -513,21 +522,19 @@
         ],
         [(12, CX) + layer, (12, CX) + layer, (CX,) + layer],
     )
-    q1, q2, line, b_next, u_edge = call(
+    q1, q2, line, b_next, u_next = call(
         outer_kernel, 20,
         (misfit, damage, halo, x_a, x_b, p1, p2, kept, opened, sums),
-        [(3, 5) + layer, (3, 5) + layer, (devices, CZ), (3,) + layer, (3, 8, CZ)],
+        [(3, 5) + layer, (3, 5) + layer, (devices, CZ), (3,) + layer, (3,) + layer],
         [
             (11,) + layer, (11,) + layer, (5,) + layer, (12, 15) + layer, (12, 5) + layer,
             (6, 8, CZ),
         ],
     )
     parts = lax.all_to_all(line, AXES, 0, 0, tiled=True)
-    n = lax.axis_size("gx")
-    u_next = lax.ppermute(u_first, "gx", [(i, i - 1) for i in range(1, n)])
     (t,) = call(
         products, 20,
-        (misfit, displacement, halo, b_next, u_next, u_edge, p1, p2, q1, q2),
+        (misfit, displacement, halo, b_next, u_next, p1, p2, q1, q2),
         [(3, CX, CY, CZ)],
         [(12, CX + 1) + layer] * 4,
     )

time: 53.2 us -> 53.8 us (1.011)
  waiting for transfers between devices: 15.6 us -> 17.5 us
  starting transfers between devices: 27.3 us -> 26 us
    all_to_all x1, waiting for transfers between devices: 5.61 us -> 10.9 us  [body(): parts = lax.all_to_all(line, AXES, 0, 0, tiled=True)]
    ppermute x1 -> x0, waiting for transfers between devices: 3.96 us -> none  [body(): u_next = lax.ppermute(u_first, 'gx', [(i, i - 1) for i in range(1, n)])]
    ppermute x1 -> x0, starting transfers between devices: 1.29 us -> none  [body(): u_next = lax.ppermute(u_first, 'gx', [(i, i - 1) for i in range(1, n)])]
  transfers between devices with their start and end apart: 6 -> 5, of which waited for: 4 -> 3; matrix products, arithmetic and copies ran while one was open for 0% -> 0% of each run, Pallas kernels for 8% -> 8%
where the time goes in v8:
time: 53.8 us; the launch traced here: 53.6 us
  starting transfers between devices  26 us (48%)
  waiting for transfers between devices  17.5 us (33%)
  Pallas kernels  9.45 us (18%)
  between operations  0.7 us (1%)
    all_to_all x1, starting transfers between devices, body(): parts = lax.all_to_all(line, AXES, 0, 0, tiled=True)  18.9 us
    all_to_all x1, waiting for transfers between devices, body(): parts = lax.all_to_all(line, AXES, 0, 0, tiled=True)  10.9 us
    pallas_call x6, Pallas kernels, call(): pl.pallas_call(kernel, in_specs=in_specs or [VMEM] * len(inputs), out_spe...  9.45 us
    ppermute x4, starting transfers between devices, exchange(): return lax.ppermute(x, axis, pairs)  7.08 us
    ppermute x4, waiting for transfers between devices, exchange(): return lax.ppermute(x, axis, pairs)  6.6 us
  transfers between devices with their start and end apart: 5, of which 3 were waited for; matrix products, arithmetic and copies ran while one was open for 0% of the time, Pallas kernels for 8%

profile of v8, /device:TPU:1, one launch (start us, length us, event | category | flops | bytes accessed | tf_op | source)
XLA Modules:
  0.0 53.6 jit_solution(7521976584040102331)
XLA Ops:
  0.6 1.3 %shard_map.50 = (f32[2,8,8,128]{3,2,1,0:T(8,128)S(1)}, f32[2,8,8,128]{3,2,1,0:T(8,128)S(1)}, f32[3,8,32,128]{3,2,1,0:T(8,128)S(1)}, f32[8,32,128]{2,1,0:T(8,128)S(1)}, f32[3,8,32,128]{3,2,1,0:T(8,128)S(1)}) custom-call(f32[3,8,32,128]{3,2,1,0:T(8,128)} %b.1, f32[8,32,128]{2,1,0:T(8,128)} %h.1, f32[3,8,32,128]{3,2,1,0:T(8,128)} %u.1), custom_call_target="tpu_custom_call" | custom-call | tf_op jit(solution)/shard_map/pallas_call | solution.py:484
  1.9 3.3 %collective-permute-start = (f32[2,8,8,128]{3,2,1,0:T(8,128)S(1)}, f32[2,8,8,128]{3,2,1,0:T(8,128)S(1)}, u32[]{:S(2)}, u32[]{:S(2)}) collective-permute-start(f32[2,8,8,128]{3,2,1,0:T(8,128)S(1)} %get-tuple-element.22), channel_id=1, source_target_pairs={{0,1},{1,0},{2,3},{3,2},{4,5},{5,4},{6,7},{7,6},{8,9},{9,8},{10,11... | collective-permute-start | bytes 196616 | tf_op jit(solution)/shard_map/ppermute | solution.py:22
  5.2 3.0 %collective-permute-start.1 = (f32[2,8,8,128]{3,2,1,0:T(8,128)S(1)}, f32[2,8,8,128]{3,2,1,0:T(8,128)S(1)}, u32[]{:S(2)}, u32[]{:S(2)}) collective-permute-start(f32[2,8,8,128]{3,2,1,0:T(8,128)S(1)} %get-tuple-element.23), channel_id=1, source_target_pairs={{1,2},{2,1},{5,6},{6,5},{9,10},{10,9},{13,14},{14,13},{17,18},{18,... | collective-permute-start | bytes 196616 | tf_op jit(solution)/shard_map/ppermute | solution.py:22
  8.2 0.0 collective-permute-done.y_a
  8.2 4.0 %collective-permute-done.1.y_b = f32[2,8,8,128]{3,2,1,0:T(8,128)S(1)} collective-permute-done((f32[2,8,8,128]{3,2,1,0:T(8,128)S(1)}, f32[2,8,8,128]{3,2,1,0:T(8,128)S(1)}, u32[]{:S(2)}, u32[]{:S(2)}) %collective-permute-start.1) | collective-permute-done | bytes 65568 | tf_op jit(solution)/shard_map/ppermute | solution.py:22
  12.3 0.1 shard_map.51
  12.3 0.1 collective-permute-start.2
  12.4 0.7 %collective-permute-start.3 = (f32[536,128]{1,0:T(8,128)S(1)}, f32[536,128]{1,0:T(8,128)S(1)}, u32[]{:S(2)}, u32[]{:S(2)}) collective-permute-start(f32[536,128]{1,0:T(8,128)S(1)} %get-tuple-element.27), channel_id=1, source_target_pairs={{4,8},{8,4},{12,16},{16,12},{20,24},{24,20},{28,32},{32,28},{36,40... | collective-permute-start | bytes 823304 | tf_op jit(solution)/shard_map/ppermute | solution.py:22
  13.1 2.1 %shard_map.52 = (f32[3,6,40,128]{3,2,1,0:T(8,128)S(1)}, f32[3,4,40,128]{3,2,1,0:T(8,128)S(1)}, f32[12,6,40,128]{3,2,1,0:T(8,128)S(1)}, f32[12,4,40,128]{3,2,1,0:T(8,128)S(1)}, f32[6,8,128]{2,1,0:T(8,128)S(1)}) custom-call(f32[3,8,32,128]{3,2,1,0:T(8,128)S(1)} %get-tuple-element.20.b_ref, f32[8,32,128]{2,1,0:T(8,128)S(1)} %get-tuple-element.21.h_ref, ...), custom_call_target="tpu_custom_call" | custom-call | tf_op jit(solution)/shard_map/pallas_call | solution.py:484
  15.2 2.5 %collective-permute-done.2.x_a = f32[536,128]{1,0:T(8,128)S(1)} collective-permute-done((f32[536,128]{1,0:T(8,128)S(1)}, f32[536,128]{1,0:T(8,128)S(1)}, u32[]{:S(2)}, u32[]{:S(2)}) %collective-permute-start.2) | collective-permute-done | bytes 274464 | tf_op jit(solution)/shard_map/ppermute | solution.py:22
  17.8 0.0 collective-permute-done.3.x_b
  17.8 2.8 %shard_map.53 = (f32[3,5,40,128]{3,2,1,0:T(8,128)S(1)}, f32[3,5,40,128]{3,2,1,0:T(8,128)S(1)}, f32[256,128]{1,0:T(8,128)}, f32[3,40,128]{2,1,0:T(8,128)S(1)}, f32[3,40,128]{2,1,0:T(8,128)S(1)}) custom-call(f32[3,8,32,128]{3,2,1,0:T(8,128)S(1)} %get-tuple-element.20.b_ref, f32[8,32,128]{2,1,0:T(8,128)S(1)} %get-tuple-element.21.h_ref, ...), custom_call_target="tpu_custom_call" | custom-call | tf_op jit(solution)/shard_map/pallas_call | solution.py:484
  20.6 18.9 %all-to-all-start = ((f32[256,1,128]{2,1,0:T(1,128)}), f32[256,1,128]{2,1,0:T(1,128)S(1)}, u32[]{:S(2)}, u32[]{:S(2)}) async-start(f32[256,1,128]{2,1,0:T(1,128)} %bitcast.1), calls=%async_computation | async-start | bytes 262144 | tf_op jit(solution)/shard_map/all_to_all | solution.py:534
  39.5 2.2 %shard_map.54.t = f32[3,8,32,128]{3,2,1,0:T(8,128)S(1)} custom-call(f32[3,8,32,128]{3,2,1,0:T(8,128)S(1)} %get-tuple-element.20.b_ref, f32[3,8,32,128]{3,2,1,0:T(8,128)S(1)} %get-tuple-element.24.u_ref, f32[7,8,8,128]{3,2,1,0:T(8,128)S(1)} %get-tuple-element.25.halo, f32[3,40,128]{2,1,0:T(8,128)S(1)} %get-tuple-element.36.b_next, ...), custom_call_target="tpu_custom_call" | custom-call | tf_op jit(solution)/shard_map/pallas_call | solution.py:484
  41.7 10.9 %all-to-all-done = f32[256,1,128]{2,1,0:T(1,128)S(1)} async-done(((f32[256,1,128]{2,1,0:T(1,128)}), f32[256,1,128]{2,1,0:T(1,128)S(1)}, u32[]{:S(2)}, u32[]{:S(2)}) %all-to-all-start) | async-done | bytes 131104 | tf_op jit(solution)/shard_map/all_to_all | solution.py:534
  52.5 1.0 %shard_map.55 = (f32[3,8,32,128]{3,2,1,0:T(8,128)}, f32[8,32,128]{2,1,0:T(8,128)}) custom-call(f32[256,128]{1,0:T(8,128)S(1)} %bitcast.4, f32[3,8,32,128]{3,2,1,0:T(8,128)S(1)} %get-tuple-element.20.b_ref, f32[8,32,128]{2,1,0:T(8,128)S(1)} %get-tuple-element.21.h_ref, f32[3,6,40,128]{3,2,1,0:T(8,128)S(1)} %get-tuple-element.28.p1, ...), custom_call_target="tpu_custom_call" | custom-call | tf_op jit(solution)/shard_map/pallas_call | solution.py:484
Async XLA Ops:
  1.9 6.3 %collective-permute-start = (f32[2,8,8,128]{3,2,1,0:T(8,128)S(1)}, f32[2,8,8,128]{3,2,1,0:T(8,128)S(1)}, u32[]{:S(2)}, u32[]{:S(2)}) collective-permute-start(f32[2,8,8,128]{3,2,1,0:T(8,128)S(1)} %get-tuple-element.22), channel_id=1, source_target_pairs={{0,1},{1,0},{2,3},{3,2},{4,5},{5,4},{6,7},{7,6},{8,9},{9,8},{10,11... | collective-permute-start | bytes 196616 | tf_op jit(solution)/shard_map/ppermute | solution.py:22
  5.2 7.1 %collective-permute-start.1 = (f32[2,8,8,128]{3,2,1,0:T(8,128)S(1)}, f32[2,8,8,128]{3,2,1,0:T(8,128)S(1)}, u32[]{:S(2)}, u32[]{:S(2)}) collective-permute-start(f32[2,8,8,128]{3,2,1,0:T(8,128)S(1)} %get-tuple-element.23), channel_id=1, source_target_pairs={{1,2},{2,1},{5,6},{6,5},{9,10},{10,9},{13,14},{14,13},{17,18},{18,... | collective-permute-start | bytes 196616 | tf_op jit(solution)/shard_map/ppermute | solution.py:22
  12.3 5.4 %collective-permute-start.2 = (f32[536,128]{1,0:T(8,128)S(1)}, f32[536,128]{1,0:T(8,128)S(1)}, u32[]{:S(2)}, u32[]{:S(2)}) collective-permute-start(f32[536,128]{1,0:T(8,128)S(1)} %get-tuple-element.26), channel_id=1, source_target_pairs={{0,4},{4,0},{8,12},{12,8},{16,20},{20,16},{24,28},{28,24},{32,36},... | collective-permute-start | bytes 823304 | tf_op jit(solution)/shard_map/ppermute | solution.py:22
  12.4 5.3 %collective-permute-start.3 = (f32[536,128]{1,0:T(8,128)S(1)}, f32[536,128]{1,0:T(8,128)S(1)}, u32[]{:S(2)}, u32[]{:S(2)}) collective-permute-start(f32[536,128]{1,0:T(8,128)S(1)} %get-tuple-element.27), channel_id=1, source_target_pairs={{4,8},{8,4},{12,16},{16,12},{20,24},{24,20},{28,32},{32,28},{36,40... | collective-permute-start | bytes 823304 | tf_op jit(solution)/shard_map/ppermute | solution.py:22
  20.6 32.0 %all-to-all-start = ((f32[256,1,128]{2,1,0:T(1,128)}), f32[256,1,128]{2,1,0:T(1,128)S(1)}, u32[]{:S(2)}, u32[]{:S(2)}) async-start(f32[256,1,128]{2,1,0:T(1,128)} %bitcast.1), calls=%async_computation | async-start | bytes 262144 | tf_op jit(solution)/shard_map/all_to_all | solution.py:534
